TPU v7x, 32 devices: a whole 2x2x4 slice. The times are simulated.
32 devices in a mesh: dp: 4 (over y, x), filter: 8 (over z, core).
Axes of the slice: x: 2, y: 2, z: 4, core: 2. Of those that a mesh axis runs over, the one named last changes fastest.
Arguments:
- fields: bfloat16 [4, 32, 32, 1024], P('dp', None, None, 'filter'), may hold values from -6 to 6
- weight_one: bfloat16 [3, 3, 1024, 1024], P(None, None, 'dp', 'filter'), may hold values from -0.0625 to 0.0625
- weight_two: bfloat16 [3, 3, 1024, 1024], P(None, None, 'dp', 'filter'), may hold values from -0.0625 to 0.0625
- cotangent: bfloat16 [4, 32, 32, 1024], P('dp', None, None, 'filter'), may hold values from -6 to 6
Outputs:
- output: bfloat16 [4, 32, 32, 1024], P('dp', None, None, 'filter')
- grad_one: float32 [3, 3, 1024, 1024], P(None, None, 'dp', 'filter')
- grad_two: float32 [3, 3, 1024, 1024], P(None, None, 'dp', 'filter')
All inputs are finite; a program needn't handle non-finite values.
Results may differ from a plain program's by a relative error of at most 0.018.
Values may be sent and summed in bfloat16 or wider, within the bound.
No kernel may reach another device: no remote copies, remote signals or barrier semaphores. Data moves between devices by JAX's collectives and lax.ppermute only.
A program may use at most 128 MiB of HBM per device.

v0:
```python
import jax
import jax.numpy as jnp
from jax import lax
from jax.sharding import PartitionSpec as P


def shift_cells(values, row_step, col_step):
    size = values.shape[1]
    padded = jnp.pad(values, ((0, 0), (1, 1), (1, 1), (0, 0)))
    return padded[:, 1 + row_step : 1 + row_step + size, 1 + col_step : 1 + col_step + size, :]


def conv_taps(inputs, weights):
    products = jnp.einsum("bhwc,pqcd->bhwpqd", inputs, weights, preferred_element_type=jnp.float32)
    result = jnp.zeros(inputs.shape[:3] + (weights.shape[3],), jnp.float32)
    for row_tap in range(3):
        for col_tap in range(3):
            result = result + shift_cells(
                products[:, :, :, row_tap, col_tap, :], row_tap - 1, col_tap - 1
            )
    return result


def shifted_stack(grads):
    pieces = []
    for row_tap in range(3):
        for col_tap in range(3):
            pieces.append(shift_cells(grads, 1 - row_tap, 1 - col_tap))
    return jnp.stack(pieces, axis=3).reshape(grads.shape[:3] + (3, 3, grads.shape[3]))


def transposed(grads, weights):
    stacked = shifted_stack(grads)
    return jnp.einsum("bhwpqd,pqcd->bhwc", stacked, weights, preferred_element_type=jnp.float32)


def filter_grads(inputs, grads):
    stacked = shifted_stack(grads)
    return jnp.einsum("bhwc,bhwpqd->pqcd", inputs, stacked, preferred_element_type=jnp.float32)


def body(fields, weight_one, weight_two, cotangent):
    full_one = lax.all_gather(weight_one, "dp", axis=2, tiled=True)
    gathered = lax.all_gather(fields, "filter", axis=3, tiled=True)
    pre_one = conv_taps(gathered, full_one)
    hidden = jax.nn.silu(pre_one).astype(jnp.bfloat16)
    hidden_all = lax.all_gather(hidden, "filter", axis=3, tiled=True)
    full_two = lax.all_gather(weight_two, "dp", axis=2, tiled=True)
    output = conv_taps(hidden_all, full_two).astype(jnp.bfloat16)
    grad_two = lax.psum_scatter(
        filter_grads(hidden_all, cotangent).astype(jnp.bfloat16),
        "dp",
        scatter_dimension=2,
        tiled=True,
    ).astype(jnp.float32)
    partial_back = transposed(cotangent, full_two)
    back = lax.psum_scatter(
        partial_back.astype(jnp.bfloat16), "filter", scatter_dimension=3, tiled=True
    ).astype(jnp.float32)
    sigma = jax.nn.sigmoid(pre_one)
    back_pre = (back * sigma * (1.0 + pre_one * (1.0 - sigma))).astype(jnp.bfloat16)
    grad_one = lax.psum_scatter(
        filter_grads(gathered, back_pre).astype(jnp.bfloat16), "dp", scatter_dimension=2, tiled=True
    ).astype(jnp.float32)
    return (output, grad_one, grad_two)


def solution(mesh):
    placed = (
        P("dp", None, None, "filter"),
        P(None, None, "dp", "filter"),
        P(None, None, "dp", "filter"),
        P("dp", None, None, "filter"),
    )
    return jax.shard_map(
        body,
        mesh=mesh,
        in_specs=placed,
        out_specs=(
            P("dp", None, None, "filter"),
            P(None, None, "dp", "filter"),
            P(None, None, "dp", "filter"),
        ),
        check_vma=False,
    )
```

profile of v0, /device:TPU:0, one launch (start us, length us, event | category | flops | bytes accessed | tf_op | source)
XLA Modules:
  0.0 284.4 jit_solution(1730159838617975054)
XLA Ops:
  7.2 0.7 all-gather.11.cloned.1.call-update
  8.0 0.7 all-gather.7.cloned.1.call-update
  8.7 0.0 all-gather.5.cloned.1.call-start
  8.7 0.7 all-gather.5.cloned.1.call-update
  9.4 0.0 reduce-scatter.10.cloned.1.call-start
  9.4 1.0 fusion.41
  10.5 1.0 fusion.43
  11.5 0.1 fusion.45
  11.6 0.1 fusion.47
  11.7 0.1 fusion.49
  11.8 0.1 fusion.51
  12.0 0.1 fusion.55
  12.1 38.0 %all-gather.11.cloned.1.call-done = bf16[3,3,1024,128]{3,2,1,0:T(8,128)(2,1)} async-done(((bf16[3,3,256,128]{3,2,1,0:T(8,128)(2,1)}), bf16[3,3,1024,128]{3,2,1,0:T(8,128)(2,1)}) %all-gather.11.cloned.1.call-update) | async-done | bytes 2359312 | tf_op jit(solution)/shard_map/all_gather | solution.py:48
  50.1 5.3 %fusion.16 = bf16[1,32,32,1024]{3,2,1,0:T(8,128)(2,1)S(1)} fusion(bf16[32,32,3,3,128]{4,1,0,3,2:T(8,128)(2,1)} %bitcast.223, bf16[3,3,1024,128]{3,2,1,0:T(8,128)(2,1)} %all-gather.11.cloned.1.call-done), kind=kOutput, calls=%fused_computation.15 | convolution fusion | flops 2416967680 | bytes 6815744 | tf_op jit(solution)/shard_map/bhwpqd,pqcd->bhwc/dot_general | solution.py:34
  55.4 12.2 %copy.60 = bf16[1,32,32,1024]{2,1,0,3:T(8,128)(2,1)} copy(bf16[1,32,32,1024]{3,2,1,0:T(8,128)(2,1)S(1)} %fusion.16) | data formatting | bytes 4194304
  67.5 12.5 %reshape.42 = bf16[1024,1024]{1,0:T(8,128)(2,1)} reshape(bf16[1024,1,32,32]{3,2,1,0:T(8,128)(2,1)} %bitcast.220) | data formatting | bytes 4194304
  80.0 0.0 all-gather.9.cloned.1.call-start
  80.0 9.4 %all-gather.7.cloned.1.call-done = bf16[3,3,1024,128]{3,2,1,0:T(8,128)(2,1)} async-done(((bf16[3,3,256,128]{3,2,1,0:T(8,128)(2,1)}), bf16[3,3,1024,128]{3,2,1,0:T(8,128)(2,1)}) %all-gather.7.cloned.1.call-update) | async-done | bytes 2359312 | tf_op jit(solution)/shard_map/all_gather | solution.py:43
  89.4 32.5 %all-gather.5.cloned.1.call-done = bf16[1,32,32,1024]{3,2,1,0:T(8,128)(2,1)} async-done(((bf16[1,32,32,128]{3,2,1,0:T(8,128)(2,1)}), bf16[1,32,32,1024]{3,2,1,0:T(8,128)(2,1)}) %all-gather.5.cloned.1.call-update) | async-done | bytes 2097168 | tf_op jit(solution)/shard_map/all_gather | solution.py:44
  121.9 5.2 %fusion.10 = f32[1,32,32,3,3,128]{5,2,4,3,1,0:T(8,128)S(1)} fusion(bf16[3,3,1024,128]{3,2,1,0:T(8,128)(2,1)} %all-gather.7.cloned.1.call-done, bf16[1,32,32,1024]{3,2,1,0:T(8,128)(2,1)} %all-gather.5.cloned.1.call-done), kind=kOutput, calls=%fused_computation.13 | convolution fusion | flops 2415919104 | bytes 9175040 | tf_op jit(solution)/shard_map/bhwc,pqcd->bhwpqd/dot_general | solution.py:14
  127.1 2.1 copy-done.1
  129.2 1.8 slice_bitcast_fusion.17
  130.9 28.0 %reduce-scatter.10.cloned.1.call-done = bf16[128,1024]{1,0:T(8,128)(2,1)} async-done(((bf16[1024,1024]{1,0:T(8,128)(2,1)}), bf16[128,1024]{1,0:T(8,128)(2,1)}) %reduce-scatter.10.cloned.1.call-update) | async-done | bytes 262160
  158.9 1.8 reshape.43
  160.7 1.8 copy.61
  162.5 2.3 multiply_convert_fusion
  164.8 0.8 multiply_convert_fusion.1
  165.7 0.2 reduce-scatter.6.cloned.1.call-start
  165.9 0.1 fusion.57
  166.0 0.1 fusion.61
  166.1 0.1 fusion.63
  166.3 0.1 fusion.65
  166.4 0.1 fusion.67
  166.5 0.1 fusion.71
  166.6 0.9 copy-done.5
  167.5 4.0 %fusion = bf16[3,3,1024,128]{2,3,1,0:T(8,128)(2,1)} fusion(bf16[32,32,3,3,128]{4,1,0,3,2:T(8,128)(2,1)S(1)} %bitcast.225, bf16[1,32,32,1024]{3,2,1,0:T(8,128)(2,1)S(1)} %copy-done.5), kind=kOutput, calls=%fused_computation.3 | convolution fusion | flops 2417098752 | bytes 6815744 | tf_op jit(solution)/shard_map/bhwc,bhwpqd->pqcd/dot_general | solution.py:39
  171.5 0.0 reduce-scatter.8.cloned.1.call-start
  171.6 23.8 %all-gather.9.cloned.1.call-done = bf16[1,32,32,1024]{3,2,1,0:T(8,128)(2,1)} async-done(((bf16[1,32,32,128]{3,2,1,0:T(8,128)(2,1)}), bf16[1,32,32,1024]{3,2,1,0:T(8,128)(2,1)}) %all-gather.9.cloned.1.call-update) | async-done | bytes 2097168 | tf_op jit(solution)/shard_map/all_gather | solution.py:47
  195.4 4.2 %fusion.4 = bf16[3,3,128,1024,1]{3,2,0,1,4:T(8,128)(2,1)S(1)} fusion(bf16[32,32,3,3,128]{4,1,0,3,2:T(8,128)(2,1)S(1)} %bitcast.224, bf16[1,32,32,1024]{3,2,1,0:T(8,128)(2,1)} %all-gather.9.cloned.1.call-done), kind=kOutput, calls=%fused_computation.7 | convolution fusion | flops 2415919104 | bytes 6815744 | tf_op jit(solution)/shard_map/bhwc,bhwpqd->pqcd/dot_general | solution.py:39
  199.6 1.7 copy.83
  201.4 1.6 copy-done.4
  203.0 4.8 %fusion.13 = f32[1,32,32,3,3,128]{5,2,4,3,1,0:T(8,128)S(1)} fusion(bf16[3,3,1024,128]{3,2,1,0:T(8,128)(2,1)S(1)} %copy-done.4, bf16[1,32,32,1024]{3,2,1,0:T(8,128)(2,1)} %all-gather.9.cloned.1.call-done), kind=kOutput, calls=%fused_computation.14 | convolution fusion | flops 2415919104 | bytes 9175040 | tf_op jit(solution)/shard_map/bhwc,pqcd->bhwpqd/dot_general | solution.py:14
  207.8 0.7 slice_bitcast_fusion
  208.5 1.3 fusion.39
  209.8 25.0 %reduce-scatter.6.cloned.1.call-done = bf16[3,3,256,128]{2,3,1,0:T(8,128)(2,1)} async-done(((bf16[3,3,1024,128]{2,3,1,0:T(8,128)(2,1)}), bf16[3,3,256,128]{2,3,1,0:T(8,128)(2,1)}) %reduce-scatter.6.cloned.1.call-update) | async-done | bytes 589840 | tf_op jit(solution)/shard_map/reduce_scatter | solution.py:62
  234.8 2.3 copy.45
  237.1 38.2 %reduce-scatter.8.cloned.1.call-done = bf16[3,3,256,128]{2,3,1,0:T(8,128)(2,1)} async-done(((bf16[3,3,1024,128]{2,3,1,0:T(8,128)(2,1)}), bf16[3,3,256,128]{2,3,1,0:T(8,128)(2,1)}) %reduce-scatter.8.cloned.1.call-update) | async-done | bytes 589840 | tf_op jit(solution)/shard_map/reduce_scatter | solution.py:50
  275.3 2.3 copy.46
  (20 shorter events, 0.3 us)
Async XLA Ops:
  7.2 4.3 %copy-start = (bf16[1,32,32,128]{3,2,1,0:T(8,128)(2,1)S(1)}, bf16[1,32,32,128]{3,2,1,0:T(8,128)(2,1)}, u32[]{:S(2)}) copy-start(bf16[1,32,32,128]{3,2,1,0:T(8,128)(2,1)} %param.7) | copy-start | bytes 786436
  7.2 42.9 %all-gather.11.cloned.1.call-start = ((), (), s32[]{:S(2)}) async-start(), calls=%async_computation.6 | async-start | bytes 2949120 | tf_op jit(solution)/shard_map/all_gather | solution.py:48
  7.9 81.5 %all-gather.7.cloned.1.call-start = ((), (), s32[]{:S(2)}) async-start(), calls=%async_computation.4 | async-start | bytes 2949120 | tf_op jit(solution)/shard_map/all_gather | solution.py:43
  8.7 113.2 %all-gather.5.cloned.1.call-start = ((), (), s32[]{:S(2)}) async-start(), calls=%async_computation.3 | async-start | bytes 2359296 | tf_op jit(solution)/shard_map/all_gather | solution.py:44
  9.4 149.5 %reduce-scatter.10.cloned.1.call-start = ((), (), s32[]{:S(2)}) async-start(), calls=%async_computation.9 | async-start | bytes 2359296
  12.1 38.0 %copy-start.2 = (bf16[1,32,32,9,128]{4,2,1,3,0:T(8,128)(2,1)}, bf16[1,32,32,9,128]{4,2,1,3,0:T(8,128)(2,1)S(1)}, u32[]{:S(2)}) copy-start(bf16[1,32,32,9,128]{4,2,1,3,0:T(8,128)(2,1)S(1)} %fusion.55) | copy-start | bytes 7077892
  80.0 115.4 %all-gather.9.cloned.1.call-start = ((), (), s32[]{:S(2)}) async-start(), calls=%async_computation.5 | async-start | bytes 2359296 | tf_op jit(solution)/shard_map/all_gather | solution.py:47
  127.1 2.1 copy-start.1
  165.7 69.1 %reduce-scatter.6.cloned.1.call-start = ((), (), s32[]{:S(2)}) async-start(), calls=%async_computation.7 | async-start | bytes 2949120 | tf_op jit(solution)/shard_map/reduce_scatter | solution.py:62
  165.9 1.6 copy-start.5
  171.5 23.9 %copy-start.3 = (bf16[1,32,32,9,128]{4,2,1,3,0:T(8,128)(2,1)S(1)}, bf16[1,32,32,9,128]{4,2,1,3,0:T(8,128)(2,1)}, u32[]{:S(2)}) copy-start(bf16[1,32,32,9,128]{4,2,1,3,0:T(8,128)(2,1)} %copy-done.2) | copy-start | bytes 7077892
  171.5 103.8 %reduce-scatter.8.cloned.1.call-start = ((), (), s32[]{:S(2)}) async-start(), calls=%async_computation.8 | async-start | bytes 2949120 | tf_op jit(solution)/shard_map/reduce_scatter | solution.py:50
  201.3 1.7 copy-start.4
Sparse Core Ops, SparseCore 0:
  9.9 40.1 all-gather.10
  51.9 37.4 all-gather.6
  91.0 30.8 all-gather.4
  124.0 34.8 reduce-scatter.9
  165.8 29.5 all-gather.8
  198.3 36.4 reduce-scatter.5
  237.9 37.3 reduce-scatter.7
where the time goes:
time: 285 us; the launch traced here: 284 us
  waiting for transfers between devices  197 us (69%)
  local copies, waits for them, and re-layouts  44.9 us (16%)
  matrix products  23.5 us (8%)
  between operations  14.3 us (5%)
  other arithmetic  4.4 us (2%)
    unnamed x34, local copies, waits for them, and re-layouts  40.6 us
    reduce_scatter x1, waiting for transfers between devices, body(): lax.psum_scatter(filter_grads(hidden_all, cotangent).astype(jnp.bfloat16)...  38.2 us
    all_gather x1, waiting for transfers between devices, body(): full_two = lax.all_gather(weight_two, 'dp', axis=2, tiled=True)  38 us
    all_gather x1, waiting for transfers between devices, body(): gathered = lax.all_gather(fields, 'filter', axis=3, tiled=True)  32.5 us
    unnamed x8, waiting for transfers between devices  30.1 us
    reduce_scatter x1, waiting for transfers between devices, body(): lax.psum_scatter(filter_grads(gathered, back_pre).astype(jnp.bfloat16), '...  25 us
    all_gather x1, waiting for transfers between devices, body(): hidden_all = lax.all_gather(hidden, 'filter', axis=3, tiled=True)  23.8 us
    dot_general x2, matrix products, conv_taps(): jnp.einsum('bhwc,pqcd->bhwpqd', inputs, weights, preferred_element_type=j...  9.99 us
  transfers between devices with their start and end apart: 7, of which 7 were waited for; matrix products, arithmetic and copies ran while one was open for 21% of the time, Pallas kernels for 0%

commit v1 on v0

--- a/solution.py
+++ b/solution.py
@@ -2,6 +2,93 @@
 import jax.numpy as jnp
 from jax import lax
 from jax.sharding import PartitionSpec as P
+
+
+def swap(values, axis, size, flip):
+    return lax.ppermute(values, axis, [(i, i ^ flip) for i in range(size)])
+
+
+def after(values, *earlier):
+    return lax.optimization_barrier((values,) + earlier)[0]
+
+
+def rank_blocks(values, axis, size, flips, dim):
+    held = [(0, values)]
+    for flip in flips:
+        held = held + [(k ^ flip, swap(v, axis, size, flip)) for k, v in held]
+    return held
+
+
+def place(held, axis, dim):
+    own = lax.axis_index(axis)
+    width = held[0][1].shape[dim]
+    shape = list(held[0][1].shape)
+    shape[dim] = width * len(held)
+    whole = jnp.zeros(shape, held[0][1].dtype)
+    for k, piece in held:
+        whole = lax.dynamic_update_slice_in_dim(whole, piece, (own ^ k) * width, dim)
+    return whole
+
+
+def bits(size):
+    return [1 << n for n in range(size.bit_length() - 1)]
+
+
+def gather_weights(weights, size):
+    if size != 4:
+        return place(rank_blocks(weights, "dp", size, bits(size), 2), "dp", 2)
+    half = weights.shape[2] // 2
+    along_x = swap(weights, "dp", size, 1)
+    along_y = swap(weights, "dp", size, 2)
+    far_low = swap(along_x[:, :, :half], "dp", size, 2)
+    far_high = swap(along_y[:, :, half:], "dp", size, 1)
+    far = jnp.concatenate([far_low, far_high], axis=2)
+    return place([(0, weights), (1, along_x), (2, along_y), (3, far)], "dp", 2)
+
+
+def gather_fields(values, size):
+    flips = bits(size)
+    held = rank_blocks(values, "filter", size, flips[:0:-1], 3)
+    stacked = jnp.stack([piece for unused, piece in held])
+    other = swap(stacked, "filter", size, 1)
+    held = held + [(k ^ 1, other[n]) for n, (k, unused) in enumerate(held)]
+    return place(held, "filter", 3)
+
+
+def fold(pieces, axis, size, flip):
+    keep = sorted(k for k in pieces if not k & flip)
+    got = swap(jnp.stack([pieces[k | flip] for k in keep]), axis, size, flip)
+    return {k: (pieces[k].astype(jnp.float32) + got[n].astype(jnp.float32)).astype(jnp.bfloat16) for n, k in enumerate(keep)}
+
+
+def scatter_fields(partial, size):
+    own = lax.axis_index("filter")
+    width = partial.shape[3] // size
+    pieces = {k: lax.dynamic_slice_in_dim(partial, (own ^ k) * width, width, 3) for k in range(size)}
+    for flip in bits(size):
+        pieces = fold(pieces, "filter", size, flip)
+    return pieces[0].astype(jnp.float32)
+
+
+def scatter_weights(partial, size):
+    own = lax.axis_index("dp")
+    width = partial.shape[2] // size
+    pieces = {k: lax.dynamic_slice_in_dim(partial, (own ^ k) * width, width, 2) for k in range(size)}
+    if size != 4:
+        for flip in bits(size):
+            pieces = fold(pieces, "dp", size, flip)
+        return pieces[0].astype(jnp.float32)
+    half = width // 2
+    low = {k: v[:, :, :half] for k, v in pieces.items()}
+    high = {k: v[:, :, half:] for k, v in pieces.items()}
+    over_x = swap(jnp.stack([low[3], low[1]]), "dp", size, 1)
+    over_y = swap(jnp.stack([high[3], high[2]]), "dp", size, 2)
+    wide = lambda v: v.astype(jnp.float32)
+    low_y = swap((wide(low[2]) + wide(over_x[0])).astype(jnp.bfloat16), "dp", size, 2)
+    high_x = swap((wide(high[1]) + wide(over_y[0])).astype(jnp.bfloat16), "dp", size, 1)
+    sum_low = wide(low[0]) + wide(over_x[1]) + wide(low_y)
+    sum_high = wide(high[0]) + wide(over_y[1]) + wide(high_x)
+    return jnp.concatenate([sum_low, sum_high], axis=2)
 
 
 def shift_cells(values, row_step, col_step):
@@ -39,33 +126,25 @@
     return jnp.einsum("bhwc,bhwpqd->pqcd", inputs, stacked, preferred_element_type=jnp.float32)
 
 
-def body(fields, weight_one, weight_two, cotangent):
-    full_one = lax.all_gather(weight_one, "dp", axis=2, tiled=True)
-    gathered = lax.all_gather(fields, "filter", axis=3, tiled=True)
+def body(n_dp, n_filter, fields, weight_one, weight_two, cotangent):
+    full_one = gather_weights(weight_one, n_dp)
+    gathered = gather_fields(fields, n_filter)
     pre_one = conv_taps(gathered, full_one)
     hidden = jax.nn.silu(pre_one).astype(jnp.bfloat16)
-    hidden_all = lax.all_gather(hidden, "filter", axis=3, tiled=True)
-    full_two = lax.all_gather(weight_two, "dp", axis=2, tiled=True)
+    full_two = gather_weights(after(weight_two, full_one), n_dp)
+    hidden_all = gather_fields(hidden, n_filter)
+    partial_back = transposed(cotangent, full_two)
     output = conv_taps(hidden_all, full_two).astype(jnp.bfloat16)
-    grad_two = lax.psum_scatter(
-        filter_grads(hidden_all, cotangent).astype(jnp.bfloat16),
-        "dp",
-        scatter_dimension=2,
-        tiled=True,
-    ).astype(jnp.float32)
-    partial_back = transposed(cotangent, full_two)
-    back = lax.psum_scatter(
-        partial_back.astype(jnp.bfloat16), "filter", scatter_dimension=3, tiled=True
-    ).astype(jnp.float32)
+    grad_two = scatter_weights(filter_grads(hidden_all, cotangent).astype(jnp.bfloat16), n_dp)
+    back = scatter_fields(partial_back.astype(jnp.bfloat16), n_filter)
     sigma = jax.nn.sigmoid(pre_one)
     back_pre = (back * sigma * (1.0 + pre_one * (1.0 - sigma))).astype(jnp.bfloat16)
-    grad_one = lax.psum_scatter(
-        filter_grads(gathered, back_pre).astype(jnp.bfloat16), "dp", scatter_dimension=2, tiled=True
-    ).astype(jnp.float32)
+    grad_one = scatter_weights(filter_grads(gathered, back_pre).astype(jnp.bfloat16), n_dp)
     return (output, grad_one, grad_two)
 
 
 def solution(mesh):
+    n_dp, n_filter = mesh.shape["dp"], mesh.shape["filter"]
     placed = (
         P("dp", None, None, "filter"),
         P(None, None, "dp", "filter"),
@@ -73,7 +152,7 @@
         P("dp", None, None, "filter"),
     )
     return jax.shard_map(
-        body,
+        lambda *arrays: body(n_dp, n_filter, *arrays),
         mesh=mesh,
         in_specs=placed,
         out_specs=(

time: 285 us -> 176 us (0.62)
  waiting for transfers between devices: 197 us -> 81.8 us
  starting transfers between devices: 0.46 us -> 28.8 us
  between operations: 14.3 us -> 1.12 us
  local copies, waits for them, and re-layouts: 44.9 us -> 34.1 us
  other arithmetic: 4.4 us -> 7.77 us
    all_gather x4 -> x0, waiting for transfers between devices: 104 us -> none  [the longest x1 38 us: body(): full_two = lax.all_gather(weight_two, 'dp', axis=2, tiled=True)]
    ppermute x0 -> x27, waiting for transfers between devices: none -> 81.8 us  [swap(): return lax.ppermute(values, axis, [(i, i ^ flip) for i in range(size)])]
    reduce_scatter x2 -> x0, waiting for transfers between devices: 63.2 us -> none  [the longest x1 38.2 us: body(): lax.psum_scatter(filter_grads(hidden_all, cotangent).astype(jnp.bfloat16)...]
    unnamed x8 -> x0, waiting for transfers between devices: 30.1 us -> none
    ppermute x0 -> x27, starting transfers between devices: none -> 28.8 us  [swap(): return lax.ppermute(values, axis, [(i, i ^ flip) for i in range(size)])]
    unnamed x34 -> x24, local copies, waits for them, and re-layouts: 40.6 us -> 14.2 us
    dynamic_update_slice x0 -> x21, local copies, waits for them, and re-layouts: none -> 11.2 us  [place(): lax.dynamic_update_slice_in_dim(whole, piece, (own ^ k) * width, dim)]
    another operation x0 -> x11, local copies, waits for them, and re-layouts: none -> 3.38 us
  transfers between devices with their start and end apart: 7 -> 27, of which waited for: 7 -> 14; matrix products, arithmetic and copies ran while one was open for 21% -> 29% of each run, Pallas kernels for 0% -> 0%
where the time goes in v1:
time: 176 us; the launch traced here: 175 us
  waiting for transfers between devices  81.8 us (46%)
  local copies, waits for them, and re-layouts  34.1 us (19%)
  starting transfers between devices  28.8 us (16%)
  matrix products  21.3 us (12%)
  other arithmetic  7.77 us (4%)
    ppermute x27, waiting for transfers between devices, swap(): return lax.ppermute(values, axis, [(i, i ^ flip) for i in range(size)])  81.8 us
    ppermute x27, starting transfers between devices, swap(): return lax.ppermute(values, axis, [(i, i ^ flip) for i in range(size)])  28.8 us
    unnamed x24, local copies, waits for them, and re-layouts  14.2 us
    dynamic_update_slice x21, local copies, waits for them, and re-layouts, place(): lax.dynamic_update_slice_in_dim(whole, piece, (own ^ k) * width, dim)  11.2 us
    dot_general x2, matrix products, filter_grads(): jnp.einsum('bhwc,bhwpqd->pqcd', inputs, stacked, preferred_element_type=j...  9 us
    dot_general x2, matrix products, conv_taps(): jnp.einsum('bhwc,pqcd->bhwpqd', inputs, weights, preferred_element_type=j...  7.33 us
    dot_general x1, matrix products, transposed(): jnp.einsum('bhwpqd,pqcd->bhwc', stacked, weights, preferred_element_type=...  4.99 us
  transfers between devices with their start and end apart: 27, of which 14 were waited for; matrix products, arithmetic and copies ran while one was open for 29% of the time, Pallas kernels for 0%

profile of v1, /device:TPU:0, one launch (start us, length us, event | category | flops | bytes accessed | tf_op | source)
XLA Modules:
  0.0 175.0 jit_solution(4782338841830293088)
XLA Ops:
  0.6 3.0 %collective-permute-start.4 = (bf16[3,3,256,128]{3,2,1,0:T(8,128)(2,1)}, bf16[3,3,256,128]{3,2,1,0:T(8,128)(2,1)S(1)}, u32[]{:S(2)}, u32[]{:S(2)}) collective-permute-start(bf16[3,3,256,128]{3,2,1,0:T(8,128)(2,1)} %param.5), channel_id=1, source_target_pairs={{0,8},{8,0},{16,24},{24,16},{1,9},{9,1},{17,25},{25,17},{2,10},{10... | collective-permute-start | bytes 1769480 | tf_op jit(solution)/shard_map/ppermute | solution.py:8
  3.6 1.5 collective-permute-start.5
  5.2 2.6 %collective-permute-start = (bf16[1,32,32,128]{3,2,1,0:T(8,128)(2,1)}, bf16[1,32,32,128]{3,2,1,0:T(8,128)(2,1)}, u32[]{:S(2)}, u32[]{:S(2)}) collective-permute-start(bf16[1,32,32,128]{3,2,1,0:T(8,128)(2,1)} %param.4), channel_id=1, source_target_pairs={{0,4},{1,5},{2,6},{3,7},{4,0},{5,1},{6,2},{7,3},{8,12},{9,13},{10,... | collective-permute-start | bytes 786440 | tf_op jit(solution)/shard_map/ppermute | solution.py:8
  7.8 1.6 collective-permute-start.1
  9.3 1.7 fusion.55
  11.1 1.7 fusion.57
  12.7 1.8 %fusion.59 = bf16[1,32,32,9,128]{4,2,1,3,0:T(8,128)(2,1)} fusion(bf16[1,32,32,9,128]{4,2,1,3,0:T(8,128)(2,1)} %fusion.57, bf16[1,32,32,128]{3,2,1,0:T(8,128)(2,1)} %param.7), kind=kLoop, calls=%fused_computation.160 | loop fusion | bytes 524288
  14.5 1.7 fusion.61
  16.2 1.7 bitcast_dynamic-update-slice_fusion.1
  19.5 1.6 broadcast.48.clone
  22.9 1.1 constant_dynamic-update-slice_fusion.5
  25.3 1.7 slice.386
  28.9 1.1 constant_dynamic-update-slice_fusion.3
  30.1 2.7 %collective-permute-done.6 = bf16[3,3,128,128]{3,2,1,0:T(8,128)(2,1)} collective-permute-done((bf16[3,3,128,128]{3,2,1,0:T(8,128)(2,1)}, bf16[3,3,128,128]{3,2,1,0:T(8,128)(2,1)}, u32[]{:S(2)}, u32[]{:S(2)}) %collective-permute-start.6) | collective-permute-done | bytes 294944 | tf_op jit(solution)/shard_map/ppermute | solution.py:8
  32.8 1.9 %collective-permute-done.7 = bf16[3,3,128,128]{3,2,1,0:T(8,128)(2,1)} collective-permute-done((bf16[3,3,128,128]{3,2,1,0:T(8,128)(2,1)}, bf16[3,3,128,128]{3,2,1,0:T(8,128)(2,1)}, u32[]{:S(2)}, u32[]{:S(2)}) %collective-permute-start.7) | collective-permute-done | bytes 294944 | tf_op jit(solution)/shard_map/ppermute | solution.py:8
  34.7 1.1 maximum_dynamic-update-slice_fusion
  36.4 1.5 collective-permute-start.13
  38.0 1.7 bitcast_dynamic-update-slice_fusion.8
  39.7 1.7 bitcast_dynamic-update-slice_fusion.7
  41.4 1.2 pad_maximum_fusion.2
  42.6 6.0 %collective-permute-done.12 = bf16[3,3,256,128]{3,2,1,0:T(8,128)(2,1)S(1)} collective-permute-done((bf16[3,3,256,128]{3,2,1,0:T(8,128)(2,1)S(1)}, bf16[3,3,256,128]{3,2,1,0:T(8,128)(2,1)S(1)}, u32[]{:S(2)}, u32[]{:S(2)}) %collective-permute-start.12) | collective-permute-done | bytes 589856 | tf_op jit(solution)/shard_map/ppermute | solution.py:8
  48.7 1.9 %collective-permute-start.14 = (bf16[3,3,128,128]{3,2,1,0:T(8,128)(2,1)S(1)}, bf16[3,3,128,128]{3,2,1,0:T(8,128)(2,1)S(1)}, u32[]{:S(2)}, u32[]{:S(2)}) collective-permute-start(bf16[3,3,128,128]{3,2,1,0:T(8,128)(2,1)S(1)} %slice.400), channel_id=1, source_target_pairs={{0,16},{8,24},{16,0},{24,8},{1,17},{9,25},{17,1},{25,9},{2,18},{10... | collective-permute-start | bytes 884744 | tf_op jit(solution)/shard_map/ppermute | solution.py:8
  50.6 1.7 collective-permute-start.15
  53.0 2.5 %collective-permute-done.14 = bf16[3,3,128,128]{3,2,1,0:T(8,128)(2,1)S(1)} collective-permute-done((bf16[3,3,128,128]{3,2,1,0:T(8,128)(2,1)S(1)}, bf16[3,3,128,128]{3,2,1,0:T(8,128)(2,1)S(1)}, u32[]{:S(2)}, u32[]{:S(2)}) %collective-permute-start.14) | collective-permute-done | bytes 294944 | tf_op jit(solution)/shard_map/ppermute | solution.py:8
  55.5 1.9 %collective-permute-done.15 = bf16[3,3,128,128]{3,2,1,0:T(8,128)(2,1)S(1)} collective-permute-done((bf16[3,3,128,128]{3,2,1,0:T(8,128)(2,1)S(1)}, bf16[3,3,128,128]{3,2,1,0:T(8,128)(2,1)S(1)}, u32[]{:S(2)}, u32[]{:S(2)}) %collective-permute-start.15) | collective-permute-done | bytes 294944 | tf_op jit(solution)/shard_map/ppermute | solution.py:8
  57.5 5.0 %bitcast_convert_fusion.2 = bf16[32,32,1024]{2,1,0:T(8,128)(2,1)S(1)} fusion(bf16[32,32,3,3,128]{4,1,0,3,2:T(8,128)(2,1)} %bitcast.60, bf16[3,3,1024,128]{3,2,1,0:T(8,128)(2,1)S(1)} %maximum_dynamic-update-slice_fusion.1), kind=kOutput, calls=%fused_computation.2 | convolution fusion | flops 2416967680 | bytes 6815744 | tf_op jit(solution)/shard_map/bhwpqd,pqcd->bhwc/dot_general | solution.py:121
  67.5 4.5 %fusion.8 = f32[1,32,32,3,3,128]{5,2,4,3,1,0:T(8,128)S(1)} fusion(bf16[3,3,1024,128]{3,2,1,0:T(8,128)(2,1)S(1)} %maximum_dynamic-update-slice_fusion, bf16[32,32,1024]{2,1,0:T(8,128)(2,1)} %fusion.94), kind=kOutput, calls=%fused_computation.11 | convolution fusion | flops 2415919104 | bytes 9175040 | tf_op jit(solution)/shard_map/bhwc,pqcd->bhwpqd/dot_general | solution.py:101
  72.0 9.4 %collective-permute-done.17 = bf16[2,1,32,32,128]{4,3,2,1,0:T(8,128)(2,1)S(1)} collective-permute-done((bf16[2,1,32,32,128]{4,3,2,1,0:T(8,128)(2,1)S(1)}, bf16[2,1,32,32,128]{4,3,2,1,0:T(8,128)(2,1)S(1)}, u32[]{:S(2)}, u32[]{:S(2)}) %collective-permute-start.17) | collective-permute-done | bytes 524320 | tf_op jit(solution)/shard_map/ppermute | solution.py:8
  82.6 13.3 %collective-permute-done.18 = bf16[1,1,32,32,128]{4,3,2,1,0:T(8,128)(2,1)S(1)} collective-permute-done((bf16[1,1,32,32,128]{4,3,2,1,0:T(8,128)(2,1)S(1)}, bf16[1,1,32,32,128]{4,3,2,1,0:T(8,128)(2,1)S(1)}, u32[]{:S(2)}, u32[]{:S(2)}) %collective-permute-start.18) | collective-permute-done | bytes 262176 | tf_op jit(solution)/shard_map/ppermute | solution.py:8
  98.6 10.2 %collective-permute-done.8 = bf16[1,32,32,128]{3,2,1,0:T(8,128)(2,1)S(1)} collective-permute-done((bf16[1,32,32,128]{3,2,1,0:T(8,128)(2,1)S(1)}, bf16[1,32,32,128]{3,2,1,0:T(8,128)(2,1)S(1)}, u32[]{:S(2)}, u32[]{:S(2)}) %collective-permute-start.8) | collective-permute-done | bytes 262176 | tf_op jit(solution)/shard_map/ppermute | solution.py:8
  109.0 2.1 %collective-permute-done.9 = bf16[1,32,32,128]{3,2,1,0:T(8,128)(2,1)S(1)} collective-permute-done((bf16[1,32,32,128]{3,2,1,0:T(8,128)(2,1)S(1)}, bf16[1,32,32,128]{3,2,1,0:T(8,128)(2,1)S(1)}, u32[]{:S(2)}, u32[]{:S(2)}) %collective-permute-start.9) | collective-permute-done | bytes 262176 | tf_op jit(solution)/shard_map/ppermute | solution.py:8
  111.1 5.8 %collective-permute-done.10 = bf16[1,32,32,128]{3,2,1,0:T(8,128)(2,1)S(1)} collective-permute-done((bf16[1,32,32,128]{3,2,1,0:T(8,128)(2,1)S(1)}, bf16[1,32,32,128]{3,2,1,0:T(8,128)(2,1)S(1)}, u32[]{:S(2)}, u32[]{:S(2)}) %collective-permute-start.10) | collective-permute-done | bytes 262176 | tf_op jit(solution)/shard_map/ppermute | solution.py:8
  117.1 4.2 %bitcast_convert_fusion.1 = bf16[3,3,128,1024]{3,2,1,0:T(8,128)(2,1)S(1)} fusion(bf16[32,32,3,3,128]{4,1,0,3,2:T(8,128)(2,1)S(1)} %bitcast.386, bf16[32,32,1024]{2,1,0:T(8,128)(2,1)} %fusion.94), kind=kOutput, calls=%fused_computation.1 | convolution fusion | flops 2417098752 | bytes 6815744 | tf_op jit(solution)/shard_map/bhwc,bhwpqd->pqcd/dot_general | solution.py:126
  122.1 4.8 %fusion.2 = bf16[3,3,128,1024,1]{3,2,0,1,4:T(8,128)(2,1)S(1)} fusion(bf16[32,32,3,3,128]{4,1,0,3,2:T(8,128)(2,1)} %bitcast.60, bf16[32,32,1024]{2,1,0:T(8,128)(2,1)S(1)} %fusion.90), kind=kOutput, calls=%fused_computation.5 | convolution fusion | flops 2415919104 | bytes 6815744 | tf_op jit(solution)/shard_map/bhwc,bhwpqd->pqcd/dot_general | solution.py:126
  126.8 2.9 %fusion.11 = f32[1,32,32,3,3,128]{5,2,4,3,1,0:T(8,128)S(1)} fusion(bf16[3,3,1024,128]{3,2,1,0:T(8,128)(2,1)S(1)} %maximum_dynamic-update-slice_fusion.1, bf16[32,32,1024]{2,1,0:T(8,128)(2,1)S(1)} %fusion.90), kind=kOutput, calls=%fused_computation.12 | convolution fusion | flops 2415919104 | bytes 9175040 | tf_op jit(solution)/shard_map/bhwc,pqcd->bhwpqd/dot_general | solution.py:101
  130.8 1.2 collective-permute-start.25
  132.2 2.1 %collective-permute-start.23 = (bf16[2,3,3,128,128]{3,4,2,1,0:T(8,128)(2,1)S(1)}, bf16[2,3,3,128,128]{3,4,2,1,0:T(8,128)(2,1)S(1)}, u32[]{:S(2)}, u32[]{:S(2)}) collective-permute-start(bf16[2,3,3,128,128]{3,4,2,1,0:T(8,128)(2,1)S(1)} %pad_maximum_fusion.7), channel_id=1, source_target_pairs={{0,8},{8,0},{16,24},{24,16},{1,9},{9,1},{17,25},{25,17},{2,10},{10... | collective-permute-start | bytes 1769480 | tf_op jit(solution)/shard_map/ppermute | solution.py:8
  136.2 1.3 fusion.44
  137.5 9.5 %collective-permute-done.25 = bf16[2,3,3,128,128]{3,4,2,1,0:T(8,128)(2,1)S(1)} collective-permute-done((bf16[2,3,3,128,128]{3,4,2,1,0:T(8,128)(2,1)S(1)}, bf16[2,3,3,128,128]{3,4,2,1,0:T(8,128)(2,1)S(1)}, u32[]{:S(2)}, u32[]{:S(2)}) %collective-permute-start.25) | collective-permute-done | bytes 589856 | tf_op jit(solution)/shard_map/ppermute | solution.py:8
  147.1 1.7 collective-permute-start.26
  148.9 1.6 collective-permute-start.24
  150.5 9.1 %collective-permute-done.21 = bf16[2,3,3,128,128]{3,4,2,1,0:T(8,128)(2,1)S(1)} collective-permute-done((bf16[2,3,3,128,128]{3,4,2,1,0:T(8,128)(2,1)S(1)}, bf16[2,3,3,128,128]{3,4,2,1,0:T(8,128)(2,1)S(1)}, u32[]{:S(2)}, u32[]{:S(2)}) %collective-permute-start.21) | collective-permute-done | bytes 589856 | tf_op jit(solution)/shard_map/ppermute | solution.py:8
  160.5 1.6 collective-permute-start.22
  162.9 1.6 collective-permute-start.20
  164.5 2.9 %collective-permute-done.26 = bf16[3,3,128,128]{2,3,1,0:T(8,128)(2,1)S(1)} collective-permute-done((bf16[3,3,128,128]{2,3,1,0:T(8,128)(2,1)S(1)}, bf16[3,3,128,128]{2,3,1,0:T(8,128)(2,1)S(1)}, u32[]{:S(2)}, u32[]{:S(2)}) %collective-permute-start.26) | collective-permute-done | bytes 294944 | tf_op jit(solution)/shard_map/ppermute | solution.py:8
  167.7 1.4 copy.26
  169.1 4.2 %collective-permute-done.22 = bf16[3,3,128,128]{2,3,1,0:T(8,128)(2,1)S(1)} collective-permute-done((bf16[3,3,128,128]{2,3,1,0:T(8,128)(2,1)}, bf16[3,3,128,128]{2,3,1,0:T(8,128)(2,1)S(1)}, u32[]{:S(2)}, u32[]{:S(2)}) %collective-permute-start.22) | collective-permute-done | bytes 294944 | tf_op jit(solution)/shard_map/ppermute | solution.py:8
  173.6 1.4 copy.25
  (100 shorter events, 23.2 us)
Async XLA Ops:
  0.6 17.3 %copy-start = (bf16[1,32,32,128]{3,2,1,0:T(8,128)(2,1)S(1)}, bf16[1,32,32,128]{3,2,1,0:T(8,128)(2,1)}, u32[]{:S(2)}) copy-start(bf16[1,32,32,128]{3,2,1,0:T(8,128)(2,1)} %param.7) | copy-start | bytes 786436
  0.6 23.4 %collective-permute-start.4 = (bf16[3,3,256,128]{3,2,1,0:T(8,128)(2,1)}, bf16[3,3,256,128]{3,2,1,0:T(8,128)(2,1)S(1)}, u32[]{:S(2)}, u32[]{:S(2)}) collective-permute-start(bf16[3,3,256,128]{3,2,1,0:T(8,128)(2,1)} %param.5), channel_id=1, source_target_pairs={{0,8},{8,0},{16,24},{24,16},{1,9},{9,1},{17,25},{25,17},{2,10},{10... | collective-permute-start | bytes 1769480 | tf_op jit(solution)/shard_map/ppermute | solution.py:8
  3.6 21.7 %collective-permute-start.5 = (bf16[3,3,256,128]{3,2,1,0:T(8,128)(2,1)}, bf16[3,3,256,128]{3,2,1,0:T(8,128)(2,1)}, u32[]{:S(2)}, u32[]{:S(2)}) collective-permute-start(bf16[3,3,256,128]{3,2,1,0:T(8,128)(2,1)} %param.5), channel_id=1, source_target_pairs={{0,16},{8,24},{16,0},{24,8},{1,17},{9,25},{17,1},{25,9},{2,18},{10... | collective-permute-start | bytes 1769480 | tf_op jit(solution)/shard_map/ppermute | solution.py:8
  5.2 23.2 %collective-permute-start = (bf16[1,32,32,128]{3,2,1,0:T(8,128)(2,1)}, bf16[1,32,32,128]{3,2,1,0:T(8,128)(2,1)}, u32[]{:S(2)}, u32[]{:S(2)}) collective-permute-start(bf16[1,32,32,128]{3,2,1,0:T(8,128)(2,1)} %param.4), channel_id=1, source_target_pairs={{0,4},{1,5},{2,6},{3,7},{4,0},{5,1},{6,2},{7,3},{8,12},{9,13},{10,... | collective-permute-start | bytes 786440 | tf_op jit(solution)/shard_map/ppermute | solution.py:8
  7.8 31.9 %collective-permute-start.1 = (bf16[1,32,32,128]{3,2,1,0:T(8,128)(2,1)}, bf16[1,32,32,128]{3,2,1,0:T(8,128)(2,1)}, u32[]{:S(2)}, u32[]{:S(2)}) collective-permute-start(bf16[1,32,32,128]{3,2,1,0:T(8,128)(2,1)} %param.4), channel_id=1, source_target_pairs={{0,2},{1,3},{2,0},{3,1},{4,6},{5,7},{6,4},{7,5},{8,10},{9,11},{10,... | collective-permute-start | bytes 786440 | tf_op jit(solution)/shard_map/ppermute | solution.py:8
  12.7 8.4 %copy-start.1 = (bf16[1,32,32,128]{3,2,1,0:T(8,128)(2,1)S(1)}, bf16[1,32,32,128]{3,2,1,0:T(8,128)(2,1)}, u32[]{:S(2)}) copy-start(bf16[1,32,32,128]{3,2,1,0:T(8,128)(2,1)} %param.4) | copy-start | bytes 786436
  24.8 8.0 %collective-permute-start.6 = (bf16[3,3,128,128]{3,2,1,0:T(8,128)(2,1)}, bf16[3,3,128,128]{3,2,1,0:T(8,128)(2,1)}, u32[]{:S(2)}, u32[]{:S(2)}) collective-permute-start(bf16[3,3,128,128]{3,2,1,0:T(8,128)(2,1)} %slice.385), channel_id=1, source_target_pairs={{0,16},{8,24},{16,0},{24,8},{1,17},{9,25},{17,1},{25,9},{2,18},{10... | collective-permute-start | bytes 884744 | tf_op jit(solution)/shard_map/ppermute | solution.py:8
  27.0 7.7 %collective-permute-start.7 = (bf16[3,3,128,128]{3,2,1,0:T(8,128)(2,1)}, bf16[3,3,128,128]{3,2,1,0:T(8,128)(2,1)}, u32[]{:S(2)}, u32[]{:S(2)}) collective-permute-start(bf16[3,3,128,128]{3,2,1,0:T(8,128)(2,1)} %slice.386), channel_id=1, source_target_pairs={{0,8},{8,0},{16,24},{24,16},{1,9},{9,1},{17,25},{25,17},{2,10},{10... | collective-permute-start | bytes 884744 | tf_op jit(solution)/shard_map/ppermute | solution.py:8
  28.3 7.5 %copy-start.2 = (bf16[3,3,256,128]{3,2,1,0:T(8,128)(2,1)S(1)}, bf16[3,3,256,128]{3,2,1,0:T(8,128)(2,1)}, u32[]{:S(2)}) copy-start(bf16[3,3,256,128]{3,2,1,0:T(8,128)(2,1)} %param.6) | copy-start | bytes 1769476
  28.3 13.0 %collective-permute-start.2 = (bf16[1,32,32,128]{3,2,1,0:T(8,128)(2,1)}, bf16[1,32,32,128]{3,2,1,0:T(8,128)(2,1)S(1)}, u32[]{:S(2)}, u32[]{:S(2)}) collective-permute-start(bf16[1,32,32,128]{3,2,1,0:T(8,128)(2,1)} %collective-permute-done), channel_id=1, source_target_pairs={{0,2},{1,3},{2,0},{3,1},{4,6},{5,7},{6,4},{7,5},{8,10},{9,11},{10,... | collective-permute-start | bytes 786440 | tf_op jit(solution)/shard_map/ppermute | solution.py:8
  35.8 12.8 %collective-permute-start.12 = (bf16[3,3,256,128]{3,2,1,0:T(8,128)(2,1)S(1)}, bf16[3,3,256,128]{3,2,1,0:T(8,128)(2,1)S(1)}, u32[]{:S(2)}, u32[]{:S(2)}) collective-permute-start(bf16[3,3,256,128]{3,2,1,0:T(8,128)(2,1)S(1)} %copy-done.2), channel_id=1, source_target_pairs={{0,8},{8,0},{16,24},{24,16},{1,9},{9,1},{17,25},{25,17},{2,10},{10... | collective-permute-start | bytes 1769480 | tf_op jit(solution)/shard_map/ppermute | solution.py:8
  36.4 14.2 %collective-permute-start.13 = (bf16[3,3,256,128]{3,2,1,0:T(8,128)(2,1)S(1)}, bf16[3,3,256,128]{3,2,1,0:T(8,128)(2,1)S(1)}, u32[]{:S(2)}, u32[]{:S(2)}) collective-permute-start(bf16[3,3,256,128]{3,2,1,0:T(8,128)(2,1)S(1)} %copy-done.2), channel_id=1, source_target_pairs={{0,16},{8,24},{16,0},{24,8},{1,17},{9,25},{17,1},{25,9},{2,18},{10... | collective-permute-start | bytes 1769480 | tf_op jit(solution)/shard_map/ppermute | solution.py:8
  42.6 21.2 %collective-permute-start.3 = (bf16[4,1,32,32,128]{4,3,2,1,0:T(8,128)(2,1)S(1)}, bf16[4,1,32,32,128]{4,3,2,1,0:T(8,128)(2,1)S(1)}, u32[]{:S(2)}, u32[]{:S(2)}) collective-permute-start(bf16[4,1,32,32,128]{4,3,2,1,0:T(8,128)(2,1)S(1)} %pad_maximum_fusion.2), channel_id=1, source_target_pairs={{0,1},{1,0},{2,3},{3,2},{4,5},{5,4},{6,7},{7,6},{8,9},{9,8},{10,11... | collective-permute-start | bytes 3145736 | tf_op jit(solution)/shard_map/ppermute | solution.py:8
  48.7 6.8 %collective-permute-start.14 = (bf16[3,3,128,128]{3,2,1,0:T(8,128)(2,1)S(1)}, bf16[3,3,128,128]{3,2,1,0:T(8,128)(2,1)S(1)}, u32[]{:S(2)}, u32[]{:S(2)}) collective-permute-start(bf16[3,3,128,128]{3,2,1,0:T(8,128)(2,1)S(1)} %slice.400), channel_id=1, source_target_pairs={{0,16},{8,24},{16,0},{24,8},{1,17},{9,25},{17,1},{25,9},{2,18},{10... | collective-permute-start | bytes 884744 | tf_op jit(solution)/shard_map/ppermute | solution.py:8
  50.6 6.8 %collective-permute-start.15 = (bf16[3,3,128,128]{3,2,1,0:T(8,128)(2,1)S(1)}, bf16[3,3,128,128]{3,2,1,0:T(8,128)(2,1)S(1)}, u32[]{:S(2)}, u32[]{:S(2)}) collective-permute-start(bf16[3,3,128,128]{3,2,1,0:T(8,128)(2,1)S(1)} %slice.401), channel_id=1, source_target_pairs={{0,8},{8,0},{16,24},{24,16},{1,9},{9,1},{17,25},{25,17},{2,10},{10... | collective-permute-start | bytes 884744 | tf_op jit(solution)/shard_map/ppermute | solution.py:8
  62.9 3.9 %collective-permute-start.16 = (bf16[4,1,32,32,128]{4,3,2,1,0:T(8,128)(2,1)S(1)}, bf16[4,1,32,32,128]{4,3,2,1,0:T(8,128)(2,1)S(1)}, u32[]{:S(2)}, u32[]{:S(2)}) collective-permute-start(bf16[4,1,32,32,128]{4,3,2,1,0:T(8,128)(2,1)S(1)} %pad_maximum_fusion.4), channel_id=1, source_target_pairs={{0,1},{1,0},{2,3},{3,2},{4,5},{5,4},{6,7},{7,6},{8,9},{9,8},{10,11... | collective-permute-start | bytes 3145736 | tf_op jit(solution)/shard_map/ppermute | solution.py:8
  67.0 14.4 %collective-permute-start.17 = (bf16[2,1,32,32,128]{4,3,2,1,0:T(8,128)(2,1)S(1)}, bf16[2,1,32,32,128]{4,3,2,1,0:T(8,128)(2,1)S(1)}, u32[]{:S(2)}, u32[]{:S(2)}) collective-permute-start(bf16[2,1,32,32,128]{4,3,2,1,0:T(8,128)(2,1)S(1)} %pad_maximum_fusion.9), channel_id=1, source_target_pairs={{0,2},{1,3},{2,0},{3,1},{4,6},{5,7},{6,4},{7,5},{8,10},{9,11},{10,... | collective-permute-start | bytes 1572872 | tf_op jit(solution)/shard_map/ppermute | solution.py:8
  81.5 14.4 %collective-permute-start.18 = (bf16[1,1,32,32,128]{4,3,2,1,0:T(8,128)(2,1)S(1)}, bf16[1,1,32,32,128]{4,3,2,1,0:T(8,128)(2,1)S(1)}, u32[]{:S(2)}, u32[]{:S(2)}) collective-permute-start(bf16[1,1,32,32,128]{4,3,2,1,0:T(8,128)(2,1)S(1)} %fusion.88), channel_id=1, source_target_pairs={{0,4},{1,5},{2,6},{3,7},{4,0},{5,1},{6,2},{7,3},{8,12},{9,13},{10,... | collective-permute-start | bytes 786440 | tf_op jit(solution)/shard_map/ppermute | solution.py:8
  97.1 11.7 %collective-permute-start.8 = (bf16[1,32,32,128]{3,2,1,0:T(8,128)(2,1)S(1)}, bf16[1,32,32,128]{3,2,1,0:T(8,128)(2,1)S(1)}, u32[]{:S(2)}, u32[]{:S(2)}) collective-permute-start(bf16[1,32,32,128]{3,2,1,0:T(8,128)(2,1)S(1)} %get-tuple-element.11), channel_id=1, source_target_pairs={{0,4},{1,5},{2,6},{3,7},{4,0},{5,1},{6,2},{7,3},{8,12},{9,13},{10,... | collective-permute-start | bytes 786440 | tf_op jit(solution)/shard_map/ppermute | solution.py:8
  97.2 13.9 %collective-permute-start.9 = (bf16[1,32,32,128]{3,2,1,0:T(8,128)(2,1)S(1)}, bf16[1,32,32,128]{3,2,1,0:T(8,128)(2,1)S(1)}, u32[]{:S(2)}, u32[]{:S(2)}) collective-permute-start(bf16[1,32,32,128]{3,2,1,0:T(8,128)(2,1)S(1)} %get-tuple-element.11), channel_id=1, source_target_pairs={{0,2},{1,3},{2,0},{3,1},{4,6},{5,7},{6,4},{7,5},{8,10},{9,11},{10,... | collective-permute-start | bytes 786440 | tf_op jit(solution)/shard_map/ppermute | solution.py:8
  108.8 8.2 %collective-permute-start.10 = (bf16[1,32,32,128]{3,2,1,0:T(8,128)(2,1)S(1)}, bf16[1,32,32,128]{3,2,1,0:T(8,128)(2,1)S(1)}, u32[]{:S(2)}, u32[]{:S(2)}) collective-permute-start(bf16[1,32,32,128]{3,2,1,0:T(8,128)(2,1)S(1)} %collective-permute-done.8), channel_id=1, source_target_pairs={{0,2},{1,3},{2,0},{3,1},{4,6},{5,7},{6,4},{7,5},{8,10},{9,11},{10,... | collective-permute-start | bytes 786440 | tf_op jit(solution)/shard_map/ppermute | solution.py:8
  117.1 4.6 %collective-permute-start.11 = (bf16[4,1,32,32,128]{4,3,2,1,0:T(8,128)(2,1)S(1)}, bf16[4,1,32,32,128]{4,3,2,1,0:T(8,128)(2,1)S(1)}, u32[]{:S(2)}, u32[]{:S(2)}) collective-permute-start(bf16[4,1,32,32,128]{4,3,2,1,0:T(8,128)(2,1)S(1)} %pad_maximum_fusion.3), channel_id=1, source_target_pairs={{0,1},{1,0},{2,3},{3,2},{4,5},{5,4},{6,7},{7,6},{8,9},{9,8},{10,11... | collective-permute-start | bytes 3145736 | tf_op jit(solution)/shard_map/ppermute | solution.py:8
  130.8 16.2 %collective-permute-start.25 = (bf16[2,3,3,128,128]{3,4,2,1,0:T(8,128)(2,1)S(1)}, bf16[2,3,3,128,128]{3,4,2,1,0:T(8,128)(2,1)S(1)}, u32[]{:S(2)}, u32[]{:S(2)}) collective-permute-start(bf16[2,3,3,128,128]{3,4,2,1,0:T(8,128)(2,1)S(1)} %pad_maximum_fusion.8), channel_id=1, source_target_pairs={{0,16},{8,24},{16,0},{24,8},{1,17},{9,25},{17,1},{25,9},{2,18},{10... | collective-permute-start | bytes 1769480 | tf_op jit(solution)/shard_map/ppermute | solution.py:8
  132.2 16.6 %collective-permute-start.23 = (bf16[2,3,3,128,128]{3,4,2,1,0:T(8,128)(2,1)S(1)}, bf16[2,3,3,128,128]{3,4,2,1,0:T(8,128)(2,1)S(1)}, u32[]{:S(2)}, u32[]{:S(2)}) collective-permute-start(bf16[2,3,3,128,128]{3,4,2,1,0:T(8,128)(2,1)S(1)} %pad_maximum_fusion.7), channel_id=1, source_target_pairs={{0,8},{8,0},{16,24},{24,16},{1,9},{9,1},{17,25},{25,17},{2,10},{10... | collective-permute-start | bytes 1769480 | tf_op jit(solution)/shard_map/ppermute | solution.py:8
  134.6 25.1 %collective-permute-start.21 = (bf16[2,3,3,128,128]{3,4,2,1,0:T(8,128)(2,1)S(1)}, bf16[2,3,3,128,128]{3,4,2,1,0:T(8,128)(2,1)S(1)}, u32[]{:S(2)}, u32[]{:S(2)}) collective-permute-start(bf16[2,3,3,128,128]{3,4,2,1,0:T(8,128)(2,1)S(1)} %pad_maximum_fusion.6), channel_id=1, source_target_pairs={{0,16},{8,24},{16,0},{24,8},{1,17},{9,25},{17,1},{25,9},{2,18},{10... | collective-permute-start | bytes 1769480 | tf_op jit(solution)/shard_map/ppermute | solution.py:8
  135.2 26.9 %collective-permute-start.19 = (bf16[2,3,3,128,128]{3,4,2,1,0:T(8,128)(2,1)S(1)}, bf16[2,3,3,128,128]{3,4,2,1,0:T(8,128)(2,1)S(1)}, u32[]{:S(2)}, u32[]{:S(2)}) collective-permute-start(bf16[2,3,3,128,128]{3,4,2,1,0:T(8,128)(2,1)S(1)} %pad_maximum_fusion.5), channel_id=1, source_target_pairs={{0,8},{8,0},{16,24},{24,16},{1,9},{9,1},{17,25},{25,17},{2,10},{10... | collective-permute-start | bytes 1769480 | tf_op jit(solution)/shard_map/ppermute | solution.py:8
  147.1 20.2 %collective-permute-start.26 = (bf16[3,3,128,128]{2,3,1,0:T(8,128)(2,1)S(1)}, bf16[3,3,128,128]{2,3,1,0:T(8,128)(2,1)S(1)}, u32[]{:S(2)}, u32[]{:S(2)}) collective-permute-start(bf16[3,3,128,128]{2,3,1,0:T(8,128)(2,1)S(1)} %fusion.20), channel_id=1, source_target_pairs={{0,8},{8,0},{16,24},{24,16},{1,9},{9,1},{17,25},{25,17},{2,10},{10... | collective-permute-start | bytes 884744 | tf_op jit(solution)/shard_map/ppermute | solution.py:8
  148.9 18.4 %collective-permute-start.24 = (bf16[3,3,128,128]{2,3,1,0:T(8,128)(2,1)S(1)}, bf16[3,3,128,128]{2,3,1,0:T(8,128)(2,1)S(1)}, u32[]{:S(2)}, u32[]{:S(2)}) collective-permute-start(bf16[3,3,128,128]{2,3,1,0:T(8,128)(2,1)S(1)} %fusion.22), channel_id=1, source_target_pairs={{0,16},{8,24},{16,0},{24,8},{1,17},{9,25},{17,1},{25,9},{2,18},{10... | collective-permute-start | bytes 884744 | tf_op jit(solution)/shard_map/ppermute | solution.py:8
  160.5 12.8 %collective-permute-start.22 = (bf16[3,3,128,128]{2,3,1,0:T(8,128)(2,1)}, bf16[3,3,128,128]{2,3,1,0:T(8,128)(2,1)S(1)}, u32[]{:S(2)}, u32[]{:S(2)}) collective-permute-start(bf16[3,3,128,128]{2,3,1,0:T(8,128)(2,1)} %fusion.24), channel_id=1, source_target_pairs={{0,8},{8,0},{16,24},{24,16},{1,9},{9,1},{17,25},{25,17},{2,10},{10... | collective-permute-start | bytes 884744 | tf_op jit(solution)/shard_map/ppermute | solution.py:8
  162.9 10.4 %collective-permute-start.20 = (bf16[3,3,128,128]{2,3,1,0:T(8,128)(2,1)}, bf16[3,3,128,128]{2,3,1,0:T(8,128)(2,1)S(1)}, u32[]{:S(2)}, u32[]{:S(2)}) collective-permute-start(bf16[3,3,128,128]{2,3,1,0:T(8,128)(2,1)} %fusion.26), channel_id=1, source_target_pairs={{0,16},{8,24},{16,0},{24,8},{1,17},{9,25},{17,1},{25,9},{2,18},{10... | collective-permute-start | bytes 884744 | tf_op jit(solution)/shard_map/ppermute | solution.py:8

commit v2 on v1

--- a/solution.py
+++ b/solution.py
@@ -1,7 +1,16 @@
+import functools
+
 import jax
 import jax.numpy as jnp
 from jax import lax
+from jax.experimental import pallas as pl
+from jax.experimental.pallas import tpu as pltpu
 from jax.sharding import PartitionSpec as P
+
+F32, BF16 = jnp.float32, jnp.bfloat16
+ANY = pl.BlockSpec(memory_space=pl.ANY)
+VMEM = pl.BlockSpec(memory_space=pltpu.VMEM)
+SMEM = pl.BlockSpec(memory_space=pltpu.SMEM)
 
 
 def swap(values, axis, size, flip):
@@ -143,8 +152,276 @@
     return (output, grad_one, grad_two)
 
 
+ROWS, COLS, CELLS, WIDE, TALL, TILE = 32, 32, 1024, 128, 256, 256
+
+
+def kernel_call(kernel, out_shape, in_specs, scratch, flops):
+    return pl.pallas_call(
+        kernel,
+        out_shape=out_shape,
+        in_specs=in_specs,
+        out_specs=[VMEM] * len(out_shape),
+        scratch_shapes=scratch,
+        compiler_params=pltpu.CompilerParams(vmem_limit_bytes=56 * 2**20),
+        cost_estimate=pl.CostEstimate(flops=flops, bytes_accessed=8 * 2**20, transcendentals=0),
+    )
+
+
+def column(rows):
+    return lax.broadcasted_iota(jnp.int32, (rows, WIDE), 0) % COLS
+
+
+def from_left(values):
+    return jnp.where(column(values.shape[0]) == 0, 0.0, pltpu.roll(values, 1, 0))
+
+
+def from_right(values):
+    return jnp.where(column(values.shape[0]) == COLS - 1, 0.0, pltpu.roll(values, values.shape[0] - 1, 0))
+
+
+def start_all(pairs, sems):
+    copies = [pltpu.make_async_copy(src, dst, sems.at[n]) for n, (src, dst) in enumerate(pairs)]
+    for copy in copies:
+        copy.start()
+    return copies
+
+
+def block(index, size):
+    return pl.ds(pl.multiple_of(index * size, size), size)
+
+
+def weight_pairs(own, refs, whole):
+    near, along_x, along_y, low, high = refs
+    pairs = [(ref, whole.at[:, :, block(own ^ k, TALL), :]) for k, ref in enumerate((near, along_x, along_y))]
+    half = TALL // 2
+    far = (own ^ 3) * 2
+    return pairs + [(low, whole.at[:, :, block(far, half), :]), (high, whole.at[:, :, block(far + 1, half), :])]
+
+
+def field_pairs(own, refs, whole):
+    pieces = [*refs[:4], *(refs[4].at[n] for n in range(3)), refs[5]]
+    flips = (0, 2, 4, 6, 1, 3, 5, 7)
+    return [(ref, whole.at[pl.ds(COLS, CELLS), block(own ^ k, WIDE)]) for k, ref in zip(flips, pieces)]
+
+
+def conv_kernel(first, place, *refs):
+    fields, weights = refs[:6], refs[6:11]
+    outs, (held, taps, sems) = refs[11:-3], refs[-3:]
+    copies = start_all(field_pairs(place[0], fields, held) + weight_pairs(place[1], weights, taps), sems)
+    edge = jnp.zeros((COLS, held.shape[1]), BF16)
+    held[:COLS, :] = edge
+    held[COLS + CELLS :, :] = edge
+    for copy in copies:
+        copy.wait()
+    for start in range(0, CELLS, TILE):
+        sums = jnp.zeros((TILE, 3 * WIDE), F32)
+        for row_tap in range(3):
+            across = jnp.concatenate([taps[row_tap, col_tap] for col_tap in range(3)], axis=1)
+            begin = start + row_tap * COLS
+            sums = sums + jnp.dot(held[begin : begin + TILE, :], across, preferred_element_type=F32)
+        total = sums[:, WIDE : 2 * WIDE] + from_left(sums[:, :WIDE]) + from_right(sums[:, 2 * WIDE :])
+        if first:
+            outs[0][start : start + TILE, :] = total
+            outs[1][start : start + TILE, :] = (total / (1.0 + jnp.exp(-total))).astype(BF16)
+        else:
+            outs[0][start : start + TILE, :] = total.astype(BF16)
+
+
+def conv(place, fields, weights, first):
+    channels = 8 * WIDE
+    out = [jax.ShapeDtypeStruct((CELLS, WIDE), F32)] if first else []
+    return kernel_call(
+        functools.partial(conv_kernel, first),
+        out + [jax.ShapeDtypeStruct((CELLS, WIDE), BF16)],
+        [SMEM] + [ANY] * 11,
+        [
+            pltpu.VMEM((CELLS + 2 * COLS, channels), BF16),
+            pltpu.VMEM((3, 3, channels, WIDE), BF16),
+            pltpu.SemaphoreType.DMA((13,)),
+        ],
+        2 * 9 * CELLS * channels * WIDE,
+    )(place, *fields, *weights)
+
+
+def spread(values, shifted):
+    edge = jnp.zeros((COLS, 3 * WIDE), BF16)
+    shifted[:COLS, :] = edge
+    shifted[COLS + CELLS :, :] = edge
+    wide = values.astype(F32)
+    inside = slice(COLS, COLS + CELLS)
+    shifted[inside, :WIDE] = from_right(wide).astype(BF16)
+    shifted[inside, WIDE : 2 * WIDE] = values
+    shifted[inside, 2 * WIDE :] = from_left(wide).astype(BF16)
+
+
+def back_kernel(place, grads, *refs):
+    weights, (keep, send, shifted, taps, sems) = refs[:5], refs[5:]
+    copies = start_all(weight_pairs(place[1], weights, taps), sems)
+    spread(grads[...], shifted)
+    for copy in copies:
+        copy.wait()
+    odd = (place[0] & 1) == 1
+    for pair in range(4):
+        rows = slice(pair * 2 * WIDE, (pair + 1) * 2 * WIDE)
+        across = jnp.concatenate([taps[p, q, rows, :] for p in range(3) for q in range(3)], axis=1)
+        slot = (place[0] >> 1) ^ pair
+        for start in range(0, CELLS, TILE):
+            begins = [start + (2 - p) * COLS for p in range(3)]
+            stacked = jnp.concatenate([shifted[begin : begin + TILE, :] for begin in begins], axis=1)
+            sums = lax.dot_general(stacked, across, (((1,), (1,)), ((), ())), preferred_element_type=F32)
+            even_part, odd_part = sums[:, :WIDE], sums[:, WIDE:]
+            keep[slot, start : start + TILE, :] = jnp.where(odd, odd_part, even_part).astype(BF16)
+            send[slot, start : start + TILE, :] = jnp.where(odd, even_part, odd_part).astype(BF16)
+
+
+def partial_backs(place, grads, weights):
+    return kernel_call(
+        back_kernel,
+        [jax.ShapeDtypeStruct((4, CELLS, WIDE), BF16)] * 2,
+        [SMEM, VMEM] + [ANY] * 5,
+        [
+            pltpu.VMEM((CELLS + 2 * COLS, 3 * WIDE), BF16),
+            pltpu.VMEM((3, 3, 8 * WIDE, WIDE), BF16),
+            pltpu.SemaphoreType.DMA((5,)),
+        ],
+        2 * 9 * CELLS * 8 * WIDE * WIDE,
+    )(place, grads, *weights)
+
+
+def grad_kernel(place, *refs):
+    mine, other, grads, (out, held, cots, shifted, sems) = refs[:4], refs[4], refs[5:9], refs[9:]
+    mine = [ref if len(ref.shape) == 2 else ref.at[1] for ref in mine]
+    grads = [ref if len(ref.shape) == 2 else ref.at[0] for ref in grads]
+    core = place[0] & 1
+    pairs = []
+    for k in range(4):
+        pairs.append((mine[k], held.at[k, :, block(core, WIDE)]))
+        pairs.append((other.at[k], held.at[k, :, block(1 - core, WIDE)]))
+        pairs.append((grads[k], cots.at[k]))
+    copies = start_all(pairs, sems)
+    for k in range(4):
+        for copy in copies[3 * k : 3 * k + 3]:
+            copy.wait()
+        spread(cots[k], shifted)
+        for p in range(3):
+            begin = (2 - p) * COLS
+            sums = lax.dot_general(
+                held[k], shifted[begin : begin + CELLS, :], (((0,), (0,)), ((), ())), preferred_element_type=F32
+            )
+            for q in range(3):
+                part = sums[:, q * WIDE : (q + 1) * WIDE]
+                out[p, q] = part if k == 0 else out[p, q] + part
+
+
+def weight_grads(place, mine, other, grads):
+    return kernel_call(
+        grad_kernel,
+        [jax.ShapeDtypeStruct((3, 3, TALL, WIDE), F32)],
+        [SMEM] + [ANY] * 9,
+        [
+            pltpu.VMEM((4, CELLS, TALL), BF16),
+            pltpu.VMEM((4, CELLS, WIDE), BF16),
+            pltpu.VMEM((CELLS + 2 * COLS, 3 * WIDE), BF16),
+            pltpu.SemaphoreType.DMA((12,)),
+        ],
+        2 * 9 * CELLS * 8 * WIDE * WIDE,
+    )(place, *mine, other, *grads)[0]
+
+
+def over_dp(values, flip):
+    return swap(values, "dp", 4, flip)
+
+
+def over_filter(values, flip):
+    return swap(values, "filter", 8, flip)
+
+
+def far_weights(along_x, along_y):
+    half = TALL // 2
+    return over_dp(along_x[:, :, :half], 2), over_dp(along_y[:, :, half:], 1)
+
+
+def at_owner(stacked, index):
+    return lax.dynamic_index_in_dim(stacked, index, 0, keepdims=False)
+
+
+def together(*values):
+    return lax.optimization_barrier(values)
+
+
+def quick_body(n_dp, n_filter, fields, weight_one, weight_two, cotangent):
+    own_filter, own_dp = lax.axis_index("filter"), lax.axis_index("dp")
+    place = jnp.stack([own_filter, own_dp]).astype(jnp.int32)
+    owner = own_dp ^ (own_filter >> 1)
+    fields, cotangent = fields.reshape(CELLS, WIDE), cotangent.reshape(CELLS, WIDE)
+
+    one_x, one_y = over_dp(weight_one, 1), over_dp(weight_one, 2)
+    field_far, field_near = over_filter(fields, 4), over_filter(fields, 2)
+    one_x, one_y, field_far, field_near = together(one_x, one_y, field_far, field_near)
+
+    one_low, one_high = far_weights(one_x, one_y)
+    field_last = over_filter(field_far, 2)
+    field_other = over_filter(jnp.stack([fields, field_near, field_far]), 1)
+    one_low, one_high, field_last, field_other, weight_two = together(
+        one_low, one_high, field_last, field_other, weight_two
+    )
+
+    two_x, two_y = over_dp(weight_two, 1), over_dp(weight_two, 2)
+    field_rest = over_filter(field_last, 1)
+    full_one = (weight_one, one_x, one_y, one_low, one_high)
+    pre_one, hidden = conv(place, (fields, field_near, field_far, field_last, field_other, field_rest), full_one, True)
+    two_x, two_y, hidden = together(two_x, two_y, hidden)
+
+    hidden_far, hidden_near = over_filter(hidden, 4), over_filter(hidden, 2)
+    two_low, two_high = far_weights(two_x, two_y)
+    hidden_far, hidden_near, two_low, two_high, cotangent, field_last = together(
+        hidden_far, hidden_near, two_low, two_high, cotangent, field_last
+    )
+
+    hidden_last = over_filter(hidden_far, 2)
+    hidden_other = over_filter(jnp.stack([hidden, hidden_near, hidden_far]), 1)
+    field_stack = jnp.stack([fields, field_near, field_far, field_last])
+    inputs = [jnp.stack([cotangent, at_owner(field_stack, owner ^ k)]) for k in range(4)]
+    inputs = [inputs[0]] + [over_dp(inputs[k], k) for k in (1, 2, 3)]
+    full_two = (weight_two, two_x, two_y, two_low, two_high)
+    keep, send = partial_backs(place, cotangent, full_two)
+    keep, send, hidden_last, hidden_other = together(keep, send, hidden_last, hidden_other)
+
+    got = over_filter(send, 1)
+    hidden_rest = over_filter(hidden_last, 1)
+    chip = lambda n: keep[n].astype(F32) + got[n].astype(F32)
+    chip_three, chip_one = chip(3).astype(BF16), chip(1).astype(BF16)
+    chip_three, chip_one, hidden_rest, hidden_last = together(chip_three, chip_one, hidden_rest, hidden_last)
+    relayed, nearby = over_filter(chip_three, 2), over_filter(chip_one, 2)
+    hidden_stack = jnp.stack([hidden, hidden_near, hidden_far, hidden_last])
+    hidden_mine = [at_owner(hidden_stack, owner ^ k) for k in range(4)]
+    hidden_mine = [hidden_mine[0]] + [over_dp(hidden_mine[k], k) for k in (1, 2, 3)]
+    hidden_parts = (hidden, hidden_near, hidden_far, hidden_last, hidden_other, hidden_rest)
+    output = conv(place, hidden_parts, full_two, False)[0]
+    relayed, nearby, output, *inputs = together(relayed, nearby, output, *inputs)
+
+    distant = over_filter((chip(2) + relayed.astype(F32)).astype(BF16), 4)
+    hidden_swapped = over_filter(jnp.stack(hidden_mine), 1)
+    grad_two = weight_grads(place, hidden_mine, hidden_swapped, inputs)
+    distant, grad_two = together(distant, grad_two)
+
+    back = chip(0) + nearby.astype(F32) + distant.astype(F32)
+    sigma = jax.nn.sigmoid(pre_one)
+    back_pre = (back * sigma * (1.0 + pre_one * (1.0 - sigma))).astype(BF16)
+    back_all = [back_pre] + [over_dp(back_pre, k) for k in (1, 2, 3)]
+    field_swapped = over_filter(jnp.stack([v[1] for v in inputs]), 1)
+    grad_one = weight_grads(place, inputs, field_swapped, back_all)
+    return (output.reshape(1, ROWS, COLS, WIDE), grad_one, grad_two)
+
+
 def solution(mesh):
     n_dp, n_filter = mesh.shape["dp"], mesh.shape["filter"]
+
+    def choose(arrays):
+        fields, weights = arrays[0].shape, arrays[1].shape
+        fits = (n_dp, n_filter) == (4, 8) and fields == (1, 32, 32, 128) and weights == (3, 3, 256, 128)
+        return quick_body if fits else body
+
     placed = (
         P("dp", None, None, "filter"),
         P(None, None, "dp", "filter"),
@@ -152,7 +429,7 @@
         P("dp", None, None, "filter"),
     )
     return jax.shard_map(
-        lambda *arrays: body(n_dp, n_filter, *arrays),
+        lambda *arrays: choose(arrays)(n_dp, n_filter, *arrays),
         mesh=mesh,
         in_specs=placed,
         out_specs=(

time: 176 us -> 155 us (0.88)
  Pallas kernels: 0 us -> 35.8 us
  local copies, waits for them, and re-layouts: 34.1 us -> 4.92 us
  matrix products: 21.3 us -> 0 us
  waiting for transfers between devices: 81.8 us -> 76.4 us
  other arithmetic: 7.77 us -> 4.18 us
  starting transfers between devices: 28.8 us -> 31.8 us
    pallas_call x0 -> x5, Pallas kernels: none -> 35.8 us  [the longest x2 14.7 us: conv(): kernel_call(functools.partial(conv_kernel, first), out + [jax.ShapeDtypeS...]
    dot_general x5 -> x0, matrix products: 21.3 us -> none  [the longest x2 9 us: filter_grads(): jnp.einsum('bhwc,bhwpqd->pqcd', inputs, stacked, preferred_element_type=j...]
    dynamic_update_slice x21 -> x0, local copies, waits for them, and re-layouts: 11.2 us -> none  [place(): lax.dynamic_update_slice_in_dim(whole, piece, (own ^ k) * width, dim)]
    unnamed x24 -> x80, local copies, waits for them, and re-layouts: 14.2 us -> 4.61 us
    ppermute x27 -> x33, waiting for transfers between devices: 81.8 us -> 76.4 us  [swap(): return lax.ppermute(values, axis, [(i, i ^ flip) for i in range(size)])]
    another operation x13 -> x0, local copies, waits for them, and re-layouts: 4.26 us -> none
    convert_element_type x6 -> x3, other arithmetic: 3.79 us -> 0.54 us  [the longest x1 0.3 us: quick_body(): back_pre = (back * sigma * (1.0 + pre_one * (1.0 - sigma))).astype(BF16)]
    ppermute x27 -> x33, starting transfers between devices: 28.8 us -> 31.8 us  [swap(): return lax.ppermute(values, axis, [(i, i ^ flip) for i in range(size)])]
  transfers between devices with their start and end apart: 27 -> 33, of which waited for: 14 -> 21; matrix products, arithmetic and copies ran while one was open for 29% -> 2% of each run, Pallas kernels for 0% -> 19%
where the time goes in v2:
time: 155 us; the launch traced here: 154 us
  waiting for transfers between devices  76.4 us (49%)
  Pallas kernels  35.8 us (23%)
  starting transfers between devices  31.8 us (21%)
  local copies, waits for them, and re-layouts  4.92 us (3%)
  other arithmetic  4.18 us (3%)
    ppermute x33, waiting for transfers between devices, swap(): return lax.ppermute(values, axis, [(i, i ^ flip) for i in range(size)])  76.4 us
    ppermute x33, starting transfers between devices, swap(): return lax.ppermute(values, axis, [(i, i ^ flip) for i in range(size)])  31.8 us
    pallas_call x2, Pallas kernels, conv(): kernel_call(functools.partial(conv_kernel, first), out + [jax.ShapeDtypeS...  14.7 us
    pallas_call x2, Pallas kernels, weight_grads(): kernel_call(grad_kernel, [jax.ShapeDtypeStruct((3, 3, TALL, WIDE), F32)],...  14.3 us
    pallas_call x1, Pallas kernels, partial_backs(): kernel_call(back_kernel, [jax.ShapeDtypeStruct((4, CELLS, WIDE), BF16)] *...  6.82 us
    unnamed x80, local copies, waits for them, and re-layouts  4.61 us
  transfers between devices with their start and end apart: 33, of which 21 were waited for; matrix products, arithmetic and copies ran while one was open for 2% of the time, Pallas kernels for 19%

profile of v2, /device:TPU:0, one launch (start us, length us, event | category | flops | bytes accessed | tf_op | source)
XLA Modules:
  0.0 154.4 jit_solution(11613756844511030710)
XLA Ops:
  0.6 3.0 %collective-permute-start = (bf16[3,3,256,128]{3,2,1,0:T(8,128)(2,1)}, bf16[3,3,256,128]{3,2,1,0:T(8,128)(2,1)S(1)}, u32[]{:S(2)}, u32[]{:S(2)}) collective-permute-start(bf16[3,3,256,128]{3,2,1,0:T(8,128)(2,1)} %refs_6_.1), channel_id=1, source_target_pairs={{0,8},{8,0},{16,24},{24,16},{1,9},{9,1},{17,25},{25,17},{2,10},{10... | collective-permute-start | bytes 1769480 | tf_op jit(solution)/shard_map/ppermute | solution.py:17
  3.6 1.5 collective-permute-start.1
  5.2 1.6 %collective-permute-start.3 = (bf16[1024,128]{1,0:T(8,128)(2,1)}, bf16[1024,128]{1,0:T(8,128)(2,1)S(1)}, u32[]{:S(2)}, u32[]{:S(2)}) collective-permute-start(bf16[1024,128]{1,0:T(8,128)(2,1)} %bitcast.43), channel_id=1, source_target_pairs={{0,2},{1,3},{2,0},{3,1},{4,6},{5,7},{6,4},{7,5},{8,10},{9,11},{10,... | collective-permute-start | bytes 786440 | tf_op jit(solution)/shard_map/ppermute | solution.py:17
  6.7 2.6 %collective-permute-start.2 = (bf16[1024,128]{1,0:T(8,128)(2,1)}, bf16[1024,128]{1,0:T(8,128)(2,1)S(1)}, u32[]{:S(2)}, u32[]{:S(2)}) collective-permute-start(bf16[1024,128]{1,0:T(8,128)(2,1)} %bitcast.44), channel_id=1, source_target_pairs={{0,4},{1,5},{2,6},{3,7},{4,0},{5,1},{6,2},{7,3},{8,12},{9,13},{10,... | collective-permute-start | bytes 786440 | tf_op jit(solution)/shard_map/ppermute | solution.py:17
  9.3 9.0 %collective-permute-done.3.refs_1_ = bf16[1024,128]{1,0:T(8,128)(2,1)S(1)} collective-permute-done((bf16[1024,128]{1,0:T(8,128)(2,1)}, bf16[1024,128]{1,0:T(8,128)(2,1)S(1)}, u32[]{:S(2)}, u32[]{:S(2)}) %collective-permute-start.3) | collective-permute-done | bytes 262176 | tf_op jit(solution)/shard_map/ppermute | solution.py:17
  18.3 2.4 %collective-permute-done.2.refs_2_ = bf16[1024,128]{1,0:T(8,128)(2,1)S(1)} collective-permute-done((bf16[1024,128]{1,0:T(8,128)(2,1)}, bf16[1024,128]{1,0:T(8,128)(2,1)S(1)}, u32[]{:S(2)}, u32[]{:S(2)}) %collective-permute-start.2) | collective-permute-done | bytes 262176 | tf_op jit(solution)/shard_map/ppermute | solution.py:17
  20.8 1.3 pad_maximum_fusion.4
  23.8 7.7 %collective-permute-done.6.refs_3_ = bf16[1024,128]{1,0:T(8,128)(2,1)S(1)} collective-permute-done((bf16[1024,128]{1,0:T(8,128)(2,1)S(1)}, bf16[1024,128]{1,0:T(8,128)(2,1)S(1)}, u32[]{:S(2)}, u32[]{:S(2)}) %collective-permute-start.6) | collective-permute-done | bytes 262176 | tf_op jit(solution)/shard_map/ppermute | solution.py:17
  32.0 0.7 copy-done.35
  32.7 1.2 collective-permute-start.9
  33.9 1.5 collective-permute-start.8
  35.3 0.6 pad_add_fusion.place
  36.0 1.1 collective-permute-done.10.refs_5_
  37.0 7.3 %shard_map.67 = (f32[1024,128]{1,0:T(8,128)}, bf16[1024,128]{1,0:T(8,128)(2,1)}) custom-call(s32[2]{0:T(128)} %pad_add_fusion.place, bf16[1024,128]{1,0:T(8,128)(2,1)} %bitcast.46, bf16[1024,128]{1,0:T(8,128)(2,1)} %copy-done.5, bf16[1024,128]{1,0:T(8,128)(2,1)} %copy-done.7, bf16[1024,128]{1,0:T(8,128)(2,1)} %copy-done.17, ...), custom_call_target="tpu_custom_call" | custom-call | flops 2415919104 | bytes 8388608 | tf_op jit(solution)/shard_map/pallas_call | solution.py:233
  44.4 3.1 %collective-permute-done.9.refs_2_.refs_8_ = bf16[3,3,256,128]{3,2,1,0:T(8,128)(2,1)S(1)} collective-permute-done((bf16[3,3,256,128]{3,2,1,0:T(8,128)(2,1)S(1)}, bf16[3,3,256,128]{3,2,1,0:T(8,128)(2,1)S(1)}, u32[]{:S(2)}, u32[]{:S(2)}) %collective-permute-start.9) | collective-permute-done | bytes 589856 | tf_op jit(solution)/shard_map/ppermute | solution.py:17
  47.9 1.6 %collective-permute-start.14 = (bf16[3,3,128,128]{3,2,1,0:T(8,128)(2,1)S(1)}, bf16[3,3,128,128]{3,2,1,0:T(8,128)(2,1)S(1)}, u32[]{:S(2)}, u32[]{:S(2)}) collective-permute-start(bf16[3,3,128,128]{3,2,1,0:T(8,128)(2,1)S(1)} %slice.51), channel_id=1, source_target_pairs={{0,8},{8,0},{16,24},{24,16},{1,9},{9,1},{17,25},{25,17},{2,10},{10... | collective-permute-start | bytes 884744 | tf_op jit(solution)/shard_map/ppermute | solution.py:17
  49.5 1.2 collective-permute-start.13
  51.2 2.6 %collective-permute-start.11 = (bf16[1024,128]{1,0:T(8,128)(2,1)S(1)}, bf16[1024,128]{1,0:T(8,128)(2,1)S(1)}, u32[]{:S(2)}, u32[]{:S(2)}) collective-permute-start(bf16[1024,128]{1,0:T(8,128)(2,1)S(1)} %copy-done.4), channel_id=1, source_target_pairs={{0,4},{1,5},{2,6},{3,7},{4,0},{5,1},{6,2},{7,3},{8,12},{9,13},{10,... | collective-permute-start | bytes 786440 | tf_op jit(solution)/shard_map/ppermute | solution.py:17
  53.7 8.0 %collective-permute-done.12.refs_1_ = bf16[1024,128]{1,0:T(8,128)(2,1)S(1)} collective-permute-done((bf16[1024,128]{1,0:T(8,128)(2,1)S(1)}, bf16[1024,128]{1,0:T(8,128)(2,1)S(1)}, u32[]{:S(2)}, u32[]{:S(2)}) %collective-permute-start.12) | collective-permute-done | bytes 262176 | tf_op jit(solution)/shard_map/ppermute | solution.py:17
  61.8 1.5 collective-permute-done.11.refs_2_
  64.2 6.8 %shard_map.68 = (bf16[4,1024,128]{2,1,0:T(8,128)(2,1)}, bf16[4,1024,128]{2,1,0:T(8,128)(2,1)}) custom-call(s32[2]{0:T(128)} %pad_add_fusion.place, bf16[1024,128]{1,0:T(8,128)(2,1)} %bitcast.58, bf16[3,3,256,128]{3,2,1,0:T(8,128)(2,1)} %refs_6_.2, bf16[3,3,256,128]{3,2,1,0:T(8,128)(2,1)} %copy-done.22, bf16[3,3,256,128]{3,2,1,0:T(8,128)(2,1)} %copy-done.21, ...), custom_call_target="tpu_custom_call" | custom-call | flops 2415919104 | bytes 8388608 | tf_op jit(solution)/shard_map/pallas_call | solution.py:278
  71.0 1.3 collective-permute-done.15.refs_3_
  72.3 0.7 copy-done.15
  73.8 1.1 pad_maximum_fusion
  74.9 1.2 collective-permute-done.17
  77.2 1.2 collective-permute-start.28
  78.4 1.2 collective-permute-start.27
  79.7 1.1 collective-permute-start.26
  81.0 1.3 collective-permute-start.23
  82.3 5.1 %collective-permute-done.28.refs_3_ = bf16[1024,128]{1,0:T(8,128)(2,1)S(1)} collective-permute-done((bf16[1024,128]{1,0:T(8,128)(2,1)S(1)}, bf16[1024,128]{1,0:T(8,128)(2,1)S(1)}, u32[]{:S(2)}, u32[]{:S(2)}) %collective-permute-start.28) | collective-permute-done | bytes 262176 | tf_op jit(solution)/shard_map/ppermute | solution.py:17
  87.3 5.5 %collective-permute-done.27.refs_2_ = bf16[1024,128]{1,0:T(8,128)(2,1)S(1)} collective-permute-done((bf16[1024,128]{1,0:T(8,128)(2,1)S(1)}, bf16[1024,128]{1,0:T(8,128)(2,1)S(1)}, u32[]{:S(2)}, u32[]{:S(2)}) %collective-permute-start.27) | collective-permute-done | bytes 262176 | tf_op jit(solution)/shard_map/ppermute | solution.py:17
  93.1 1.0 collective-permute-start.21
  94.1 0.8 collective-permute-start.22
  95.5 8.7 %collective-permute-done.23.refs_8_.refs_3_ = bf16[2,1024,128]{2,1,0:T(8,128)(2,1)S(1)} collective-permute-done((bf16[2,1024,128]{2,1,0:T(8,128)(2,1)S(1)}, bf16[2,1024,128]{2,1,0:T(8,128)(2,1)S(1)}, u32[]{:S(2)}, u32[]{:S(2)}) %collective-permute-start.23) | collective-permute-done | bytes 524320 | tf_op jit(solution)/shard_map/ppermute | solution.py:17
  104.5 7.3 %shard_map.69 = bf16[1024,128]{1,0:T(8,128)(2,1)} custom-call(s32[2]{0:T(128)} %pad_add_fusion.place, bf16[1024,128]{1,0:T(8,128)(2,1)} %get-tuple-element.52.refs_0_, bf16[1024,128]{1,0:T(8,128)(2,1)} %copy-done.9, bf16[1024,128]{1,0:T(8,128)(2,1)} %copy-done.10, bf16[1024,128]{1,0:T(8,128)(2,1)} %copy-done.15, bf16[3,1024,128]{2,1,0:T(8,128)(2,1)} %copy-done.29, ...), custom_call_target="tpu_custom_call" | custom-call | flops 2415919104 | bytes 8388608 | tf_op jit(solution)/shard_map/pallas_call | solution.py:233
  111.9 2.1 %collective-permute-done.21.refs_6_.refs_1_ = bf16[2,1024,128]{2,1,0:T(8,128)(2,1)S(1)} collective-permute-done((bf16[2,1024,128]{2,1,0:T(8,128)(2,1)S(1)}, bf16[2,1024,128]{2,1,0:T(8,128)(2,1)S(1)}, u32[]{:S(2)}, u32[]{:S(2)}) %collective-permute-start.21) | collective-permute-done | bytes 524320 | tf_op jit(solution)/shard_map/ppermute | solution.py:17
  114.0 0.6 collective-permute-done.22.refs_7_.refs_2_
  115.6 1.1 collective-permute-start.25
  116.7 7.2 %shard_map.70 = f32[3,3,256,128]{3,2,1,0:T(8,128)} custom-call(s32[2]{0:T(128)} %pad_add_fusion.place, bf16[1024,128]{1,0:T(8,128)(2,1)} %bitcast.42, bf16[1024,128]{1,0:T(8,128)(2,1)} %copy-done.20, bf16[1024,128]{1,0:T(8,128)(2,1)} %copy-done.19, bf16[1024,128]{1,0:T(8,128)(2,1)} %copy-done.18, bf16[4,1024,128]{2,1,0:T(8,128)(2,1)} %collective-permute-done.29.refs_4_, ...), custom_call_target="tpu_custom_call" | custom-call | flops 2415919104 | bytes 8388608 | tf_op jit(solution)/shard_map/pallas_call | solution.py:317
  123.9 6.6 %collective-permute-done.25 = bf16[1024,128]{1,0:T(8,128)(2,1)S(1)} collective-permute-done((bf16[1024,128]{1,0:T(8,128)(2,1)S(1)}, bf16[1024,128]{1,0:T(8,128)(2,1)S(1)}, u32[]{:S(2)}, u32[]{:S(2)}) %collective-permute-start.25) | collective-permute-done | bytes 262176 | tf_op jit(solution)/shard_map/ppermute | solution.py:17
  130.8 1.6 %collective-permute-start.32 = (bf16[1024,128]{1,0:T(8,128)(2,1)S(1)}, bf16[1024,128]{1,0:T(8,128)(2,1)S(1)}, u32[]{:S(2)}, u32[]{:S(2)}) collective-permute-start(bf16[1024,128]{1,0:T(8,128)(2,1)S(1)} %fusion.4.refs_5_), channel_id=1, source_target_pairs={{0,24},{8,16},{16,8},{24,0},{1,25},{9,17},{17,9},{25,1},{2,26},{10... | collective-permute-start | bytes 786440 | tf_op jit(solution)/shard_map/ppermute | solution.py:17
  132.4 0.9 collective-permute-start.31
  133.3 1.1 collective-permute-start.30
  134.4 6.6 %collective-permute-done.32.refs_8_ = bf16[1024,128]{1,0:T(8,128)(2,1)S(1)} collective-permute-done((bf16[1024,128]{1,0:T(8,128)(2,1)S(1)}, bf16[1024,128]{1,0:T(8,128)(2,1)S(1)}, u32[]{:S(2)}, u32[]{:S(2)}) %collective-permute-start.32) | collective-permute-done | bytes 262176 | tf_op jit(solution)/shard_map/ppermute | solution.py:17
  141.0 4.7 %collective-permute-done.31.refs_7_ = bf16[1024,128]{1,0:T(8,128)(2,1)S(1)} collective-permute-done((bf16[1024,128]{1,0:T(8,128)(2,1)S(1)}, bf16[1024,128]{1,0:T(8,128)(2,1)S(1)}, u32[]{:S(2)}, u32[]{:S(2)}) %collective-permute-start.31) | collective-permute-done | bytes 262176 | tf_op jit(solution)/shard_map/ppermute | solution.py:17
  145.7 0.7 copy-done.38
  146.4 0.7 copy-done.39
  147.1 7.1 %shard_map.71 = f32[3,3,256,128]{3,2,1,0:T(8,128)} custom-call(s32[2]{0:T(128)} %pad_add_fusion.place, bf16[2,1024,128]{2,1,0:T(8,128)(2,1)} %copy-done, bf16[2,1024,128]{2,1,0:T(8,128)(2,1)} %copy-done.26, bf16[2,1024,128]{2,1,0:T(8,128)(2,1)} %copy-done.27, bf16[2,1024,128]{2,1,0:T(8,128)(2,1)} %copy-done.25, bf16[4,1024,128]{2,1,0:T(8,128)(2,1)} %copy-done.28, ...), custom_call_target="tpu_custom_call" | custom-call | flops 2415919104 | bytes 8388608 | tf_op jit(solution)/shard_map/pallas_call | solution.py:317
  (124 shorter events, 8.2 us)
Async XLA Ops:
  0.6 20.1 %collective-permute-start = (bf16[3,3,256,128]{3,2,1,0:T(8,128)(2,1)}, bf16[3,3,256,128]{3,2,1,0:T(8,128)(2,1)S(1)}, u32[]{:S(2)}, u32[]{:S(2)}) collective-permute-start(bf16[3,3,256,128]{3,2,1,0:T(8,128)(2,1)} %refs_6_.1), channel_id=1, source_target_pairs={{0,8},{8,0},{16,24},{24,16},{1,9},{9,1},{17,25},{25,17},{2,10},{10... | collective-permute-start | bytes 1769480 | tf_op jit(solution)/shard_map/ppermute | solution.py:17
  3.6 17.1 %collective-permute-start.1 = (bf16[3,3,256,128]{3,2,1,0:T(8,128)(2,1)}, bf16[3,3,256,128]{3,2,1,0:T(8,128)(2,1)S(1)}, u32[]{:S(2)}, u32[]{:S(2)}) collective-permute-start(bf16[3,3,256,128]{3,2,1,0:T(8,128)(2,1)} %refs_6_.1), channel_id=1, source_target_pairs={{0,16},{8,24},{16,0},{24,8},{1,17},{9,25},{17,1},{25,9},{2,18},{10... | collective-permute-start | bytes 1769480 | tf_op jit(solution)/shard_map/ppermute | solution.py:17
  5.2 13.2 %collective-permute-start.3 = (bf16[1024,128]{1,0:T(8,128)(2,1)}, bf16[1024,128]{1,0:T(8,128)(2,1)S(1)}, u32[]{:S(2)}, u32[]{:S(2)}) collective-permute-start(bf16[1024,128]{1,0:T(8,128)(2,1)} %bitcast.43), channel_id=1, source_target_pairs={{0,2},{1,3},{2,0},{3,1},{4,6},{5,7},{6,4},{7,5},{8,10},{9,11},{10,... | collective-permute-start | bytes 786440 | tf_op jit(solution)/shard_map/ppermute | solution.py:17
  6.7 14.0 %collective-permute-start.2 = (bf16[1024,128]{1,0:T(8,128)(2,1)}, bf16[1024,128]{1,0:T(8,128)(2,1)S(1)}, u32[]{:S(2)}, u32[]{:S(2)}) collective-permute-start(bf16[1024,128]{1,0:T(8,128)(2,1)} %bitcast.44), channel_id=1, source_target_pairs={{0,4},{1,5},{2,6},{3,7},{4,0},{5,1},{6,2},{7,3},{8,12},{9,13},{10,... | collective-permute-start | bytes 786440 | tf_op jit(solution)/shard_map/ppermute | solution.py:17
  20.8 11.9 %copy-start.31 = (bf16[3,3,256,128]{3,2,1,0:T(8,128)(2,1)S(1)}, bf16[3,3,256,128]{3,2,1,0:T(8,128)(2,1)}, u32[]{:S(2)}) copy-start(bf16[3,3,256,128]{3,2,1,0:T(8,128)(2,1)} %refs_6_.2) | copy-start | bytes 1769476
  22.1 10.6 %collective-permute-start.7 = (bf16[3,1024,128]{2,1,0:T(8,128)(2,1)S(1)}, bf16[3,1024,128]{2,1,0:T(8,128)(2,1)S(1)}, u32[]{:S(2)}, u32[]{:S(2)}) collective-permute-start(bf16[3,1024,128]{2,1,0:T(8,128)(2,1)S(1)} %pad_maximum_fusion.4), channel_id=1, source_target_pairs={{0,1},{1,0},{2,3},{3,2},{4,5},{5,4},{6,7},{7,6},{8,9},{9,8},{10,11... | collective-permute-start | bytes 2359304 | tf_op jit(solution)/shard_map/ppermute | solution.py:17
  22.2 9.5 %collective-permute-start.5 = (bf16[3,3,128,128]{3,2,1,0:T(8,128)(2,1)S(1)}, bf16[3,3,128,128]{3,2,1,0:T(8,128)(2,1)S(1)}, u32[]{:S(2)}, u32[]{:S(2)}) collective-permute-start(bf16[3,3,128,128]{3,2,1,0:T(8,128)(2,1)S(1)} %slice.49), channel_id=1, source_target_pairs={{0,8},{8,0},{16,24},{24,16},{1,9},{9,1},{17,25},{25,17},{2,10},{10... | collective-permute-start | bytes 884744 | tf_op jit(solution)/shard_map/ppermute | solution.py:17
  22.8 9.1 %collective-permute-start.4 = (bf16[3,3,128,128]{3,2,1,0:T(8,128)(2,1)S(1)}, bf16[3,3,128,128]{3,2,1,0:T(8,128)(2,1)S(1)}, u32[]{:S(2)}, u32[]{:S(2)}) collective-permute-start(bf16[3,3,128,128]{3,2,1,0:T(8,128)(2,1)S(1)} %slice.48), channel_id=1, source_target_pairs={{0,16},{8,24},{16,0},{24,8},{1,17},{9,25},{17,1},{25,9},{2,18},{10... | collective-permute-start | bytes 884744 | tf_op jit(solution)/shard_map/ppermute | solution.py:17
  23.3 8.1 %collective-permute-start.6 = (bf16[1024,128]{1,0:T(8,128)(2,1)S(1)}, bf16[1024,128]{1,0:T(8,128)(2,1)S(1)}, u32[]{:S(2)}, u32[]{:S(2)}) collective-permute-start(bf16[1024,128]{1,0:T(8,128)(2,1)S(1)} %collective-permute-done.2.refs_2_), channel_id=1, source_target_pairs={{0,2},{1,3},{2,0},{3,1},{4,6},{5,7},{6,4},{7,5},{8,10},{9,11},{10,... | collective-permute-start | bytes 786440 | tf_op jit(solution)/shard_map/ppermute | solution.py:17
  32.7 14.8 %collective-permute-start.9 = (bf16[3,3,256,128]{3,2,1,0:T(8,128)(2,1)S(1)}, bf16[3,3,256,128]{3,2,1,0:T(8,128)(2,1)S(1)}, u32[]{:S(2)}, u32[]{:S(2)}) collective-permute-start(bf16[3,3,256,128]{3,2,1,0:T(8,128)(2,1)S(1)} %copy-done.31), channel_id=1, source_target_pairs={{0,16},{8,24},{16,0},{24,8},{1,17},{9,25},{17,1},{25,9},{2,18},{10... | collective-permute-start | bytes 1769480 | tf_op jit(solution)/shard_map/ppermute | solution.py:17
  33.9 14.0 %collective-permute-start.8 = (bf16[3,3,256,128]{3,2,1,0:T(8,128)(2,1)S(1)}, bf16[3,3,256,128]{3,2,1,0:T(8,128)(2,1)S(1)}, u32[]{:S(2)}, u32[]{:S(2)}) collective-permute-start(bf16[3,3,256,128]{3,2,1,0:T(8,128)(2,1)S(1)} %copy-done.31), channel_id=1, source_target_pairs={{0,8},{8,0},{16,24},{24,16},{1,9},{9,1},{17,25},{25,17},{2,10},{10... | collective-permute-start | bytes 1769480 | tf_op jit(solution)/shard_map/ppermute | solution.py:17
  35.3 1.7 %collective-permute-start.10 = (bf16[1024,128]{1,0:T(8,128)(2,1)S(1)}, bf16[1024,128]{1,0:T(8,128)(2,1)}, u32[]{:S(2)}, u32[]{:S(2)}) collective-permute-start(bf16[1024,128]{1,0:T(8,128)(2,1)S(1)} %collective-permute-done.6.refs_3_), channel_id=1, source_target_pairs={{0,1},{1,0},{2,3},{3,2},{4,5},{5,4},{6,7},{7,6},{8,9},{9,8},{10,11... | collective-permute-start | bytes 786440 | tf_op jit(solution)/shard_map/ppermute | solution.py:17
  47.5 16.0 %copy-start.21 = (bf16[3,3,256,128]{3,2,1,0:T(8,128)(2,1)}, bf16[3,3,256,128]{3,2,1,0:T(8,128)(2,1)S(1)}, u32[]{:S(2)}) copy-start(bf16[3,3,256,128]{3,2,1,0:T(8,128)(2,1)S(1)} %collective-permute-done.9.refs_2_.refs_8_) | copy-start | bytes 1769476
  47.9 15.4 %collective-permute-start.14 = (bf16[3,3,128,128]{3,2,1,0:T(8,128)(2,1)S(1)}, bf16[3,3,128,128]{3,2,1,0:T(8,128)(2,1)S(1)}, u32[]{:S(2)}, u32[]{:S(2)}) collective-permute-start(bf16[3,3,128,128]{3,2,1,0:T(8,128)(2,1)S(1)} %slice.51), channel_id=1, source_target_pairs={{0,8},{8,0},{16,24},{24,16},{1,9},{9,1},{17,25},{25,17},{2,10},{10... | collective-permute-start | bytes 884744 | tf_op jit(solution)/shard_map/ppermute | solution.py:17
  49.5 13.8 %collective-permute-start.13 = (bf16[3,3,128,128]{3,2,1,0:T(8,128)(2,1)S(1)}, bf16[3,3,128,128]{3,2,1,0:T(8,128)(2,1)S(1)}, u32[]{:S(2)}, u32[]{:S(2)}) collective-permute-start(bf16[3,3,128,128]{3,2,1,0:T(8,128)(2,1)S(1)} %slice.50), channel_id=1, source_target_pairs={{0,16},{8,24},{16,0},{24,8},{1,17},{9,25},{17,1},{25,9},{2,18},{10... | collective-permute-start | bytes 884744 | tf_op jit(solution)/shard_map/ppermute | solution.py:17
  50.7 11.0 %collective-permute-start.12 = (bf16[1024,128]{1,0:T(8,128)(2,1)S(1)}, bf16[1024,128]{1,0:T(8,128)(2,1)S(1)}, u32[]{:S(2)}, u32[]{:S(2)}) collective-permute-start(bf16[1024,128]{1,0:T(8,128)(2,1)S(1)} %copy-done.4), channel_id=1, source_target_pairs={{0,2},{1,3},{2,0},{3,1},{4,6},{5,7},{6,4},{7,5},{8,10},{9,11},{10,... | collective-permute-start | bytes 786440 | tf_op jit(solution)/shard_map/ppermute | solution.py:17
  51.2 12.2 %collective-permute-start.11 = (bf16[1024,128]{1,0:T(8,128)(2,1)S(1)}, bf16[1024,128]{1,0:T(8,128)(2,1)S(1)}, u32[]{:S(2)}, u32[]{:S(2)}) collective-permute-start(bf16[1024,128]{1,0:T(8,128)(2,1)S(1)} %copy-done.4), channel_id=1, source_target_pairs={{0,4},{1,5},{2,6},{3,7},{4,0},{5,1},{6,2},{7,3},{8,12},{9,13},{10,... | collective-permute-start | bytes 786440 | tf_op jit(solution)/shard_map/ppermute | solution.py:17
  61.8 14.8 %copy-start.9 = (bf16[1024,128]{1,0:T(8,128)(2,1)}, bf16[1024,128]{1,0:T(8,128)(2,1)S(1)}, u32[]{:S(2)}) copy-start(bf16[1024,128]{1,0:T(8,128)(2,1)S(1)} %collective-permute-done.12.refs_1_) | copy-start | bytes 786436
  63.4 10.3 %copy-start.3 = (bf16[1,32,32,128]{3,2,1,0:T(8,128)(2,1)S(1)}, bf16[1,32,32,128]{3,2,1,0:T(8,128)(2,1)}, u32[]{:S(2)}) copy-start(bf16[1,32,32,128]{3,2,1,0:T(8,128)(2,1)} %param.4) | copy-start | bytes 786436
  63.5 10.3 %copy-start.6 = (bf16[1024,128]{1,0:T(8,128)(2,1)S(1)}, bf16[1024,128]{1,0:T(8,128)(2,1)}, u32[]{:S(2)}) copy-start(bf16[1024,128]{1,0:T(8,128)(2,1)} %copy-done.5) | copy-start | bytes 786436
  63.5 10.3 %copy-start.8 = (bf16[1024,128]{1,0:T(8,128)(2,1)S(1)}, bf16[1024,128]{1,0:T(8,128)(2,1)}, u32[]{:S(2)}) copy-start(bf16[1024,128]{1,0:T(8,128)(2,1)} %copy-done.7) | copy-start | bytes 786436
  63.5 8.8 %collective-permute-start.16 = (bf16[3,1024,128]{2,1,0:T(8,128)(2,1)S(1)}, bf16[3,1024,128]{2,1,0:T(8,128)(2,1)S(1)}, u32[]{:S(2)}, u32[]{:S(2)}) collective-permute-start(bf16[3,1024,128]{2,1,0:T(8,128)(2,1)S(1)} %pad_maximum_fusion.5), channel_id=1, source_target_pairs={{0,1},{1,0},{2,3},{3,2},{4,5},{5,4},{6,7},{7,6},{8,9},{9,8},{10,11... | collective-permute-start | bytes 2359304 | tf_op jit(solution)/shard_map/ppermute | solution.py:17
  63.6 8.7 %collective-permute-start.15 = (bf16[1024,128]{1,0:T(8,128)(2,1)S(1)}, bf16[1024,128]{1,0:T(8,128)(2,1)S(1)}, u32[]{:S(2)}, u32[]{:S(2)}) collective-permute-start(bf16[1024,128]{1,0:T(8,128)(2,1)S(1)} %collective-permute-done.11.refs_2_), channel_id=1, source_target_pairs={{0,2},{1,3},{2,0},{3,1},{4,6},{5,7},{6,4},{7,5},{8,10},{9,11},{10,... | collective-permute-start | bytes 786440 | tf_op jit(solution)/shard_map/ppermute | solution.py:17
  73.3 2.9 %collective-permute-start.17 = (bf16[4,1024,128]{2,1,0:T(8,128)(2,1)}, bf16[4,1024,128]{2,1,0:T(8,128)(2,1)S(1)}, u32[]{:S(2)}, u32[]{:S(2)}) collective-permute-start(bf16[4,1024,128]{2,1,0:T(8,128)(2,1)} %get-tuple-element.63), channel_id=1, source_target_pairs={{0,1},{1,0},{2,3},{3,2},{4,5},{5,4},{6,7},{7,6},{8,9},{9,8},{10,11... | collective-permute-start | bytes 3145736 | tf_op jit(solution)/shard_map/ppermute | solution.py:17
  73.3 3.2 %collective-permute-start.18 = (bf16[1024,128]{1,0:T(8,128)(2,1)}, bf16[1024,128]{1,0:T(8,128)(2,1)S(1)}, u32[]{:S(2)}, u32[]{:S(2)}) collective-permute-start(bf16[1024,128]{1,0:T(8,128)(2,1)} %copy-done.15), channel_id=1, source_target_pairs={{0,1},{1,0},{2,3},{3,2},{4,5},{5,4},{6,7},{7,6},{8,9},{9,8},{10,11... | collective-permute-start | bytes 786440 | tf_op jit(solution)/shard_map/ppermute | solution.py:17
  77.2 15.6 %copy-start.2 = (bf16[1,1024,128]{2,1,0:T(8,128)(2,1)}, bf16[1,1024,128]{2,1,0:T(8,128)(2,1)S(1)}, u32[]{:S(2)}) copy-start(bf16[1,1024,128]{2,1,0:T(8,128)(2,1)S(1)} %get-tuple-element.86) | copy-start | bytes 786436
  77.2 10.1 %collective-permute-start.28 = (bf16[1024,128]{1,0:T(8,128)(2,1)S(1)}, bf16[1024,128]{1,0:T(8,128)(2,1)S(1)}, u32[]{:S(2)}, u32[]{:S(2)}) collective-permute-start(bf16[1024,128]{1,0:T(8,128)(2,1)S(1)} %get-tuple-element.83), channel_id=1, source_target_pairs={{0,24},{8,16},{16,8},{24,0},{1,25},{9,17},{17,9},{25,1},{2,26},{10... | collective-permute-start | bytes 786440 | tf_op jit(solution)/shard_map/ppermute | solution.py:17
  78.4 14.4 %collective-permute-start.27 = (bf16[1024,128]{1,0:T(8,128)(2,1)S(1)}, bf16[1024,128]{1,0:T(8,128)(2,1)S(1)}, u32[]{:S(2)}, u32[]{:S(2)}) collective-permute-start(bf16[1024,128]{1,0:T(8,128)(2,1)S(1)} %get-tuple-element.84), channel_id=1, source_target_pairs={{0,16},{8,24},{16,0},{24,8},{1,17},{9,25},{17,1},{25,9},{2,18},{10... | collective-permute-start | bytes 786440 | tf_op jit(solution)/shard_map/ppermute | solution.py:17
  79.7 13.2 %collective-permute-start.26 = (bf16[1024,128]{1,0:T(8,128)(2,1)S(1)}, bf16[1024,128]{1,0:T(8,128)(2,1)S(1)}, u32[]{:S(2)}, u32[]{:S(2)}) collective-permute-start(bf16[1024,128]{1,0:T(8,128)(2,1)S(1)} %get-tuple-element.85), channel_id=1, source_target_pairs={{0,8},{8,0},{16,24},{24,16},{1,9},{9,1},{17,25},{25,17},{2,10},{10... | collective-permute-start | bytes 786440 | tf_op jit(solution)/shard_map/ppermute | solution.py:17
  81.0 33.7 %copy-start = (bf16[2,1024,128]{2,1,0:T(8,128)(2,1)}, bf16[2,1024,128]{2,1,0:T(8,128)(2,1)S(1)}, u32[]{:S(2)}) copy-start(bf16[2,1024,128]{2,1,0:T(8,128)(2,1)S(1)} %get-tuple-element.72.refs_5_.refs_0_) | copy-start | bytes 1572868
  81.0 23.2 %collective-permute-start.23 = (bf16[2,1024,128]{2,1,0:T(8,128)(2,1)S(1)}, bf16[2,1024,128]{2,1,0:T(8,128)(2,1)S(1)}, u32[]{:S(2)}, u32[]{:S(2)}) collective-permute-start(bf16[2,1024,128]{2,1,0:T(8,128)(2,1)S(1)} %get-tuple-element.91), channel_id=1, source_target_pairs={{0,24},{8,16},{16,8},{24,0},{1,25},{9,17},{17,9},{25,1},{2,26},{10... | collective-permute-start | bytes 1572872 | tf_op jit(solution)/shard_map/ppermute | solution.py:17
  87.3 24.5 %copy-start.18 = (bf16[1024,128]{1,0:T(8,128)(2,1)}, bf16[1024,128]{1,0:T(8,128)(2,1)S(1)}, u32[]{:S(2)}) copy-start(bf16[1024,128]{1,0:T(8,128)(2,1)S(1)} %collective-permute-done.28.refs_3_) | copy-start | bytes 786436
  92.9 19.0 %copy-start.19 = (bf16[1024,128]{1,0:T(8,128)(2,1)}, bf16[1024,128]{1,0:T(8,128)(2,1)S(1)}, u32[]{:S(2)}) copy-start(bf16[1024,128]{1,0:T(8,128)(2,1)S(1)} %collective-permute-done.27.refs_2_) | copy-start | bytes 786436
  92.9 19.0 %copy-start.20 = (bf16[1024,128]{1,0:T(8,128)(2,1)}, bf16[1024,128]{1,0:T(8,128)(2,1)S(1)}, u32[]{:S(2)}) copy-start(bf16[1024,128]{1,0:T(8,128)(2,1)S(1)} %collective-permute-done.26.refs_1_) | copy-start | bytes 786436
  93.0 23.7 %collective-permute-start.29 = (bf16[4,1024,128]{2,1,0:T(8,128)(2,1)S(1)}, bf16[4,1024,128]{2,1,0:T(8,128)(2,1)}, u32[]{:S(2)}, u32[]{:S(2)}) collective-permute-start(bf16[4,1024,128]{2,1,0:T(8,128)(2,1)S(1)} %pad_maximum_fusion.3), channel_id=1, source_target_pairs={{0,1},{1,0},{2,3},{3,2},{4,5},{5,4},{6,7},{7,6},{8,9},{9,8},{10,11... | collective-permute-start | bytes 3145736 | tf_op jit(solution)/shard_map/ppermute | solution.py:17
  93.1 20.9 %collective-permute-start.21 = (bf16[2,1024,128]{2,1,0:T(8,128)(2,1)S(1)}, bf16[2,1024,128]{2,1,0:T(8,128)(2,1)S(1)}, u32[]{:S(2)}, u32[]{:S(2)}) collective-permute-start(bf16[2,1024,128]{2,1,0:T(8,128)(2,1)S(1)} %get-tuple-element.92), channel_id=1, source_target_pairs={{0,8},{8,0},{16,24},{24,16},{1,9},{9,1},{17,25},{25,17},{2,10},{10... | collective-permute-start | bytes 1572872 | tf_op jit(solution)/shard_map/ppermute | solution.py:17
  94.1 20.5 %collective-permute-start.22 = (bf16[2,1024,128]{2,1,0:T(8,128)(2,1)S(1)}, bf16[2,1024,128]{2,1,0:T(8,128)(2,1)S(1)}, u32[]{:S(2)}, u32[]{:S(2)}) collective-permute-start(bf16[2,1024,128]{2,1,0:T(8,128)(2,1)S(1)} %get-tuple-element.93), channel_id=1, source_target_pairs={{0,16},{8,24},{16,0},{24,8},{1,17},{9,25},{17,1},{25,9},{2,18},{10... | collective-permute-start | bytes 1572872 | tf_op jit(solution)/shard_map/ppermute | solution.py:17
  94.9 19.7 %collective-permute-start.19 = (bf16[1024,128]{1,0:T(8,128)(2,1)S(1)}, bf16[1024,128]{1,0:T(8,128)(2,1)S(1)}, u32[]{:S(2)}, u32[]{:S(2)}) collective-permute-start(bf16[1024,128]{1,0:T(8,128)(2,1)S(1)} %get-tuple-element.65), channel_id=1, source_target_pairs={{0,2},{1,3},{2,0},{3,1},{4,6},{5,7},{6,4},{7,5},{8,10},{9,11},{10,... | collective-permute-start | bytes 786440 | tf_op jit(solution)/shard_map/ppermute | solution.py:17
  104.2 10.5 %copy-start.25 = (bf16[2,1024,128]{2,1,0:T(8,128)(2,1)}, bf16[2,1024,128]{2,1,0:T(8,128)(2,1)S(1)}, u32[]{:S(2)}) copy-start(bf16[2,1024,128]{2,1,0:T(8,128)(2,1)S(1)} %collective-permute-done.23.refs_8_.refs_3_) | copy-start | bytes 1572868
  104.2 10.4 %collective-permute-start.20 = (bf16[1024,128]{1,0:T(8,128)(2,1)S(1)}, bf16[1024,128]{1,0:T(8,128)(2,1)S(1)}, u32[]{:S(2)}, u32[]{:S(2)}) collective-permute-start(bf16[1024,128]{1,0:T(8,128)(2,1)S(1)} %get-tuple-element.66), channel_id=1, source_target_pairs={{0,2},{1,3},{2,0},{3,1},{4,6},{5,7},{6,4},{7,5},{8,10},{9,11},{10,... | collective-permute-start | bytes 786440 | tf_op jit(solution)/shard_map/ppermute | solution.py:17
  115.4 19.0 %collective-permute-start.24 = (bf16[4,1024,128]{2,1,0:T(8,128)(2,1)S(1)}, bf16[4,1024,128]{2,1,0:T(8,128)(2,1)S(1)}, u32[]{:S(2)}, u32[]{:S(2)}) collective-permute-start(bf16[4,1024,128]{2,1,0:T(8,128)(2,1)S(1)} %pad_maximum_fusion.1), channel_id=1, source_target_pairs={{0,1},{1,0},{2,3},{3,2},{4,5},{5,4},{6,7},{7,6},{8,9},{9,8},{10,11... | collective-permute-start | bytes 3145736 | tf_op jit(solution)/shard_map/ppermute | solution.py:17
  115.6 15.0 %collective-permute-start.25 = (bf16[1024,128]{1,0:T(8,128)(2,1)S(1)}, bf16[1024,128]{1,0:T(8,128)(2,1)S(1)}, u32[]{:S(2)}, u32[]{:S(2)}) collective-permute-start(bf16[1024,128]{1,0:T(8,128)(2,1)S(1)} %fusion), channel_id=1, source_target_pairs={{0,4},{1,5},{2,6},{3,7},{4,0},{5,1},{6,2},{7,3},{8,12},{9,13},{10,... | collective-permute-start | bytes 786440 | tf_op jit(solution)/shard_map/ppermute | solution.py:17
  116.7 13.8 %copy-start.12 = (f32[1024,128]{1,0:T(8,128)S(1)}, f32[1024,128]{1,0:T(8,128)}, u32[]{:S(2)}) copy-start(f32[1024,128]{1,0:T(8,128)} %get-tuple-element.79) | copy-start | bytes 1572868
  130.8 14.9 %copy-start.13 = (bf16[1024,128]{1,0:T(8,128)(2,1)}, bf16[1024,128]{1,0:T(8,128)(2,1)S(1)}, u32[]{:S(2)}) copy-start(bf16[1024,128]{1,0:T(8,128)(2,1)S(1)} %fusion.4.refs_5_) | copy-start | bytes 786436
  130.8 10.2 %collective-permute-start.32 = (bf16[1024,128]{1,0:T(8,128)(2,1)S(1)}, bf16[1024,128]{1,0:T(8,128)(2,1)S(1)}, u32[]{:S(2)}, u32[]{:S(2)}) collective-permute-start(bf16[1024,128]{1,0:T(8,128)(2,1)S(1)} %fusion.4.refs_5_), channel_id=1, source_target_pairs={{0,24},{8,16},{16,8},{24,0},{1,25},{9,17},{17,9},{25,1},{2,26},{10... | collective-permute-start | bytes 786440 | tf_op jit(solution)/shard_map/ppermute | solution.py:17
  132.4 13.3 %collective-permute-start.31 = (bf16[1024,128]{1,0:T(8,128)(2,1)S(1)}, bf16[1024,128]{1,0:T(8,128)(2,1)S(1)}, u32[]{:S(2)}, u32[]{:S(2)}) collective-permute-start(bf16[1024,128]{1,0:T(8,128)(2,1)S(1)} %fusion.4.refs_5_), channel_id=1, source_target_pairs={{0,16},{8,24},{16,0},{24,8},{1,17},{9,25},{17,1},{25,9},{2,18},{10... | collective-permute-start | bytes 786440 | tf_op jit(solution)/shard_map/ppermute | solution.py:17
  133.3 12.4 %collective-permute-start.30 = (bf16[1024,128]{1,0:T(8,128)(2,1)S(1)}, bf16[1024,128]{1,0:T(8,128)(2,1)S(1)}, u32[]{:S(2)}, u32[]{:S(2)}) collective-permute-start(bf16[1024,128]{1,0:T(8,128)(2,1)S(1)} %fusion.4.refs_5_), channel_id=1, source_target_pairs={{0,8},{8,0},{16,24},{24,16},{1,9},{9,1},{17,25},{25,17},{2,10},{10... | collective-permute-start | bytes 786440 | tf_op jit(solution)/shard_map/ppermute | solution.py:17
  134.4 11.3 %copy-start.28 = (bf16[4,1024,128]{2,1,0:T(8,128)(2,1)}, bf16[4,1024,128]{2,1,0:T(8,128)(2,1)S(1)}, u32[]{:S(2)}) copy-start(bf16[4,1024,128]{2,1,0:T(8,128)(2,1)S(1)} %collective-permute-done.24.refs_4_) | copy-start | bytes 3145732
  (25 other events, 66.6 us)

commit v3 on v1

--- a/solution.py
+++ b/solution.py
@@ -1,7 +1,16 @@
+import functools
+
 import jax
 import jax.numpy as jnp
 from jax import lax
+from jax.experimental import pallas as pl
+from jax.experimental.pallas import tpu as pltpu
 from jax.sharding import PartitionSpec as P
+
+F32, BF16 = jnp.float32, jnp.bfloat16
+ANY = pl.BlockSpec(memory_space=pl.ANY)
+VMEM = pl.BlockSpec(memory_space=pltpu.VMEM)
+SMEM = pl.BlockSpec(memory_space=pltpu.SMEM)
 
 
 def swap(values, axis, size, flip):
@@ -143,8 +152,362 @@
     return (output, grad_one, grad_two)
 
 
+ROWS, COLS, CELLS, WIDE, TALL, TILE = 32, 32, 1024, 128, 256, 256
+TAPS = range(3)
+
+
+def kernel_call(kernel, out_shape, in_specs, scratch, share, out_specs=None, aliases=None):
+    return pl.pallas_call(
+        kernel,
+        out_shape=out_shape,
+        in_specs=in_specs,
+        out_specs=out_specs or [VMEM] * len(out_shape),
+        scratch_shapes=scratch,
+        input_output_aliases=aliases or {},
+        compiler_params=pltpu.CompilerParams(vmem_limit_bytes=56 * 2**20),
+        cost_estimate=pl.CostEstimate(
+            flops=int(share * 2 * 9 * CELLS * CELLS * WIDE), bytes_accessed=int(share * 2**23), transcendentals=0
+        ),
+    )
+
+
+def bf16(*shape):
+    return jax.ShapeDtypeStruct(shape, BF16)
+
+
+def f32(*shape):
+    return jax.ShapeDtypeStruct(shape, F32)
+
+
+def column(rows):
+    return lax.broadcasted_iota(jnp.int32, (rows, WIDE), 0) % COLS
+
+
+def from_left(values):
+    return jnp.where(column(values.shape[0]) == 0, 0.0, pltpu.roll(values, 1, 0))
+
+
+def from_right(values):
+    return jnp.where(column(values.shape[0]) == COLS - 1, 0.0, pltpu.roll(values, values.shape[0] - 1, 0))
+
+
+def start_all(pairs, sems):
+    copies = [pltpu.make_async_copy(src, dst, sems.at[n]) for n, (src, dst) in enumerate(pairs)]
+    for copy in copies:
+        copy.start()
+    return copies
+
+
+def block(index, size):
+    return pl.ds(pl.multiple_of(index * size, size), size)
+
+
+def weight_pairs(refs, whole, far_only=False):
+    half = TALL // 2
+    if far_only:
+        spans = [(0, half), (half, half)]
+    else:
+        spans = [(0, TALL), (TALL, TALL), (2 * TALL, TALL), (3 * TALL, half), (3 * TALL + half, half)]
+    return [(ref, whole.at[:, :, pl.ds(*span), :]) for ref, span in zip(refs, spans)]
+
+
+def field_pairs(place, refs, whole):
+    pieces = [*refs[:4], *([refs[4].at[n] for n in range(4)] if len(refs) == 5 else refs[4:])]
+    pairs = []
+    for flip, ref in zip((0, 2, 4, 6, 1, 3, 5, 7), pieces):
+        channels = place[0] ^ flip
+        spot = (((channels >> 1) ^ place[1]) << 1) + (channels & 1)
+        pairs.append((ref, whole.at[pl.ds(COLS, CELLS), block(spot, WIDE)]))
+    return pairs
+
+
+def clear_edges(held):
+    edge = jnp.zeros((COLS, held.shape[1]), BF16)
+    held[:COLS, :] = edge
+    held[COLS + CELLS :, :] = edge
+
+
+def taps_sum(held, taps, depth, start):
+    sums = None
+    for p in TAPS:
+        across = jnp.concatenate([taps[p, q, :depth] for q in TAPS], axis=1)
+        begin = start + p * COLS
+        part = jnp.dot(held[begin : begin + TILE, :depth], across, preferred_element_type=F32)
+        sums = part if sums is None else sums + part
+    return sums[:, WIDE : 2 * WIDE] + from_left(sums[:, :WIDE]) + from_right(sums[:, 2 * WIDE :])
+
+
+def conv_kernel(layer, count, place, *refs):
+    outs = refs[-5:-3] if layer == 0 else refs[-4:-3]
+    fields, weights, (held, taps, sems) = refs[:count], refs[count : -3 - len(outs)], refs[-3:]
+    copies = start_all(field_pairs(place, fields, held) + weight_pairs(weights, taps), sems)
+    clear_edges(held)
+    for copy in copies:
+        copy.wait()
+    for start in range(0, CELLS, TILE):
+        rows = slice(start, start + TILE)
+        total = taps_sum(held, taps, 4 * TALL, start)
+        if layer == 0:
+            outs[0][rows, :] = total
+            outs[1][rows, :] = (total / (1.0 + jnp.exp(-total))).astype(BF16)
+        else:
+            outs[0][rows, :] = total.astype(BF16)
+
+
+def conv(layer, place, fields, weights):
+    return kernel_call(
+        functools.partial(conv_kernel, layer, len(fields)),
+        ([f32(CELLS, WIDE)] if layer == 0 else []) + [bf16(CELLS, WIDE)],
+        [SMEM] + [ANY] * (len(fields) + 5),
+        [
+            pltpu.VMEM((CELLS + 2 * COLS, 4 * TALL), BF16),
+            pltpu.VMEM((3, 3, 4 * TALL, WIDE), BF16),
+            pltpu.SemaphoreType.DMA((13,)),
+        ],
+        1,
+    )(place, *fields, *weights)
+
+
+def spread(values, shifted):
+    clear_edges(shifted)
+    wide = values.astype(F32)
+    inside = slice(COLS, COLS + CELLS)
+    shifted[inside, :WIDE] = from_right(wide).astype(BF16)
+    shifted[inside, WIDE : 2 * WIDE] = values
+    shifted[inside, 2 * WIDE :] = from_left(wide).astype(BF16)
+
+
+def back_tile(shifted, taps, first, start, odd):
+    across = jnp.concatenate([taps[p, q, first : first + TALL, :] for p in TAPS for q in TAPS], axis=1)
+    begins = [start + (2 - p) * COLS for p in TAPS]
+    stacked = jnp.concatenate([shifted[begin : begin + TILE, :] for begin in begins], axis=1)
+    sums = lax.dot_general(stacked, across, (((1,), (1,)), ((), ())), preferred_element_type=F32)
+    even_part, odd_part = sums[:, :WIDE], sums[:, WIDE:]
+    return jnp.where(odd, odd_part, even_part).astype(BF16), jnp.where(odd, even_part, odd_part).astype(BF16)
+
+
+def back_near_kernel(place, grads, own, along_x, along_y, keep, send, shifted, taps, sems):
+    copies = start_all(weight_pairs((own, along_x, along_y), taps), sems)
+    spread(grads[...], shifted)
+    for copy in copies:
+        copy.wait()
+    odd = (place[0] & 1) == 1
+    for k in range(3):
+        slot = (place[0] >> 1) ^ place[1] ^ k
+        for start in range(0, CELLS, TILE):
+            rows = slice(start, start + TILE)
+            keep[slot, rows, :], send[slot, rows, :] = back_tile(shifted, taps, k * TALL, start, odd)
+
+
+def back_near(place, grads, weights):
+    return kernel_call(
+        back_near_kernel,
+        [bf16(4, CELLS, WIDE)] * 2,
+        [SMEM, VMEM] + [ANY] * 3,
+        [
+            pltpu.VMEM((CELLS + 2 * COLS, 3 * WIDE), BF16),
+            pltpu.VMEM((3, 3, 3 * TALL, WIDE), BF16),
+            pltpu.SemaphoreType.DMA((3,)),
+        ],
+        0.75,
+    )(place, grads, *weights)
+
+
+def back_far_kernel(place, grads, low, high, keep_in, send_in, keep, send, parts, shifted, taps, sems):
+    copies = start_all(weight_pairs((low, high), taps, True), sems)
+    spread(grads[...], shifted)
+    for copy in copies:
+        copy.wait()
+    odd = (place[0] & 1) == 1
+    slot = (place[0] >> 1) ^ place[1] ^ 3
+    for start in range(0, CELLS, TILE):
+        rows = slice(start, start + TILE)
+        parts[0, rows, :], parts[1, rows, :] = back_tile(shifted, taps, 0, start, odd)
+    outward = [pltpu.make_async_copy(parts.at[n], ref.at[slot], sems.at[2 + n]) for n, ref in enumerate((keep, send))]
+    for copy in outward:
+        copy.start()
+    for copy in outward:
+        copy.wait()
+
+
+def back_far(place, grads, weights, keep, send):
+    return kernel_call(
+        back_far_kernel,
+        [bf16(4, CELLS, WIDE)] * 2,
+        [SMEM, VMEM] + [ANY] * 4,
+        [
+            pltpu.VMEM((2, CELLS, WIDE), BF16),
+            pltpu.VMEM((CELLS + 2 * COLS, 3 * WIDE), BF16),
+            pltpu.VMEM((3, 3, TALL, WIDE), BF16),
+            pltpu.SemaphoreType.DMA((4,)),
+        ],
+        0.25,
+        [ANY, ANY],
+        {4: 0, 5: 1},
+    )(place, grads, *weights, keep, send)
+
+
+def grad_kernel(slots, adds, place, *refs):
+    count = len(slots)
+    mine, other, grads = refs[:count], refs[count], refs[count + 1 : 2 * count + 1]
+    before = refs[2 * count + 1] if adds else None
+    out, held, cots, shifted, sems = refs[2 * count + 1 + adds :]
+    mine = [ref if len(ref.shape) == 2 else ref.at[1] for ref in mine]
+    grads = [ref if len(ref.shape) == 2 else ref.at[0] for ref in grads]
+    core = place[0] & 1
+    pairs = []
+    for n, slot in enumerate(slots):
+        pairs.append((mine[n], held.at[n, :, block(core, WIDE)]))
+        pairs.append((other.at[slot], held.at[n, :, block(1 - core, WIDE)]))
+        pairs.append((grads[n], cots.at[n]))
+    copies = start_all(pairs, sems)
+    for n in range(count):
+        for copy in copies[3 * n : 3 * n + 3]:
+            copy.wait()
+        spread(cots[n], shifted)
+        for p in TAPS:
+            begin = (2 - p) * COLS
+            sums = lax.dot_general(
+                held[n], shifted[begin : begin + CELLS, :], (((0,), (0,)), ((), ())), preferred_element_type=F32
+            )
+            for q in TAPS:
+                part = sums[:, q * WIDE : (q + 1) * WIDE]
+                earlier = before if n == 0 else out
+                out[p, q] = part if earlier is None else earlier[p, q] + part
+
+
+def weight_grads(place, mine, other, grads, before, slots):
+    count = len(slots)
+    adds = 0 if before is None else 1
+    return kernel_call(
+        functools.partial(grad_kernel, slots, adds),
+        [f32(3, 3, TALL, WIDE)],
+        [SMEM] + [ANY] * (2 * count + 1) + [VMEM] * adds,
+        [
+            pltpu.VMEM((count, CELLS, TALL), BF16),
+            pltpu.VMEM((count, CELLS, WIDE), BF16),
+            pltpu.VMEM((CELLS + 2 * COLS, 3 * WIDE), BF16),
+            pltpu.SemaphoreType.DMA((3 * count,)),
+        ],
+        count / 4,
+    )(place, *mine, other, *grads, *([] if before is None else [before]))[0]
+
+
+def over_dp(values, flip, name):
+    with jax.named_scope(name):
+        return swap(values, "dp", 4, flip)
+
+
+def over_filter(values, flip, name):
+    with jax.named_scope(name):
+        return swap(values, "filter", 8, flip)
+
+
+def together(*values):
+    return lax.optimization_barrier(values)
+
+
+def others(pieces, name):
+    return [pieces[0]] + [over_dp(pieces[k], k, name + str(k)) for k in (1, 2, 3)]
+
+
+def pick(pieces, index):
+    chosen = pieces[0]
+    for n in (1, 2, 3):
+        chosen = jnp.where(index == n, pieces[n], chosen)
+    return chosen
+
+
+def scoped(name, function, *arguments):
+    with jax.named_scope(name):
+        return function(*arguments)
+
+
+def quick_body(n_dp, n_filter, fields, weight_one, weight_two, cotangent):
+    own_filter, own_dp = lax.axis_index("filter"), lax.axis_index("dp")
+    place = jnp.stack([own_filter, own_dp]).astype(jnp.int32)
+    owner = own_dp ^ (own_filter >> 1)
+    fields, cotangent = fields.reshape(CELLS, WIDE), cotangent.reshape(CELLS, WIDE)
+
+    half = TALL // 2
+
+    def far_weights(along_x, along_y, name):
+        return over_dp(along_x[:, :, :half], 2, name + "_low"), over_dp(along_y[:, :, half:], 1, name + "_high")
+
+    one_x, one_y = over_dp(weight_one, 1, "one_x"), over_dp(weight_one, 2, "one_y")
+    field_near, field_far = over_filter(fields, 2, "field_near"), over_filter(fields, 4, "field_far")
+    field_core0 = over_filter(fields, 1, "field_core0")
+    field_near, field_far, one_x, one_y, field_core0, place = together(
+        field_near, field_far, one_x, one_y, field_core0, place)
+    one_low, one_high = far_weights(one_x, one_y, "one")
+    field_last = over_filter(field_far, 2, "field_last")
+    field_core1, field_core2 = over_filter(field_near, 1, "field_core1"), over_filter(field_far, 1, "field_core2")
+    field_last, field_core1, field_core2, one_low, one_high = together(
+        field_last, field_core1, field_core2, one_low, one_high)
+    field_core3 = over_filter(field_last, 1, "field_core3")
+    field_z = (fields, field_near, field_far, field_last)
+    field_core3, weight_gated = together(field_core3, weight_two)
+    two_x, two_y = over_dp(weight_gated, 1, "two_x"), over_dp(weight_gated, 2, "two_y")
+    pre_one, hidden = scoped(
+        "conv_one", conv, 0, place, (*field_z, field_core0, field_core1, field_core2, field_core3),
+        (weight_one, one_x, one_y, one_low, one_high)
+    )
+    hidden_far, hidden_near = over_filter(hidden, 4, "hidden_far"), over_filter(hidden, 2, "hidden_near")
+    two_x, two_y, gate, *field_z = together(two_x, two_y, hidden, *field_z)
+
+    two_low, two_high = far_weights(two_x, two_y, "two")
+    keep, send = scoped("back_near", back_near, place, cotangent, (weight_two, two_x, two_y))
+    inputs = [jnp.stack([cotangent, pick(field_z, owner ^ k)]) for k in range(4)]
+    two_low, two_high, keep, send, hidden_far, hidden_near, *inputs = together(
+        two_low, two_high, keep, send, hidden_far, hidden_near, *inputs
+    )
+
+    inputs = others(inputs, "input")
+    hidden_last = over_filter(hidden_far, 2, "hidden_last")
+    keep, send = scoped("back_far", back_far, place, cotangent, (two_low, two_high), keep, send)
+    got = over_filter(send, 1, "back_core")
+    chip = lambda n: keep[n].astype(F32) + got[n].astype(F32)
+    chip_one, chip_three = chip(1).astype(BF16), chip(3).astype(BF16)
+    relayed = over_filter(chip_three, 2, "relayed")
+    hidden_z = (hidden, hidden_near, hidden_far, hidden_last)
+    hidden_stack = jnp.stack(hidden_z)
+    hidden_picked = [pick(hidden_z, owner ^ k) for k in range(4)]
+    chip_two = (chip(2) + relayed.astype(F32)).astype(BF16)
+    hidden_core = over_filter(hidden_stack, 1, "hidden_core")
+    chip_one, chip_two, *hidden_picked = together(chip_one, chip_two, *hidden_picked)
+
+    distant, nearby = over_filter(chip_two, 4, "distant"), over_filter(chip_one, 2, "nearby")
+    full_two = (weight_two, two_x, two_y, two_low, two_high)
+    output = scoped("conv_two", conv, 1, place, (*hidden_z, hidden_core), full_two)[0]
+    hidden_mine = others(hidden_picked, "hidden_to")
+    distant, nearby, output, *rest = together(distant, nearby, output, *hidden_mine, *inputs)
+    hidden_mine, inputs = rest[:4], rest[4:]
+
+    field_swapped = over_filter(jnp.stack([v[1] for v in inputs]), 1, "field_swap")
+    back = chip(0) + nearby.astype(F32) + distant.astype(F32)
+    sigma = jax.nn.sigmoid(pre_one)
+    back_pre = (back * sigma * (1.0 + pre_one * (1.0 - sigma))).astype(BF16)
+    back_all = others([back_pre] * 4, "pre")
+    hidden_swapped = over_filter(jnp.stack(hidden_mine), 1, "hidden_swap")
+    grad_two = scoped(
+        "grad_two", weight_grads, place, hidden_mine, hidden_swapped, inputs, None, (0, 1, 2, 3)
+    )
+    grad_one = scoped("grad_one_own", weight_grads, place, inputs[:1], field_swapped, back_all[:1], None, (0,))
+    *back_rest, grad_two, grad_one, output = together(*back_all[1:], grad_two, grad_one, output)
+    grad_one = scoped(
+        "grad_one", weight_grads, place, inputs[1:], field_swapped, back_rest, grad_one, (1, 2, 3)
+    )
+    return (output.reshape(1, ROWS, COLS, WIDE), grad_one, grad_two)
+
+
 def solution(mesh):
     n_dp, n_filter = mesh.shape["dp"], mesh.shape["filter"]
+
+    def choose(arrays):
+        fields, weights = arrays[0].shape, arrays[1].shape
+        fits = (n_dp, n_filter) == (4, 8) and fields == (1, 32, 32, 128) and weights == (3, 3, 256, 128)
+        return quick_body if fits else body
+
     placed = (
         P("dp", None, None, "filter"),
         P(None, None, "dp", "filter"),
@@ -152,7 +515,7 @@
         P("dp", None, None, "filter"),
     )
     return jax.shard_map(
-        lambda *arrays: body(n_dp, n_filter, *arrays),
+        lambda *arrays: choose(arrays)(n_dp, n_filter, *arrays),
         mesh=mesh,
         in_specs=placed,
         out_specs=(

time: 176 us -> 137 us (0.78)
  Pallas kernels: 0 us -> 42.2 us
  waiting for transfers between devices: 81.8 us -> 50.3 us
  local copies, waits for them, and re-layouts: 34.1 us -> 8.27 us
  matrix products: 21.3 us -> 0 us
  other arithmetic: 7.77 us -> 1.96 us
  starting transfers between devices: 28.8 us -> 32.4 us
    pallas_call x0 -> x7, Pallas kernels: none -> 42.2 us  [the longest x3 17.6 us: weight_grads(): kernel_call(functools.partial(grad_kernel, slots, adds), [f32(3, 3, TALL,...]
    ppermute x27 -> x34, waiting for transfers between devices: 81.8 us -> 50.3 us  [swap(): return lax.ppermute(values, axis, [(i, i ^ flip) for i in range(size)])]
    dot_general x5 -> x0, matrix products: 21.3 us -> none  [the longest x2 9 us: filter_grads(): jnp.einsum('bhwc,bhwpqd->pqcd', inputs, stacked, preferred_element_type=j...]
    dynamic_update_slice x21 -> x0, local copies, waits for them, and re-layouts: 11.2 us -> none  [place(): lax.dynamic_update_slice_in_dim(whole, piece, (own ^ k) * width, dim)]
    unnamed x24 -> x82, local copies, waits for them, and re-layouts: 14.2 us -> 7.12 us
    another operation x13 -> x0, local copies, waits for them, and re-layouts: 4.26 us -> none
    ppermute x27 -> x34, starting transfers between devices: 28.8 us -> 32.4 us  [swap(): return lax.ppermute(values, axis, [(i, i ^ flip) for i in range(size)])]
    convert_element_type x6 -> x3, other arithmetic: 3.79 us -> 0.54 us  [the longest x1 0.3 us: quick_body(): back_pre = (back * sigma * (1.0 + pre_one * (1.0 - sigma))).astype(BF16)]
  transfers between devices with their start and end apart: 27 -> 34, of which waited for: 14 -> 12; matrix products, arithmetic and copies ran while one was open for 29% -> 1% of each run, Pallas kernels for 0% -> 23%
where the time goes in v3:
time: 137 us
  waiting for transfers between devices  50.3 us (37%)
  Pallas kernels  42.2 us (31%)
  starting transfers between devices  32.4 us (24%)
  local copies, waits for them, and re-layouts  8.27 us (6%)
  other arithmetic  1.96 us (1%)
  between operations  1.42 us (1%)
    ppermute x34, waiting for transfers between devices, swap(): return lax.ppermute(values, axis, [(i, i ^ flip) for i in range(size)])  50.3 us
    ppermute x34, starting transfers between devices, swap(): return lax.ppermute(values, axis, [(i, i ^ flip) for i in range(size)])  32.4 us
    pallas_call x3, Pallas kernels, weight_grads(): kernel_call(functools.partial(grad_kernel, slots, adds), [f32(3, 3, TALL,...  17.6 us
    pallas_call x2, Pallas kernels, conv(): kernel_call(functools.partial(conv_kernel, layer, len(fields)), ([f32(CEL...  14.7 us
    unnamed x82, local copies, waits for them, and re-layouts  7.12 us
    pallas_call x1, Pallas kernels, back_near(): kernel_call(back_near_kernel, [bf16(4, CELLS, WIDE)] * 2, [SMEM, VMEM] +...  6.15 us
    pallas_call x1, Pallas kernels, back_far(): kernel_call(back_far_kernel, [bf16(4, CELLS, WIDE)] * 2, [SMEM, VMEM] + [...  3.75 us
  transfers between devices with their start and end apart: 34, of which 12 were waited for; matrix products, arithmetic and copies ran while one was open for 1% of the time, Pallas kernels for 23%

profile of v3, /device:TPU:0, one launch (start us, length us, event | category | flops | bytes accessed | tf_op | source)
XLA Modules:
  0.0 136.7 jit_solution(17055344643159342315)
XLA Ops:
  0.6 3.0 %collective-permute-start.2 = (bf16[3,3,256,128]{3,2,1,0:T(8,128)(2,1)}, bf16[3,3,256,128]{3,2,1,0:T(8,128)(2,1)S(1)}, u32[]{:S(2)}, u32[]{:S(2)}) collective-permute-start(bf16[3,3,256,128]{3,2,1,0:T(8,128)(2,1)} %refs_8_.1), channel_id=1, source_target_pairs={{0,8},{8,0},{16,24},{24,16},{1,9},{9,1},{17,25},{25,17},{2,10},{10... | collective-permute-start | bytes 1769480 | tf_op jit(solution)/shard_map/one_x/ppermute | solution.py:17
  3.6 1.5 %collective-permute-start.3 = (bf16[3,3,256,128]{3,2,1,0:T(8,128)(2,1)}, bf16[3,3,256,128]{3,2,1,0:T(8,128)(2,1)S(1)}, u32[]{:S(2)}, u32[]{:S(2)}) collective-permute-start(bf16[3,3,256,128]{3,2,1,0:T(8,128)(2,1)} %refs_8_.1), channel_id=1, source_target_pairs={{0,16},{8,24},{16,0},{24,8},{1,17},{9,25},{17,1},{25,9},{2,18},{10... | collective-permute-start | bytes 1769480 | tf_op jit(solution)/shard_map/one_y/ppermute | solution.py:17
  5.2 1.6 %collective-permute-start = (bf16[1024,128]{1,0:T(8,128)(2,1)}, bf16[1024,128]{1,0:T(8,128)(2,1)S(1)}, u32[]{:S(2)}, u32[]{:S(2)}) collective-permute-start(bf16[1024,128]{1,0:T(8,128)(2,1)} %bitcast.48), channel_id=1, source_target_pairs={{0,2},{1,3},{2,0},{3,1},{4,6},{5,7},{6,4},{7,5},{8,10},{9,11},{10,... | collective-permute-start | bytes 786440 | tf_op jit(solution)/shard_map/field_near/ppermute | solution.py:17
  6.7 2.6 %collective-permute-start.1 = (bf16[1024,128]{1,0:T(8,128)(2,1)}, bf16[1024,128]{1,0:T(8,128)(2,1)S(1)}, u32[]{:S(2)}, u32[]{:S(2)}) collective-permute-start(bf16[1024,128]{1,0:T(8,128)(2,1)} %bitcast.49), channel_id=1, source_target_pairs={{0,4},{1,5},{2,6},{3,7},{4,0},{5,1},{6,2},{7,3},{8,12},{9,13},{10,... | collective-permute-start | bytes 786440 | tf_op jit(solution)/shard_map/field_far/ppermute | solution.py:17
  9.3 0.6 pad_add_fusion.place
  9.9 8.4 %collective-permute-done.refs_1_ = bf16[1024,128]{1,0:T(8,128)(2,1)S(1)} collective-permute-done((bf16[1024,128]{1,0:T(8,128)(2,1)}, bf16[1024,128]{1,0:T(8,128)(2,1)S(1)}, u32[]{:S(2)}, u32[]{:S(2)}) %collective-permute-start) | collective-permute-done | bytes 262176 | tf_op jit(solution)/shard_map/field_near/ppermute | solution.py:17
  18.3 2.4 %collective-permute-done.1.refs_2_ = bf16[1024,128]{1,0:T(8,128)(2,1)S(1)} collective-permute-done((bf16[1024,128]{1,0:T(8,128)(2,1)}, bf16[1024,128]{1,0:T(8,128)(2,1)S(1)}, u32[]{:S(2)}, u32[]{:S(2)}) %collective-permute-start.1) | collective-permute-done | bytes 262176 | tf_op jit(solution)/shard_map/field_far/ppermute | solution.py:17
  20.8 0.6 collective-permute-start.8
  21.5 0.5 collective-permute-start.9
  23.0 5.4 %collective-permute-done.5.refs_3_ = bf16[1024,128]{1,0:T(8,128)(2,1)S(1)} collective-permute-done((bf16[1024,128]{1,0:T(8,128)(2,1)S(1)}, bf16[1024,128]{1,0:T(8,128)(2,1)S(1)}, u32[]{:S(2)}, u32[]{:S(2)}) %collective-permute-start.5) | collective-permute-done | bytes 262176 | tf_op jit(solution)/shard_map/field_last/ppermute | solution.py:17
  28.5 0.6 copy-done.37
  29.1 1.0 collective-permute-done.10.refs_7_
  30.2 1.5 %collective-permute-start.11 = (bf16[3,3,256,128]{3,2,1,0:T(8,128)(2,1)}, bf16[3,3,256,128]{3,2,1,0:T(8,128)(2,1)S(1)}, u32[]{:S(2)}, u32[]{:S(2)}) collective-permute-start(bf16[3,3,256,128]{3,2,1,0:T(8,128)(2,1)} %refs_5_.1), channel_id=1, source_target_pairs={{0,8},{8,0},{16,24},{24,16},{1,9},{9,1},{17,25},{25,17},{2,10},{10... | collective-permute-start | bytes 1769480 | tf_op jit(solution)/shard_map/two_x/ppermute | solution.py:17
  31.7 1.5 %collective-permute-start.12 = (bf16[3,3,256,128]{3,2,1,0:T(8,128)(2,1)}, bf16[3,3,256,128]{3,2,1,0:T(8,128)(2,1)S(1)}, u32[]{:S(2)}, u32[]{:S(2)}) collective-permute-start(bf16[3,3,256,128]{3,2,1,0:T(8,128)(2,1)} %refs_5_.1), channel_id=1, source_target_pairs={{0,16},{8,24},{16,0},{24,8},{1,17},{9,25},{17,1},{25,9},{2,18},{10... | collective-permute-start | bytes 1769480 | tf_op jit(solution)/shard_map/two_y/ppermute | solution.py:17
  33.2 7.4 %conv_one.1 = (f32[1024,128]{1,0:T(8,128)}, bf16[1024,128]{1,0:T(8,128)(2,1)}) custom-call(s32[2]{0:T(128)} %pad_add_fusion.place, bf16[1024,128]{1,0:T(8,128)(2,1)} %bitcast.51, bf16[1024,128]{1,0:T(8,128)(2,1)} %copy-done.15, bf16[1024,128]{1,0:T(8,128)(2,1)} %copy-done.17, bf16[1024,128]{1,0:T(8,128)(2,1)} %copy-done.19, bf16[1024,128]{1,0:T(8,128)(2,1)} %copy-done.35, ...), custom_call_target="tpu_custom_call" | custom-call | flops 2415919104 | bytes 8388608 | tf_op jit(solution)/shard_map/conv_one/pallas_call | solution.py:258
  40.6 1.1 collective-permute-start.15
  41.7 2.0 %collective-permute-start.16 = (bf16[1024,128]{1,0:T(8,128)(2,1)}, bf16[1024,128]{1,0:T(8,128)(2,1)S(1)}, u32[]{:S(2)}, u32[]{:S(2)}) collective-permute-start(bf16[1024,128]{1,0:T(8,128)(2,1)} %get-tuple-element.74.refs_0_), channel_id=1, source_target_pairs={{0,2},{1,3},{2,0},{3,1},{4,6},{5,7},{6,4},{7,5},{8,10},{9,11},{10,... | collective-permute-start | bytes 786440 | tf_op jit(solution)/shard_map/hidden_near/ppermute | solution.py:17
  43.7 2.0 %collective-permute-done.11.along_x.refs_6_ = bf16[3,3,256,128]{3,2,1,0:T(8,128)(2,1)S(1)} collective-permute-done((bf16[3,3,256,128]{3,2,1,0:T(8,128)(2,1)}, bf16[3,3,256,128]{3,2,1,0:T(8,128)(2,1)S(1)}, u32[]{:S(2)}, u32[]{:S(2)}) %collective-permute-start.11) | collective-permute-done | bytes 589856 | tf_op jit(solution)/shard_map/two_x/ppermute | solution.py:17
  45.8 1.2 collective-permute-done.12.along_y.refs_7_
  47.0 1.6 %collective-permute-start.13 = (bf16[3,3,128,128]{3,2,1,0:T(8,128)(2,1)S(1)}, bf16[3,3,128,128]{3,2,1,0:T(8,128)(2,1)S(1)}, u32[]{:S(2)}, u32[]{:S(2)}) collective-permute-start(bf16[3,3,128,128]{3,2,1,0:T(8,128)(2,1)S(1)} %slice.50), channel_id=1, source_target_pairs={{0,16},{8,24},{16,0},{24,8},{1,17},{9,25},{17,1},{25,9},{2,18},{10... | collective-permute-start | bytes 884744 | tf_op jit(solution)/shard_map/two_low/ppermute | solution.py:17
  48.6 0.6 collective-permute-start.14
  49.7 6.1 %back_near.1 = (bf16[4,1024,128]{2,1,0:T(8,128)(2,1)}, bf16[4,1024,128]{2,1,0:T(8,128)(2,1)}) custom-call(s32[2]{0:T(128)} %pad_add_fusion.place, bf16[1024,128]{1,0:T(8,128)(2,1)} %bitcast.40, bf16[3,3,256,128]{3,2,1,0:T(8,128)(2,1)} %refs_5_.1, bf16[3,3,256,128]{3,2,1,0:T(8,128)(2,1)} %copy-done.24, bf16[3,3,256,128]{3,2,1,0:T(8,128)(2,1)} %copy-done.25), custom_call_target="tpu_custom_call" | custom-call | flops 1811939328 | bytes 6291456 | tf_op jit(solution)/shard_map/back_near/pallas_call | solution.py:303
  57.0 3.7 %back_far.1 = (bf16[4,1024,128]{2,1,0:T(8,128)(2,1)}, bf16[4,1024,128]{2,1,0:T(8,128)(2,1)}) custom-call(s32[2]{0:T(128)} %pad_add_fusion.place, bf16[1024,128]{1,0:T(8,128)(2,1)} %bitcast.41, bf16[3,3,128,128]{3,2,1,0:T(8,128)(2,1)} %copy-done.12, bf16[3,3,128,128]{3,2,1,0:T(8,128)(2,1)} %copy-done.13, ...), custom_call_target="tpu_custom_call", output_to_operand_aliasing={{0}: (4, {}), {1}: (5, {})} | custom-call | flops 603979776 | bytes 2097152 | tf_op jit(solution)/shard_map/back_far/pallas_call | solution.py:334
  61.4 8.2 %collective-permute-done.19.refs_3_ = bf16[1024,128]{1,0:T(8,128)(2,1)S(1)} collective-permute-done((bf16[1024,128]{1,0:T(8,128)(2,1)S(1)}, bf16[1024,128]{1,0:T(8,128)(2,1)S(1)}, u32[]{:S(2)}, u32[]{:S(2)}) %collective-permute-start.19) | collective-permute-done | bytes 262176 | tf_op jit(solution)/shard_map/hidden_last/ppermute | solution.py:17
  69.8 1.2 collective-permute-start.26
  71.5 1.9 %collective-permute-start.28 = (bf16[2,1024,128]{2,1,0:T(8,128)(2,1)S(1)}, bf16[2,1024,128]{2,1,0:T(8,128)(2,1)S(1)}, u32[]{:S(2)}, u32[]{:S(2)}) collective-permute-start(bf16[2,1024,128]{2,1,0:T(8,128)(2,1)S(1)} %get-tuple-element.100), channel_id=1, source_target_pairs={{0,24},{8,16},{16,8},{24,0},{1,25},{9,17},{17,9},{25,1},{2,26},{10... | collective-permute-start | bytes 1572872 | tf_op jit(solution)/shard_map/input3/ppermute | solution.py:17
  74.2 7.2 %collective-permute-done.18 = bf16[1024,128]{1,0:T(8,128)(2,1)S(1)} collective-permute-done((bf16[1024,128]{1,0:T(8,128)(2,1)S(1)}, bf16[1024,128]{1,0:T(8,128)(2,1)S(1)}, u32[]{:S(2)}, u32[]{:S(2)}) %collective-permute-start.18) | collective-permute-done | bytes 262176 | tf_op jit(solution)/shard_map/relayed/ppermute | solution.py:17
  81.5 1.3 collective-permute-start.20
  82.9 1.7 %collective-permute-done.26.refs_6_.refs_0_ = bf16[2,1024,128]{2,1,0:T(8,128)(2,1)S(1)} collective-permute-done((bf16[2,1024,128]{2,1,0:T(8,128)(2,1)S(1)}, bf16[2,1024,128]{2,1,0:T(8,128)(2,1)S(1)}, u32[]{:S(2)}, u32[]{:S(2)}) %collective-permute-start.26) | collective-permute-done | bytes 524320 | tf_op jit(solution)/shard_map/input1/ppermute | solution.py:17
  85.1 11.2 %collective-permute-done.27.refs_7_.refs_1_ = bf16[2,1024,128]{2,1,0:T(8,128)(2,1)S(1)} collective-permute-done((bf16[2,1024,128]{2,1,0:T(8,128)(2,1)S(1)}, bf16[2,1024,128]{2,1,0:T(8,128)(2,1)S(1)}, u32[]{:S(2)}, u32[]{:S(2)}) %collective-permute-start.27) | collective-permute-done | bytes 524320 | tf_op jit(solution)/shard_map/input2/ppermute | solution.py:17
  96.3 0.9 collective-permute-start.23
  97.2 0.8 copy-done.29
  98.0 1.0 copy-done.31
  98.9 1.8 %collective-permute-start.25 = (bf16[1024,128]{1,0:T(8,128)(2,1)S(1)}, bf16[1024,128]{1,0:T(8,128)(2,1)S(1)}, u32[]{:S(2)}, u32[]{:S(2)}) collective-permute-start(bf16[1024,128]{1,0:T(8,128)(2,1)S(1)} %get-tuple-element.96), channel_id=1, source_target_pairs={{0,24},{8,16},{16,8},{24,0},{1,25},{9,17},{17,9},{25,1},{2,26},{10... | collective-permute-start | bytes 786440 | tf_op jit(solution)/shard_map/hidden_to3/ppermute | solution.py:17
  100.7 7.3 %conv_two.1 = bf16[1024,128]{1,0:T(8,128)(2,1)} custom-call(s32[2]{0:T(128)} %pad_add_fusion.place, bf16[1024,128]{1,0:T(8,128)(2,1)} %get-tuple-element.74.refs_0_, bf16[1024,128]{1,0:T(8,128)(2,1)} %copy-done.7, bf16[1024,128]{1,0:T(8,128)(2,1)} %copy-done.6, bf16[1024,128]{1,0:T(8,128)(2,1)} %copy-done.9, bf16[4,1024,128]{2,1,0:T(8,128)(2,1)} %copy-done.31, ...), custom_call_target="tpu_custom_call" | custom-call | flops 2415919104 | bytes 8388608 | tf_op jit(solution)/shard_map/conv_two/pallas_call | solution.py:258
  108.1 1.0 collective-permute-done.24.refs_2_
  109.3 1.0 slice-done
  110.7 0.5 collective-permute-start.32
  111.8 1.7 %collective-permute-start.29 = (bf16[1024,128]{1,0:T(8,128)(2,1)S(1)}, bf16[1024,128]{1,0:T(8,128)(2,1)S(1)}, u32[]{:S(2)}, u32[]{:S(2)}) collective-permute-start(bf16[1024,128]{1,0:T(8,128)(2,1)S(1)} %fusion.4.refs_2_), channel_id=1, source_target_pairs={{0,8},{8,0},{16,24},{24,16},{1,9},{9,1},{17,25},{25,17},{2,10},{10... | collective-permute-start | bytes 786440 | tf_op jit(solution)/shard_map/pre1/ppermute | solution.py:17
  113.5 0.7 collective-permute-start.30
  114.2 1.2 collective-permute-start.31
  115.4 1.0 copy-done.2
  116.3 3.9 %grad_one_own.1.refs_7_ = f32[3,3,256,128]{3,2,1,0:T(8,128)} custom-call(s32[2]{0:T(128)} %pad_add_fusion.place, bf16[2,1024,128]{2,1,0:T(8,128)(2,1)} %copy-done.1, bf16[4,1024,128]{2,1,0:T(8,128)(2,1)} %copy-done.2, bf16[1024,128]{1,0:T(8,128)(2,1)} %copy-done.3), custom_call_target="tpu_custom_call" | custom-call | flops 603979776 | bytes 2097152 | tf_op jit(solution)/shard_map/grad_one_own/pallas_call | solution.py:382
  120.3 1.0 copy-done.32
  121.2 7.1 %grad_two.1 = f32[3,3,256,128]{3,2,1,0:T(8,128)} custom-call(s32[2]{0:T(128)} %pad_add_fusion.place, bf16[1024,128]{1,0:T(8,128)(2,1)} %copy-done.8, bf16[1024,128]{1,0:T(8,128)(2,1)} %copy-done.21, bf16[1024,128]{1,0:T(8,128)(2,1)} %copy-done.22, bf16[1024,128]{1,0:T(8,128)(2,1)} %copy-done.23, bf16[4,1024,128]{2,1,0:T(8,128)(2,1)} %copy-done.32, ...), custom_call_target="tpu_custom_call" | custom-call | flops 2415919104 | bytes 8388608 | tf_op jit(solution)/shard_map/grad_two/pallas_call | solution.py:382
  128.4 0.7 copy-done.38
  129.1 0.7 copy-done.40
  129.8 6.7 %grad_one.1 = f32[3,3,256,128]{3,2,1,0:T(8,128)} custom-call(s32[2]{0:T(128)} %pad_add_fusion.place, bf16[2,1024,128]{2,1,0:T(8,128)(2,1)} %copy-done.10, bf16[2,1024,128]{2,1,0:T(8,128)(2,1)} %copy-done.28, bf16[2,1024,128]{2,1,0:T(8,128)(2,1)} %copy-done.29, bf16[4,1024,128]{2,1,0:T(8,128)(2,1)} %copy-done.2, bf16[1024,128]{1,0:T(8,128)(2,1)} %copy-done.38, ...), custom_call_target="tpu_custom_call" | custom-call | flops 1811939328 | bytes 6291456 | tf_op jit(solution)/shard_map/grad_one/pallas_call | solution.py:382
  (128 shorter events, 6.5 us)
Async XLA Ops:
  0.6 20.1 %collective-permute-start.2 = (bf16[3,3,256,128]{3,2,1,0:T(8,128)(2,1)}, bf16[3,3,256,128]{3,2,1,0:T(8,128)(2,1)S(1)}, u32[]{:S(2)}, u32[]{:S(2)}) collective-permute-start(bf16[3,3,256,128]{3,2,1,0:T(8,128)(2,1)} %refs_8_.1), channel_id=1, source_target_pairs={{0,8},{8,0},{16,24},{24,16},{1,9},{9,1},{17,25},{25,17},{2,10},{10... | collective-permute-start | bytes 1769480 | tf_op jit(solution)/shard_map/one_x/ppermute | solution.py:17
  3.6 17.1 %collective-permute-start.3 = (bf16[3,3,256,128]{3,2,1,0:T(8,128)(2,1)}, bf16[3,3,256,128]{3,2,1,0:T(8,128)(2,1)S(1)}, u32[]{:S(2)}, u32[]{:S(2)}) collective-permute-start(bf16[3,3,256,128]{3,2,1,0:T(8,128)(2,1)} %refs_8_.1), channel_id=1, source_target_pairs={{0,16},{8,24},{16,0},{24,8},{1,17},{9,25},{17,1},{25,9},{2,18},{10... | collective-permute-start | bytes 1769480 | tf_op jit(solution)/shard_map/one_y/ppermute | solution.py:17
  5.2 13.2 %collective-permute-start = (bf16[1024,128]{1,0:T(8,128)(2,1)}, bf16[1024,128]{1,0:T(8,128)(2,1)S(1)}, u32[]{:S(2)}, u32[]{:S(2)}) collective-permute-start(bf16[1024,128]{1,0:T(8,128)(2,1)} %bitcast.48), channel_id=1, source_target_pairs={{0,2},{1,3},{2,0},{3,1},{4,6},{5,7},{6,4},{7,5},{8,10},{9,11},{10,... | collective-permute-start | bytes 786440 | tf_op jit(solution)/shard_map/field_near/ppermute | solution.py:17
  6.7 14.0 %collective-permute-start.1 = (bf16[1024,128]{1,0:T(8,128)(2,1)}, bf16[1024,128]{1,0:T(8,128)(2,1)S(1)}, u32[]{:S(2)}, u32[]{:S(2)}) collective-permute-start(bf16[1024,128]{1,0:T(8,128)(2,1)} %bitcast.49), channel_id=1, source_target_pairs={{0,4},{1,5},{2,6},{3,7},{4,0},{5,1},{6,2},{7,3},{8,12},{9,13},{10,... | collective-permute-start | bytes 786440 | tf_op jit(solution)/shard_map/field_far/ppermute | solution.py:17
  9.3 11.4 %collective-permute-start.4 = (bf16[1024,128]{1,0:T(8,128)(2,1)}, bf16[1024,128]{1,0:T(8,128)(2,1)S(1)}, u32[]{:S(2)}, u32[]{:S(2)}) collective-permute-start(bf16[1024,128]{1,0:T(8,128)(2,1)} %bitcast.50), channel_id=1, source_target_pairs={{0,1},{1,0},{2,3},{3,2},{4,5},{5,4},{6,7},{7,6},{8,9},{9,8},{10,11... | collective-permute-start | bytes 786440 | tf_op jit(solution)/shard_map/field_core0/ppermute | solution.py:17
  18.3 14.9 %copy-start.15 = (bf16[1024,128]{1,0:T(8,128)(2,1)}, bf16[1024,128]{1,0:T(8,128)(2,1)S(1)}, u32[]{:S(2)}) copy-start(bf16[1024,128]{1,0:T(8,128)(2,1)S(1)} %collective-permute-done.refs_1_) | copy-start | bytes 786436
  20.7 12.5 %copy-start.17 = (bf16[1024,128]{1,0:T(8,128)(2,1)}, bf16[1024,128]{1,0:T(8,128)(2,1)S(1)}, u32[]{:S(2)}) copy-start(bf16[1024,128]{1,0:T(8,128)(2,1)S(1)} %collective-permute-done.1.refs_2_) | copy-start | bytes 786436
  20.7 12.5 %copy-start.26 = (bf16[3,3,256,128]{3,2,1,0:T(8,128)(2,1)}, bf16[3,3,256,128]{3,2,1,0:T(8,128)(2,1)S(1)}, u32[]{:S(2)}) copy-start(bf16[3,3,256,128]{3,2,1,0:T(8,128)(2,1)S(1)} %collective-permute-done.2.refs_9_) | copy-start | bytes 1769476
  20.8 12.4 %copy-start.27 = (bf16[3,3,256,128]{3,2,1,0:T(8,128)(2,1)}, bf16[3,3,256,128]{3,2,1,0:T(8,128)(2,1)S(1)}, u32[]{:S(2)}) copy-start(bf16[3,3,256,128]{3,2,1,0:T(8,128)(2,1)S(1)} %collective-permute-done.3.refs_10_) | copy-start | bytes 1769476
  20.8 7.6 %collective-permute-start.8 = (bf16[3,3,128,128]{3,2,1,0:T(8,128)(2,1)S(1)}, bf16[3,3,128,128]{3,2,1,0:T(8,128)(2,1)S(1)}, u32[]{:S(2)}, u32[]{:S(2)}) collective-permute-start(bf16[3,3,128,128]{3,2,1,0:T(8,128)(2,1)S(1)} %slice.48), channel_id=1, source_target_pairs={{0,16},{8,24},{16,0},{24,8},{1,17},{9,25},{17,1},{25,9},{2,18},{10... | collective-permute-start | bytes 884744 | tf_op jit(solution)/shard_map/one_low/ppermute | solution.py:17
  21.5 7.0 %collective-permute-start.9 = (bf16[3,3,128,128]{3,2,1,0:T(8,128)(2,1)S(1)}, bf16[3,3,128,128]{3,2,1,0:T(8,128)(2,1)S(1)}, u32[]{:S(2)}, u32[]{:S(2)}) collective-permute-start(bf16[3,3,128,128]{3,2,1,0:T(8,128)(2,1)S(1)} %slice.49), channel_id=1, source_target_pairs={{0,8},{8,0},{16,24},{24,16},{1,9},{9,1},{17,25},{25,17},{2,10},{10... | collective-permute-start | bytes 884744 | tf_op jit(solution)/shard_map/one_high/ppermute | solution.py:17
  22.0 6.4 %collective-permute-start.5 = (bf16[1024,128]{1,0:T(8,128)(2,1)S(1)}, bf16[1024,128]{1,0:T(8,128)(2,1)S(1)}, u32[]{:S(2)}, u32[]{:S(2)}) collective-permute-start(bf16[1024,128]{1,0:T(8,128)(2,1)S(1)} %collective-permute-done.1.refs_2_), channel_id=1, source_target_pairs={{0,2},{1,3},{2,0},{3,1},{4,6},{5,7},{6,4},{7,5},{8,10},{9,11},{10,... | collective-permute-start | bytes 786440 | tf_op jit(solution)/shard_map/field_last/ppermute | solution.py:17
  22.5 5.9 %collective-permute-start.7 = (bf16[1024,128]{1,0:T(8,128)(2,1)S(1)}, bf16[1024,128]{1,0:T(8,128)(2,1)S(1)}, u32[]{:S(2)}, u32[]{:S(2)}) collective-permute-start(bf16[1024,128]{1,0:T(8,128)(2,1)S(1)} %collective-permute-done.1.refs_2_), channel_id=1, source_target_pairs={{0,1},{1,0},{2,3},{3,2},{4,5},{5,4},{6,7},{7,6},{8,9},{9,8},{10,11... | collective-permute-start | bytes 786440 | tf_op jit(solution)/shard_map/field_core2/ppermute | solution.py:17
  22.5 5.9 %collective-permute-start.6 = (bf16[1024,128]{1,0:T(8,128)(2,1)S(1)}, bf16[1024,128]{1,0:T(8,128)(2,1)S(1)}, u32[]{:S(2)}, u32[]{:S(2)}) collective-permute-start(bf16[1024,128]{1,0:T(8,128)(2,1)S(1)} %collective-permute-done.refs_1_), channel_id=1, source_target_pairs={{0,1},{1,0},{2,3},{3,2},{4,5},{5,4},{6,7},{7,6},{8,9},{9,8},{10,11... | collective-permute-start | bytes 786440 | tf_op jit(solution)/shard_map/field_core1/ppermute | solution.py:17
  28.4 1.7 %collective-permute-start.10 = (bf16[1024,128]{1,0:T(8,128)(2,1)S(1)}, bf16[1024,128]{1,0:T(8,128)(2,1)}, u32[]{:S(2)}, u32[]{:S(2)}) collective-permute-start(bf16[1024,128]{1,0:T(8,128)(2,1)S(1)} %collective-permute-done.5.refs_3_), channel_id=1, source_target_pairs={{0,1},{1,0},{2,3},{3,2},{4,5},{5,4},{6,7},{7,6},{8,9},{9,8},{10,11... | collective-permute-start | bytes 786440 | tf_op jit(solution)/shard_map/field_core3/ppermute | solution.py:17
  30.2 15.6 %collective-permute-start.11 = (bf16[3,3,256,128]{3,2,1,0:T(8,128)(2,1)}, bf16[3,3,256,128]{3,2,1,0:T(8,128)(2,1)S(1)}, u32[]{:S(2)}, u32[]{:S(2)}) collective-permute-start(bf16[3,3,256,128]{3,2,1,0:T(8,128)(2,1)} %refs_5_.1), channel_id=1, source_target_pairs={{0,8},{8,0},{16,24},{24,16},{1,9},{9,1},{17,25},{25,17},{2,10},{10... | collective-permute-start | bytes 1769480 | tf_op jit(solution)/shard_map/two_x/ppermute | solution.py:17
  31.7 15.3 %collective-permute-start.12 = (bf16[3,3,256,128]{3,2,1,0:T(8,128)(2,1)}, bf16[3,3,256,128]{3,2,1,0:T(8,128)(2,1)S(1)}, u32[]{:S(2)}, u32[]{:S(2)}) collective-permute-start(bf16[3,3,256,128]{3,2,1,0:T(8,128)(2,1)} %refs_5_.1), channel_id=1, source_target_pairs={{0,16},{8,24},{16,0},{24,8},{1,17},{9,25},{17,1},{25,9},{2,18},{10... | collective-permute-start | bytes 1769480 | tf_op jit(solution)/shard_map/two_y/ppermute | solution.py:17
  40.6 8.6 %copy-start.14 = (bf16[1,32,32,128]{3,2,1,0:T(8,128)(2,1)S(1)}, bf16[1,32,32,128]{3,2,1,0:T(8,128)(2,1)}, u32[]{:S(2)}) copy-start(bf16[1,32,32,128]{3,2,1,0:T(8,128)(2,1)} %param.4) | copy-start | bytes 786436
  40.6 8.6 %copy-start.16 = (bf16[1024,128]{1,0:T(8,128)(2,1)S(1)}, bf16[1024,128]{1,0:T(8,128)(2,1)}, u32[]{:S(2)}) copy-start(bf16[1024,128]{1,0:T(8,128)(2,1)} %copy-done.15) | copy-start | bytes 786436
  40.6 15.3 %collective-permute-start.15 = (bf16[1024,128]{1,0:T(8,128)(2,1)}, bf16[1024,128]{1,0:T(8,128)(2,1)S(1)}, u32[]{:S(2)}, u32[]{:S(2)}) collective-permute-start(bf16[1024,128]{1,0:T(8,128)(2,1)} %get-tuple-element.74.refs_0_), channel_id=1, source_target_pairs={{0,4},{1,5},{2,6},{3,7},{4,0},{5,1},{6,2},{7,3},{8,12},{9,13},{10,... | collective-permute-start | bytes 786440 | tf_op jit(solution)/shard_map/hidden_far/ppermute | solution.py:17
  41.7 14.2 %collective-permute-start.16 = (bf16[1024,128]{1,0:T(8,128)(2,1)}, bf16[1024,128]{1,0:T(8,128)(2,1)S(1)}, u32[]{:S(2)}, u32[]{:S(2)}) collective-permute-start(bf16[1024,128]{1,0:T(8,128)(2,1)} %get-tuple-element.74.refs_0_), channel_id=1, source_target_pairs={{0,2},{1,3},{2,0},{3,1},{4,6},{5,7},{6,4},{7,5},{8,10},{9,11},{10,... | collective-permute-start | bytes 786440 | tf_op jit(solution)/shard_map/hidden_near/ppermute | solution.py:17
  47.0 8.9 %collective-permute-start.13 = (bf16[3,3,128,128]{3,2,1,0:T(8,128)(2,1)S(1)}, bf16[3,3,128,128]{3,2,1,0:T(8,128)(2,1)S(1)}, u32[]{:S(2)}, u32[]{:S(2)}) collective-permute-start(bf16[3,3,128,128]{3,2,1,0:T(8,128)(2,1)S(1)} %slice.50), channel_id=1, source_target_pairs={{0,16},{8,24},{16,0},{24,8},{1,17},{9,25},{17,1},{25,9},{2,18},{10... | collective-permute-start | bytes 884744 | tf_op jit(solution)/shard_map/two_low/ppermute | solution.py:17
  48.6 7.7 %collective-permute-start.14 = (bf16[3,3,128,128]{3,2,1,0:T(8,128)(2,1)S(1)}, bf16[3,3,128,128]{3,2,1,0:T(8,128)(2,1)S(1)}, u32[]{:S(2)}, u32[]{:S(2)}) collective-permute-start(bf16[3,3,128,128]{3,2,1,0:T(8,128)(2,1)S(1)} %slice.51), channel_id=1, source_target_pairs={{0,8},{8,0},{16,24},{24,16},{1,9},{9,1},{17,25},{25,17},{2,10},{10... | collective-permute-start | bytes 884744 | tf_op jit(solution)/shard_map/two_high/ppermute | solution.py:17
  49.7 59.4 %copy-start.1 = (bf16[2,1024,128]{2,1,0:T(8,128)(2,1)}, bf16[2,1024,128]{2,1,0:T(8,128)(2,1)S(1)}, u32[]{:S(2)}) copy-start(bf16[2,1024,128]{2,1,0:T(8,128)(2,1)S(1)} %get-tuple-element.108.refs_5_.refs_0_) | copy-start | bytes 1572868
  55.9 18.1 %copy-start.6 = (bf16[1024,128]{1,0:T(8,128)(2,1)}, bf16[1024,128]{1,0:T(8,128)(2,1)S(1)}, u32[]{:S(2)}) copy-start(bf16[1024,128]{1,0:T(8,128)(2,1)S(1)} %collective-permute-done.15.refs_2_) | copy-start | bytes 786436
  55.9 18.1 %copy-start.7 = (bf16[1024,128]{1,0:T(8,128)(2,1)}, bf16[1024,128]{1,0:T(8,128)(2,1)S(1)}, u32[]{:S(2)}) copy-start(bf16[1024,128]{1,0:T(8,128)(2,1)S(1)} %collective-permute-done.16.refs_1_) | copy-start | bytes 786436
  57.0 12.6 %copy-start.5 = (bf16[1024,128]{1,0:T(8,128)(2,1)S(1)}, bf16[1024,128]{1,0:T(8,128)(2,1)}, u32[]{:S(2)}) copy-start(bf16[1024,128]{1,0:T(8,128)(2,1)} %get-tuple-element.74.refs_0_) | copy-start | bytes 786436
  60.8 12.6 %copy-start = (bf16[4,1024,128]{2,1,0:T(8,128)(2,1)S(1)}, bf16[4,1024,128]{2,1,0:T(8,128)(2,1)}, u32[]{:S(2)}) copy-start(bf16[4,1024,128]{2,1,0:T(8,128)(2,1)} %get-tuple-element.87) | copy-start | bytes 3145732
  60.8 12.6 %collective-permute-start.17 = (bf16[4,1024,128]{2,1,0:T(8,128)(2,1)}, bf16[4,1024,128]{2,1,0:T(8,128)(2,1)S(1)}, u32[]{:S(2)}, u32[]{:S(2)}) collective-permute-start(bf16[4,1024,128]{2,1,0:T(8,128)(2,1)} %get-tuple-element.88), channel_id=1, source_target_pairs={{0,1},{1,0},{2,3},{3,2},{4,5},{5,4},{6,7},{7,6},{8,9},{9,8},{10,11... | collective-permute-start | bytes 3145736 | tf_op jit(solution)/shard_map/back_core/ppermute | solution.py:17
  60.9 8.7 %collective-permute-start.19 = (bf16[1024,128]{1,0:T(8,128)(2,1)S(1)}, bf16[1024,128]{1,0:T(8,128)(2,1)S(1)}, u32[]{:S(2)}, u32[]{:S(2)}) collective-permute-start(bf16[1024,128]{1,0:T(8,128)(2,1)S(1)} %collective-permute-done.15.refs_2_), channel_id=1, source_target_pairs={{0,2},{1,3},{2,0},{3,1},{4,6},{5,7},{6,4},{7,5},{8,10},{9,11},{10,... | collective-permute-start | bytes 786440 | tf_op jit(solution)/shard_map/hidden_last/ppermute | solution.py:17
  69.8 27.4 %collective-permute-start.22 = (bf16[4,1024,128]{2,1,0:T(8,128)(2,1)S(1)}, bf16[4,1024,128]{2,1,0:T(8,128)(2,1)S(1)}, u32[]{:S(2)}, u32[]{:S(2)}) collective-permute-start(bf16[4,1024,128]{2,1,0:T(8,128)(2,1)S(1)} %pad_maximum_fusion), channel_id=1, source_target_pairs={{0,1},{1,0},{2,3},{3,2},{4,5},{5,4},{6,7},{7,6},{8,9},{9,8},{10,11... | collective-permute-start | bytes 3145736 | tf_op jit(solution)/shard_map/hidden_core/ppermute | solution.py:17
  69.8 14.8 %collective-permute-start.26 = (bf16[2,1024,128]{2,1,0:T(8,128)(2,1)S(1)}, bf16[2,1024,128]{2,1,0:T(8,128)(2,1)S(1)}, u32[]{:S(2)}, u32[]{:S(2)}) collective-permute-start(bf16[2,1024,128]{2,1,0:T(8,128)(2,1)S(1)} %get-tuple-element.98), channel_id=1, source_target_pairs={{0,8},{8,0},{16,24},{24,16},{1,9},{9,1},{17,25},{25,17},{2,10},{10... | collective-permute-start | bytes 1572872 | tf_op jit(solution)/shard_map/input1/ppermute | solution.py:17
  71.0 25.2 %collective-permute-start.27 = (bf16[2,1024,128]{2,1,0:T(8,128)(2,1)S(1)}, bf16[2,1024,128]{2,1,0:T(8,128)(2,1)S(1)}, u32[]{:S(2)}, u32[]{:S(2)}) collective-permute-start(bf16[2,1024,128]{2,1,0:T(8,128)(2,1)S(1)} %get-tuple-element.99), channel_id=1, source_target_pairs={{0,16},{8,24},{16,0},{24,8},{1,17},{9,25},{17,1},{25,9},{2,18},{10... | collective-permute-start | bytes 1572872 | tf_op jit(solution)/shard_map/input2/ppermute | solution.py:17
  71.5 25.6 %collective-permute-start.28 = (bf16[2,1024,128]{2,1,0:T(8,128)(2,1)S(1)}, bf16[2,1024,128]{2,1,0:T(8,128)(2,1)S(1)}, u32[]{:S(2)}, u32[]{:S(2)}) collective-permute-start(bf16[2,1024,128]{2,1,0:T(8,128)(2,1)S(1)} %get-tuple-element.100), channel_id=1, source_target_pairs={{0,24},{8,16},{16,8},{24,0},{1,25},{9,17},{17,9},{25,1},{2,26},{10... | collective-permute-start | bytes 1572872 | tf_op jit(solution)/shard_map/input3/ppermute | solution.py:17
  73.5 7.9 %collective-permute-start.18 = (bf16[1024,128]{1,0:T(8,128)(2,1)S(1)}, bf16[1024,128]{1,0:T(8,128)(2,1)S(1)}, u32[]{:S(2)}, u32[]{:S(2)}) collective-permute-start(bf16[1024,128]{1,0:T(8,128)(2,1)S(1)} %get-tuple-element.119), channel_id=1, source_target_pairs={{0,2},{1,3},{2,0},{3,1},{4,6},{5,7},{6,4},{7,5},{8,10},{9,11},{10,... | collective-permute-start | bytes 786440 | tf_op jit(solution)/shard_map/relayed/ppermute | solution.py:17
  74.2 36.4 %copy-start.8 = (bf16[1024,128]{1,0:T(8,128)(2,1)}, bf16[1024,128]{1,0:T(8,128)(2,1)S(1)}, u32[]{:S(2)}) copy-start(bf16[1024,128]{1,0:T(8,128)(2,1)S(1)} %get-tuple-element.104.refs_0_) | copy-start | bytes 786436
  81.5 26.6 %collective-permute-start.20 = (bf16[1024,128]{1,0:T(8,128)(2,1)S(1)}, bf16[1024,128]{1,0:T(8,128)(2,1)S(1)}, u32[]{:S(2)}, u32[]{:S(2)}) collective-permute-start(bf16[1024,128]{1,0:T(8,128)(2,1)S(1)} %fusion), channel_id=1, source_target_pairs={{0,4},{1,5},{2,6},{3,7},{4,0},{5,1},{6,2},{7,3},{8,12},{9,13},{10,... | collective-permute-start | bytes 786440 | tf_op jit(solution)/shard_map/distant/ppermute | solution.py:17
  84.6 24.6 %copy-start.10 = (bf16[2,1024,128]{2,1,0:T(8,128)(2,1)}, bf16[2,1024,128]{2,1,0:T(8,128)(2,1)S(1)}, u32[]{:S(2)}) copy-start(bf16[2,1024,128]{2,1,0:T(8,128)(2,1)S(1)} %collective-permute-done.26.refs_6_.refs_0_) | copy-start | bytes 1572868
  84.6 23.5 %collective-permute-start.21 = (bf16[1024,128]{1,0:T(8,128)(2,1)S(1)}, bf16[1024,128]{1,0:T(8,128)(2,1)S(1)}, u32[]{:S(2)}, u32[]{:S(2)}) collective-permute-start(bf16[1024,128]{1,0:T(8,128)(2,1)S(1)} %get-tuple-element.92), channel_id=1, source_target_pairs={{0,2},{1,3},{2,0},{3,1},{4,6},{5,7},{6,4},{7,5},{8,10},{9,11},{10,... | collective-permute-start | bytes 786440 | tf_op jit(solution)/shard_map/nearby/ppermute | solution.py:17
  96.3 13.0 %copy-start.28 = (bf16[2,1024,128]{2,1,0:T(8,128)(2,1)}, bf16[2,1024,128]{2,1,0:T(8,128)(2,1)S(1)}, u32[]{:S(2)}) copy-start(bf16[2,1024,128]{2,1,0:T(8,128)(2,1)S(1)} %collective-permute-done.27.refs_7_.refs_1_) | copy-start | bytes 1572868
  96.3 11.9 %collective-permute-start.23 = (bf16[1024,128]{1,0:T(8,128)(2,1)S(1)}, bf16[1024,128]{1,0:T(8,128)(2,1)S(1)}, u32[]{:S(2)}, u32[]{:S(2)}) collective-permute-start(bf16[1024,128]{1,0:T(8,128)(2,1)S(1)} %get-tuple-element.94), channel_id=1, source_target_pairs={{0,8},{8,0},{16,24},{24,16},{1,9},{9,1},{17,25},{25,17},{2,10},{10... | collective-permute-start | bytes 786440 | tf_op jit(solution)/shard_map/hidden_to1/ppermute | solution.py:17
  97.2 12.0 %collective-permute-start.24 = (bf16[1024,128]{1,0:T(8,128)(2,1)S(1)}, bf16[1024,128]{1,0:T(8,128)(2,1)S(1)}, u32[]{:S(2)}, u32[]{:S(2)}) collective-permute-start(bf16[1024,128]{1,0:T(8,128)(2,1)S(1)} %get-tuple-element.95), channel_id=1, source_target_pairs={{0,16},{8,24},{16,0},{24,8},{1,17},{9,25},{17,1},{25,9},{2,18},{10... | collective-permute-start | bytes 786440 | tf_op jit(solution)/shard_map/hidden_to2/ppermute | solution.py:17
  98.9 10.2 %collective-permute-start.25 = (bf16[1024,128]{1,0:T(8,128)(2,1)S(1)}, bf16[1024,128]{1,0:T(8,128)(2,1)S(1)}, u32[]{:S(2)}, u32[]{:S(2)}) collective-permute-start(bf16[1024,128]{1,0:T(8,128)(2,1)S(1)} %get-tuple-element.96), channel_id=1, source_target_pairs={{0,24},{8,16},{16,8},{24,0},{1,25},{9,17},{17,9},{25,1},{2,26},{10... | collective-permute-start | bytes 786440 | tf_op jit(solution)/shard_map/hidden_to3/ppermute | solution.py:17
  110.5 4.9 %collective-permute-start.33 = (bf16[4,1024,128]{2,1,0:T(8,128)(2,1)S(1)}, bf16[4,1024,128]{2,1,0:T(8,128)(2,1)S(1)}, u32[]{:S(2)}, u32[]{:S(2)}) collective-permute-start(bf16[4,1024,128]{2,1,0:T(8,128)(2,1)S(1)} %pad_maximum_fusion.2), channel_id=1, source_target_pairs={{0,1},{1,0},{2,3},{3,2},{4,5},{5,4},{6,7},{7,6},{8,9},{9,8},{10,11... | collective-permute-start | bytes 3145736 | tf_op jit(solution)/shard_map/field_swap/ppermute | solution.py:17
  110.7 9.5 %collective-permute-start.32 = (bf16[4,1024,128]{2,1,0:T(8,128)(2,1)S(1)}, bf16[4,1024,128]{2,1,0:T(8,128)(2,1)S(1)}, u32[]{:S(2)}, u32[]{:S(2)}) collective-permute-start(bf16[4,1024,128]{2,1,0:T(8,128)(2,1)S(1)} %pad_maximum_fusion.1), channel_id=1, source_target_pairs={{0,1},{1,0},{2,3},{3,2},{4,5},{5,4},{6,7},{7,6},{8,9},{9,8},{10,11... | collective-permute-start | bytes 3145736 | tf_op jit(solution)/shard_map/hidden_swap/ppermute | solution.py:17
  111.8 16.5 %collective-permute-start.29 = (bf16[1024,128]{1,0:T(8,128)(2,1)S(1)}, bf16[1024,128]{1,0:T(8,128)(2,1)S(1)}, u32[]{:S(2)}, u32[]{:S(2)}) collective-permute-start(bf16[1024,128]{1,0:T(8,128)(2,1)S(1)} %fusion.4.refs_2_), channel_id=1, source_target_pairs={{0,8},{8,0},{16,24},{24,16},{1,9},{9,1},{17,25},{25,17},{2,10},{10... | collective-permute-start | bytes 786440 | tf_op jit(solution)/shard_map/pre1/ppermute | solution.py:17
  113.5 14.8 %collective-permute-start.30 = (bf16[1024,128]{1,0:T(8,128)(2,1)S(1)}, bf16[1024,128]{1,0:T(8,128)(2,1)S(1)}, u32[]{:S(2)}, u32[]{:S(2)}) collective-permute-start(bf16[1024,128]{1,0:T(8,128)(2,1)S(1)} %fusion.4.refs_2_), channel_id=1, source_target_pairs={{0,16},{8,24},{16,0},{24,8},{1,17},{9,25},{17,1},{25,9},{2,18},{10... | collective-permute-start | bytes 786440 | tf_op jit(solution)/shard_map/pre2/ppermute | solution.py:17
  114.2 14.1 %collective-permute-start.31 = (bf16[1024,128]{1,0:T(8,128)(2,1)S(1)}, bf16[1024,128]{1,0:T(8,128)(2,1)S(1)}, u32[]{:S(2)}, u32[]{:S(2)}) collective-permute-start(bf16[1024,128]{1,0:T(8,128)(2,1)S(1)} %fusion.4.refs_2_), channel_id=1, source_target_pairs={{0,24},{8,16},{16,8},{24,0},{1,25},{9,17},{17,9},{25,1},{2,26},{10... | collective-permute-start | bytes 786440 | tf_op jit(solution)/shard_map/pre3/ppermute | solution.py:17
  (28 other events, 62.9 us)

commit v4 on v3

--- a/solution.py
+++ b/solution.py
@@ -347,13 +347,53 @@
     )(place, grads, *weights, keep, send)
 
 
+def tap_grads(fields, shifted):
+    stacked = jnp.concatenate([shifted[(2 - p) * COLS : (2 - p) * COLS + CELLS, :] for p in TAPS], axis=1)
+    sums = lax.dot_general(fields, stacked, (((0,), (0,)), ((), ())), preferred_element_type=F32)
+    return lambda p, q: sums[:, (3 * p + q) * WIDE : (3 * p + q + 1) * WIDE]
+
+
+def crop_grad_kernel(count, place, grads, *refs):
+    fields, (out_x, out_y, pass_low, pass_high, own, held, shifted, sems) = refs[:count], refs[count:]
+    copies = start_all(field_pairs(place, fields, held), sems)
+    spread(grads[...], shifted)
+    for copy in copies:
+        copy.wait()
+    half = TALL // 2
+    targets = {3: (out_x.at[0], out_y.at[0]), 1: (out_x.at[1], pass_high), 2: (pass_low, out_y.at[1])}
+    for k in (3, 1, 2, 0):
+        sums = tap_grads(held[COLS : COLS + CELLS, k * TALL : (k + 1) * TALL], shifted)
+        for p in TAPS:
+            for q in TAPS:
+                part = sums(p, q)
+                if k == 0:
+                    own[p, q] = part
+                else:
+                    low, high = targets[k]
+                    low[p, q] = part[:half].astype(BF16)
+                    high[p, q] = part[half:].astype(BF16)
+
+
+def crop_grads(place, grads, fields):
+    half = TALL // 2
+    return kernel_call(
+        functools.partial(crop_grad_kernel, len(fields)),
+        [bf16(2, 3, 3, half, WIDE)] * 2 + [bf16(3, 3, half, WIDE)] * 2 + [f32(3, 3, TALL, WIDE)],
+        [SMEM, VMEM] + [ANY] * len(fields),
+        [
+            pltpu.VMEM((CELLS + 2 * COLS, 4 * TALL), BF16),
+            pltpu.VMEM((CELLS + 2 * COLS, 3 * WIDE), BF16),
+            pltpu.SemaphoreType.DMA((8,)),
+        ],
+        1,
+    )(place, grads, *fields)
+
+
 def grad_kernel(slots, adds, place, *refs):
     count = len(slots)
     mine, other, grads = refs[:count], refs[count], refs[count + 1 : 2 * count + 1]
     before = refs[2 * count + 1] if adds else None
     out, held, cots, shifted, sems = refs[2 * count + 1 + adds :]
-    mine = [ref if len(ref.shape) == 2 else ref.at[1] for ref in mine]
-    grads = [ref if len(ref.shape) == 2 else ref.at[0] for ref in grads]
     core = place[0] & 1
     pairs = []
     for n, slot in enumerate(slots):
@@ -365,15 +405,11 @@
         for copy in copies[3 * n : 3 * n + 3]:
             copy.wait()
         spread(cots[n], shifted)
+        sums = tap_grads(held[n], shifted)
         for p in TAPS:
-            begin = (2 - p) * COLS
-            sums = lax.dot_general(
-                held[n], shifted[begin : begin + CELLS, :], (((0,), (0,)), ((), ())), preferred_element_type=F32
-            )
             for q in TAPS:
-                part = sums[:, q * WIDE : (q + 1) * WIDE]
                 earlier = before if n == 0 else out
-                out[p, q] = part if earlier is None else earlier[p, q] + part
+                out[p, q] = sums(p, q) if earlier is None else earlier[p, q] + sums(p, q)
 
 
 def weight_grads(place, mine, other, grads, before, slots):
@@ -457,7 +493,7 @@
 
     two_low, two_high = far_weights(two_x, two_y, "two")
     keep, send = scoped("back_near", back_near, place, cotangent, (weight_two, two_x, two_y))
-    inputs = [jnp.stack([cotangent, pick(field_z, owner ^ k)]) for k in range(4)]
+    inputs = [pick(field_z, owner ^ k) for k in range(4)]
     two_low, two_high, keep, send, hidden_far, hidden_near, *inputs = together(
         two_low, two_high, keep, send, hidden_far, hidden_near, *inputs
     )
@@ -465,37 +501,42 @@
     inputs = others(inputs, "input")
     hidden_last = over_filter(hidden_far, 2, "hidden_last")
     keep, send = scoped("back_far", back_far, place, cotangent, (two_low, two_high), keep, send)
+    keep, send, hidden_last = together(keep, send, hidden_last)
     got = over_filter(send, 1, "back_core")
     chip = lambda n: keep[n].astype(F32) + got[n].astype(F32)
     chip_one, chip_three = chip(1).astype(BF16), chip(3).astype(BF16)
     relayed = over_filter(chip_three, 2, "relayed")
     hidden_z = (hidden, hidden_near, hidden_far, hidden_last)
-    hidden_stack = jnp.stack(hidden_z)
-    hidden_picked = [pick(hidden_z, owner ^ k) for k in range(4)]
+    hidden_core = over_filter(jnp.stack(hidden_z), 1, "hidden_core")
+    out_x, out_y, pass_low, pass_high, own = scoped(
+        "crop_grads", crop_grads, place, cotangent, (*hidden_z, hidden_core)
+    )
     chip_two = (chip(2) + relayed.astype(F32)).astype(BF16)
-    hidden_core = over_filter(hidden_stack, 1, "hidden_core")
-    chip_one, chip_two, *hidden_picked = together(chip_one, chip_two, *hidden_picked)
+    chip_one, chip_two, out_x, out_y, *inputs = together(chip_one, chip_two, out_x, out_y, *inputs)
 
     distant, nearby = over_filter(chip_two, 4, "distant"), over_filter(chip_one, 2, "nearby")
+    got_x, got_y = over_dp(out_x, 1, "grad_x"), over_dp(out_y, 2, "grad_y")
     full_two = (weight_two, two_x, two_y, two_low, two_high)
     output = scoped("conv_two", conv, 1, place, (*hidden_z, hidden_core), full_two)[0]
-    hidden_mine = others(hidden_picked, "hidden_to")
-    distant, nearby, output, *rest = together(distant, nearby, output, *hidden_mine, *inputs)
-    hidden_mine, inputs = rest[:4], rest[4:]
-
-    field_swapped = over_filter(jnp.stack([v[1] for v in inputs]), 1, "field_swap")
+    distant, nearby, output = together(distant, nearby, output)
+
+    field_swapped = over_filter(jnp.stack(inputs), 1, "field_swap")
     back = chip(0) + nearby.astype(F32) + distant.astype(F32)
     sigma = jax.nn.sigmoid(pre_one)
     back_pre = (back * sigma * (1.0 + pre_one * (1.0 - sigma))).astype(BF16)
     back_all = others([back_pre] * 4, "pre")
-    hidden_swapped = over_filter(jnp.stack(hidden_mine), 1, "hidden_swap")
-    grad_two = scoped(
-        "grad_two", weight_grads, place, hidden_mine, hidden_swapped, inputs, None, (0, 1, 2, 3)
-    )
     grad_one = scoped("grad_one_own", weight_grads, place, inputs[:1], field_swapped, back_all[:1], None, (0,))
-    *back_rest, grad_two, grad_one, output = together(*back_all[1:], grad_two, grad_one, output)
+    wide = lambda value: value.astype(F32)
+    to_y = (wide(pass_low) + wide(got_x[0])).astype(BF16)
+    to_x = (wide(pass_high) + wide(got_y[0])).astype(BF16)
+    last_low, last_high = over_dp(to_y, 2, "grad_low"), over_dp(to_x, 1, "grad_high")
+    grad_one, *back_rest = together(grad_one, *back_all[1:])
     grad_one = scoped(
         "grad_one", weight_grads, place, inputs[1:], field_swapped, back_rest, grad_one, (1, 2, 3)
+    )
+    half = TALL // 2
+    grad_two = own + jnp.concatenate(
+        [wide(got_x[1]) + wide(last_low), wide(got_y[1]) + wide(last_high)], axis=2
     )
     return (output.reshape(1, ROWS, COLS, WIDE), grad_one, grad_two)
 

time: 137 us -> 128 us (0.934)
  waiting for transfers between devices: 50.3 us -> 40 us
  starting transfers between devices: 32.4 us -> 38.4 us
  local copies, waits for them, and re-layouts: 8.27 us -> 3.62 us
    ppermute x34, waiting for transfers between devices: 50.3 us -> 40 us  [swap(): return lax.ppermute(values, axis, [(i, i ^ flip) for i in range(size)])]
    pallas_call x3 -> x2, Pallas kernels: 17.6 us -> 10 us  [weight_grads(): kernel_call(functools.partial(grad_kernel, slots, adds), [f32(3, 3, TALL,...]
    pallas_call x0 -> x1, Pallas kernels: none -> 6.5 us  [crop_grads(): kernel_call(functools.partial(crop_grad_kernel, len(fields)), [bf16(2, 3,...]
    ppermute x34, starting transfers between devices: 32.4 us -> 38.4 us  [swap(): return lax.ppermute(values, axis, [(i, i ^ flip) for i in range(size)])]
    unnamed x82 -> x74, local copies, waits for them, and re-layouts: 7.12 us -> 3.54 us
  transfers between devices with their start and end apart: 34 -> 34, of which waited for: 12 -> 14; matrix products, arithmetic and copies ran while one was open for 1% -> 2% of each run, Pallas kernels for 23% -> 27%
where the time goes in v4:
time: 128 us; the launch traced here: 127 us
  Pallas kernels  41 us (32%)
  waiting for transfers between devices  40 us (31%)
  starting transfers between devices  38.4 us (30%)
  local copies, waits for them, and re-layouts  3.62 us (3%)
  other arithmetic  3.02 us (2%)
  between operations  1.36 us (1%)
    ppermute x34, waiting for transfers between devices, swap(): return lax.ppermute(values, axis, [(i, i ^ flip) for i in range(size)])  40 us
    ppermute x34, starting transfers between devices, swap(): return lax.ppermute(values, axis, [(i, i ^ flip) for i in range(size)])  38.4 us
    pallas_call x2, Pallas kernels, conv(): kernel_call(functools.partial(conv_kernel, layer, len(fields)), ([f32(CEL...  14.7 us
    pallas_call x2, Pallas kernels, weight_grads(): kernel_call(functools.partial(grad_kernel, slots, adds), [f32(3, 3, TALL,...  10 us
    pallas_call x1, Pallas kernels, crop_grads(): kernel_call(functools.partial(crop_grad_kernel, len(fields)), [bf16(2, 3,...  6.5 us
    pallas_call x1, Pallas kernels, back_near(): kernel_call(back_near_kernel, [bf16(4, CELLS, WIDE)] * 2, [SMEM, VMEM] +...  6.04 us
    pallas_call x1, Pallas kernels, back_far(): kernel_call(back_far_kernel, [bf16(4, CELLS, WIDE)] * 2, [SMEM, VMEM] + [...  3.71 us
    unnamed x74, local copies, waits for them, and re-layouts  3.54 us
  transfers between devices with their start and end apart: 34, of which 14 were waited for; matrix products, arithmetic and copies ran while one was open for 2% of the time, Pallas kernels for 27%

profile of v4, /device:TPU:0, one launch (start us, length us, event | category | flops | bytes accessed | tf_op | source)
XLA Modules:
  0.0 127.4 jit_solution(16207689837418295648)
XLA Ops:
  0.6 3.0 %collective-permute-start.2 = (bf16[3,3,256,128]{3,2,1,0:T(8,128)(2,1)}, bf16[3,3,256,128]{3,2,1,0:T(8,128)(2,1)S(1)}, u32[]{:S(2)}, u32[]{:S(2)}) collective-permute-start(bf16[3,3,256,128]{3,2,1,0:T(8,128)(2,1)} %refs_8_.1), channel_id=1, source_target_pairs={{0,8},{8,0},{16,24},{24,16},{1,9},{9,1},{17,25},{25,17},{2,10},{10... | collective-permute-start | bytes 1769480 | tf_op jit(solution)/shard_map/one_x/ppermute | solution.py:17
  3.6 1.5 %collective-permute-start.3 = (bf16[3,3,256,128]{3,2,1,0:T(8,128)(2,1)}, bf16[3,3,256,128]{3,2,1,0:T(8,128)(2,1)S(1)}, u32[]{:S(2)}, u32[]{:S(2)}) collective-permute-start(bf16[3,3,256,128]{3,2,1,0:T(8,128)(2,1)} %refs_8_.1), channel_id=1, source_target_pairs={{0,16},{8,24},{16,0},{24,8},{1,17},{9,25},{17,1},{25,9},{2,18},{10... | collective-permute-start | bytes 1769480 | tf_op jit(solution)/shard_map/one_y/ppermute | solution.py:17
  5.2 2.6 %collective-permute-start.1 = (bf16[1024,128]{1,0:T(8,128)(2,1)}, bf16[1024,128]{1,0:T(8,128)(2,1)S(1)}, u32[]{:S(2)}, u32[]{:S(2)}) collective-permute-start(bf16[1024,128]{1,0:T(8,128)(2,1)} %bitcast.53), channel_id=1, source_target_pairs={{0,4},{1,5},{2,6},{3,7},{4,0},{5,1},{6,2},{7,3},{8,12},{9,13},{10,... | collective-permute-start | bytes 786440 | tf_op jit(solution)/shard_map/field_far/ppermute | solution.py:17
  7.7 1.6 %collective-permute-start = (bf16[1024,128]{1,0:T(8,128)(2,1)}, bf16[1024,128]{1,0:T(8,128)(2,1)S(1)}, u32[]{:S(2)}, u32[]{:S(2)}) collective-permute-start(bf16[1024,128]{1,0:T(8,128)(2,1)} %bitcast.54), channel_id=1, source_target_pairs={{0,2},{1,3},{2,0},{3,1},{4,6},{5,7},{6,4},{7,5},{8,10},{9,11},{10,... | collective-permute-start | bytes 786440 | tf_op jit(solution)/shard_map/field_near/ppermute | solution.py:17
  9.3 0.6 pad_add_fusion.place
  9.9 10.8 %collective-permute-done.1.refs_2_ = bf16[1024,128]{1,0:T(8,128)(2,1)S(1)} collective-permute-done((bf16[1024,128]{1,0:T(8,128)(2,1)}, bf16[1024,128]{1,0:T(8,128)(2,1)S(1)}, u32[]{:S(2)}, u32[]{:S(2)}) %collective-permute-start.1) | collective-permute-done | bytes 262176 | tf_op jit(solution)/shard_map/field_far/ppermute | solution.py:17
  22.5 1.5 %collective-permute-start.5 = (bf16[1024,128]{1,0:T(8,128)(2,1)S(1)}, bf16[1024,128]{1,0:T(8,128)(2,1)S(1)}, u32[]{:S(2)}, u32[]{:S(2)}) collective-permute-start(bf16[1024,128]{1,0:T(8,128)(2,1)S(1)} %collective-permute-done.1.refs_2_), channel_id=1, source_target_pairs={{0,2},{1,3},{2,0},{3,1},{4,6},{5,7},{6,4},{7,5},{8,10},{9,11},{10,... | collective-permute-start | bytes 786440 | tf_op jit(solution)/shard_map/field_last/ppermute | solution.py:17
  24.1 6.7 %collective-permute-done.5.refs_3_ = bf16[1024,128]{1,0:T(8,128)(2,1)S(1)} collective-permute-done((bf16[1024,128]{1,0:T(8,128)(2,1)S(1)}, bf16[1024,128]{1,0:T(8,128)(2,1)S(1)}, u32[]{:S(2)}, u32[]{:S(2)}) %collective-permute-start.5) | collective-permute-done | bytes 262176 | tf_op jit(solution)/shard_map/field_last/ppermute | solution.py:17
  30.9 1.7 %collective-permute-done.10.refs_7_ = bf16[1024,128]{1,0:T(8,128)(2,1)} collective-permute-done((bf16[1024,128]{1,0:T(8,128)(2,1)S(1)}, bf16[1024,128]{1,0:T(8,128)(2,1)}, u32[]{:S(2)}, u32[]{:S(2)}) %collective-permute-start.10) | collective-permute-done | bytes 262176 | tf_op jit(solution)/shard_map/field_core3/ppermute | solution.py:17
  32.5 1.6 %collective-permute-start.12 = (bf16[3,3,256,128]{3,2,1,0:T(8,128)(2,1)}, bf16[3,3,256,128]{3,2,1,0:T(8,128)(2,1)S(1)}, u32[]{:S(2)}, u32[]{:S(2)}) collective-permute-start(bf16[3,3,256,128]{3,2,1,0:T(8,128)(2,1)} %refs_5_.1), channel_id=1, source_target_pairs={{0,16},{8,24},{16,0},{24,8},{1,17},{9,25},{17,1},{25,9},{2,18},{10... | collective-permute-start | bytes 1769480 | tf_op jit(solution)/shard_map/two_y/ppermute | solution.py:17
  34.1 1.5 %collective-permute-start.11 = (bf16[3,3,256,128]{3,2,1,0:T(8,128)(2,1)}, bf16[3,3,256,128]{3,2,1,0:T(8,128)(2,1)S(1)}, u32[]{:S(2)}, u32[]{:S(2)}) collective-permute-start(bf16[3,3,256,128]{3,2,1,0:T(8,128)(2,1)} %refs_5_.1), channel_id=1, source_target_pairs={{0,8},{8,0},{16,24},{24,16},{1,9},{9,1},{17,25},{25,17},{2,10},{10... | collective-permute-start | bytes 1769480 | tf_op jit(solution)/shard_map/two_x/ppermute | solution.py:17
  35.6 7.3 %conv_one.1 = (f32[1024,128]{1,0:T(8,128)}, bf16[1024,128]{1,0:T(8,128)(2,1)}) custom-call(s32[2]{0:T(128)} %pad_add_fusion.place, bf16[1024,128]{1,0:T(8,128)(2,1)} %bitcast.55, bf16[1024,128]{1,0:T(8,128)(2,1)} %copy-done.13, bf16[1024,128]{1,0:T(8,128)(2,1)} %copy-done.11, bf16[1024,128]{1,0:T(8,128)(2,1)} %copy-done.15, bf16[1024,128]{1,0:T(8,128)(2,1)} %copy-done.31, ...), custom_call_target="tpu_custom_call" | custom-call | flops 2415919104 | bytes 8388608 | tf_op jit(solution)/shard_map/conv_one/pallas_call | solution.py:258
  43.0 1.5 %collective-permute-start.16 = (bf16[1024,128]{1,0:T(8,128)(2,1)}, bf16[1024,128]{1,0:T(8,128)(2,1)S(1)}, u32[]{:S(2)}, u32[]{:S(2)}) collective-permute-start(bf16[1024,128]{1,0:T(8,128)(2,1)} %get-tuple-element.74.refs_0_), channel_id=1, source_target_pairs={{0,2},{1,3},{2,0},{3,1},{4,6},{5,7},{6,4},{7,5},{8,10},{9,11},{10,... | collective-permute-start | bytes 786440 | tf_op jit(solution)/shard_map/hidden_near/ppermute | solution.py:17
  44.5 2.3 %collective-permute-start.15 = (bf16[1024,128]{1,0:T(8,128)(2,1)}, bf16[1024,128]{1,0:T(8,128)(2,1)S(1)}, u32[]{:S(2)}, u32[]{:S(2)}) collective-permute-start(bf16[1024,128]{1,0:T(8,128)(2,1)} %get-tuple-element.74.refs_0_), channel_id=1, source_target_pairs={{0,4},{1,5},{2,6},{3,7},{4,0},{5,1},{6,2},{7,3},{8,12},{9,13},{10,... | collective-permute-start | bytes 786440 | tf_op jit(solution)/shard_map/hidden_far/ppermute | solution.py:17
  46.8 1.3 collective-permute-done.12.along_y.refs_7_
  48.1 1.3 %collective-permute-done.11.along_x.refs_6_ = bf16[3,3,256,128]{3,2,1,0:T(8,128)(2,1)S(1)} collective-permute-done((bf16[3,3,256,128]{3,2,1,0:T(8,128)(2,1)}, bf16[3,3,256,128]{3,2,1,0:T(8,128)(2,1)S(1)}, u32[]{:S(2)}, u32[]{:S(2)}) %collective-permute-start.11) | collective-permute-done | bytes 589856 | tf_op jit(solution)/shard_map/two_x/ppermute | solution.py:17
  49.5 1.6 %collective-permute-start.14 = (bf16[3,3,128,128]{3,2,1,0:T(8,128)(2,1)S(1)}, bf16[3,3,128,128]{3,2,1,0:T(8,128)(2,1)S(1)}, u32[]{:S(2)}, u32[]{:S(2)}) collective-permute-start(bf16[3,3,128,128]{3,2,1,0:T(8,128)(2,1)S(1)} %slice.51), channel_id=1, source_target_pairs={{0,8},{8,0},{16,24},{24,16},{1,9},{9,1},{17,25},{25,17},{2,10},{10... | collective-permute-start | bytes 884744 | tf_op jit(solution)/shard_map/two_high/ppermute | solution.py:17
  51.6 6.0 %back_near.1 = (bf16[4,1024,128]{2,1,0:T(8,128)(2,1)}, bf16[4,1024,128]{2,1,0:T(8,128)(2,1)}) custom-call(s32[2]{0:T(128)} %pad_add_fusion.place, bf16[1024,128]{1,0:T(8,128)(2,1)} %bitcast.57, bf16[3,3,256,128]{3,2,1,0:T(8,128)(2,1)} %refs_5_.1, bf16[3,3,256,128]{3,2,1,0:T(8,128)(2,1)} %copy-done.25, bf16[3,3,256,128]{3,2,1,0:T(8,128)(2,1)} %copy-done.24), custom_call_target="tpu_custom_call" | custom-call | flops 1811939328 | bytes 6291456 | tf_op jit(solution)/shard_map/back_near/pallas_call | solution.py:303
  57.8 1.0 collective-permute-done.15.refs_2_
  58.8 1.3 collective-permute-start.17
  60.1 3.7 %back_far.1 = (bf16[4,1024,128]{2,1,0:T(8,128)(2,1)}, bf16[4,1024,128]{2,1,0:T(8,128)(2,1)}) custom-call(s32[2]{0:T(128)} %pad_add_fusion.place, bf16[1024,128]{1,0:T(8,128)(2,1)} %bitcast.58, bf16[3,3,128,128]{3,2,1,0:T(8,128)(2,1)} %copy-done.7, bf16[3,3,128,128]{3,2,1,0:T(8,128)(2,1)} %copy-done.6, ...), custom_call_target="tpu_custom_call", output_to_operand_aliasing={{0}: (4, {}), {1}: (5, {})} | custom-call | flops 603979776 | bytes 2097152 | tf_op jit(solution)/shard_map/back_far/pallas_call | solution.py:334
  63.8 1.4 %collective-permute-done.17.refs_3_ = bf16[1024,128]{1,0:T(8,128)(2,1)S(1)} collective-permute-done((bf16[1024,128]{1,0:T(8,128)(2,1)S(1)}, bf16[1024,128]{1,0:T(8,128)(2,1)S(1)}, u32[]{:S(2)}, u32[]{:S(2)}) %collective-permute-start.17) | collective-permute-done | bytes 262176 | tf_op jit(solution)/shard_map/hidden_last/ppermute | solution.py:17
  66.0 2.2 %collective-permute-done.18 = bf16[4,1024,128]{2,1,0:T(8,128)(2,1)S(1)} collective-permute-done((bf16[4,1024,128]{2,1,0:T(8,128)(2,1)}, bf16[4,1024,128]{2,1,0:T(8,128)(2,1)S(1)}, u32[]{:S(2)}, u32[]{:S(2)}) %collective-permute-start.18) | collective-permute-done | bytes 1048608 | tf_op jit(solution)/shard_map/back_core/ppermute | solution.py:17
  68.3 1.3 collective-permute-start.19
  70.1 1.1 collective-permute-start.22
  71.2 1.9 %collective-permute-start.23 = (bf16[1024,128]{1,0:T(8,128)(2,1)S(1)}, bf16[1024,128]{1,0:T(8,128)(2,1)S(1)}, u32[]{:S(2)}, u32[]{:S(2)}) collective-permute-start(bf16[1024,128]{1,0:T(8,128)(2,1)S(1)} %get-tuple-element.99), channel_id=1, source_target_pairs={{0,24},{8,16},{16,8},{24,0},{1,25},{9,17},{17,9},{25,1},{2,26},{10... | collective-permute-start | bytes 786440 | tf_op jit(solution)/shard_map/input3/ppermute | solution.py:17
  73.1 1.0 copy-done.28
  74.0 6.5 %crop_grads.1 = (bf16[2,3,3,128,128]{4,3,2,1,0:T(8,128)(2,1)}, bf16[2,3,3,128,128]{4,3,2,1,0:T(8,128)(2,1)}, bf16[3,3,128,128]{3,2,1,0:T(8,128)(2,1)}, bf16[3,3,...) custom-call(s32[2]{0:T(128)} %pad_add_fusion.place, bf16[1024,128]{1,0:T(8,128)(2,1)} %bitcast.59, ...), custom_call_target="tpu_custom_call" | custom-call | flops 2415919104 | bytes 8388608 | tf_op jit(solution)/shard_map/crop_grads/pallas_call | solution.py:379
  80.7 3.1 %collective-permute-done.23.refs_2_ = bf16[1024,128]{1,0:T(8,128)(2,1)S(1)} collective-permute-done((bf16[1024,128]{1,0:T(8,128)(2,1)S(1)}, bf16[1024,128]{1,0:T(8,128)(2,1)S(1)}, u32[]{:S(2)}, u32[]{:S(2)}) %collective-permute-start.23) | collective-permute-done | bytes 262176 | tf_op jit(solution)/shard_map/input3/ppermute | solution.py:17
  83.8 1.3 %collective-permute-start.30 = (bf16[2,3,3,128,128]{4,3,2,1,0:T(8,128)(2,1)}, bf16[2,3,3,128,128]{4,3,2,1,0:T(8,128)(2,1)S(1)}, u32[]{:S(2)}, u32[]{:S(2)}) collective-permute-start(bf16[2,3,3,128,128]{4,3,2,1,0:T(8,128)(2,1)} %get-tuple-element.115), channel_id=1, source_target_pairs={{0,8},{8,0},{16,24},{24,16},{1,9},{9,1},{17,25},{25,17},{2,10},{10... | collective-permute-start | bytes 1769480 | tf_op jit(solution)/shard_map/grad_x/ppermute | solution.py:17
  85.0 2.3 %collective-permute-start.24 = (bf16[1024,128]{1,0:T(8,128)(2,1)S(1)}, bf16[1024,128]{1,0:T(8,128)(2,1)S(1)}, u32[]{:S(2)}, u32[]{:S(2)}) collective-permute-start(bf16[1024,128]{1,0:T(8,128)(2,1)S(1)} %fusion.6), channel_id=1, source_target_pairs={{0,4},{1,5},{2,6},{3,7},{4,0},{5,1},{6,2},{7,3},{8,12},{9,13},{10,... | collective-permute-start | bytes 786440 | tf_op jit(solution)/shard_map/distant/ppermute | solution.py:17
  87.7 1.1 collective-permute-start.32
  88.8 7.4 %conv_two.1 = bf16[1024,128]{1,0:T(8,128)(2,1)} custom-call(s32[2]{0:T(128)} %pad_add_fusion.place, bf16[1024,128]{1,0:T(8,128)(2,1)} %get-tuple-element.74.refs_0_, bf16[1024,128]{1,0:T(8,128)(2,1)} %copy-done.18, bf16[1024,128]{1,0:T(8,128)(2,1)} %copy-done.20, bf16[1024,128]{1,0:T(8,128)(2,1)} %copy-done.23, bf16[4,1024,128]{2,1,0:T(8,128)(2,1)} %copy-done.28, ...), custom_call_target="tpu_custom_call" | custom-call | flops 2415919104 | bytes 8388608 | tf_op jit(solution)/shard_map/conv_two/pallas_call | solution.py:258
  96.5 1.3 %collective-permute-done.24 = bf16[1024,128]{1,0:T(8,128)(2,1)S(1)} collective-permute-done((bf16[1024,128]{1,0:T(8,128)(2,1)S(1)}, bf16[1024,128]{1,0:T(8,128)(2,1)S(1)}, u32[]{:S(2)}, u32[]{:S(2)}) %collective-permute-start.24) | collective-permute-done | bytes 262176 | tf_op jit(solution)/shard_map/distant/ppermute | solution.py:17
  97.8 1.0 collective-permute-done.25
  98.9 0.8 collective-permute-start.31
  99.7 1.2 collective-permute-done.32
  101.0 1.4 %collective-permute-start.33 = (bf16[3,3,128,128]{3,2,1,0:T(8,128)(2,1)S(1)}, bf16[3,3,128,128]{3,2,1,0:T(8,128)(2,1)S(1)}, u32[]{:S(2)}, u32[]{:S(2)}) collective-permute-start(bf16[3,3,128,128]{3,2,1,0:T(8,128)(2,1)S(1)} %fusion), channel_id=1, source_target_pairs={{0,8},{8,0},{16,24},{24,16},{1,9},{9,1},{17,25},{25,17},{2,10},{10... | collective-permute-start | bytes 884744 | tf_op jit(solution)/shard_map/grad_high/ppermute | solution.py:17
  102.7 1.4 %collective-permute-start.29 = (bf16[1024,128]{1,0:T(8,128)(2,1)S(1)}, bf16[1024,128]{1,0:T(8,128)(2,1)S(1)}, u32[]{:S(2)}, u32[]{:S(2)}) collective-permute-start(bf16[1024,128]{1,0:T(8,128)(2,1)S(1)} %fusion.5.refs_2_), channel_id=1, source_target_pairs={{0,24},{8,16},{16,8},{24,0},{1,25},{9,17},{17,9},{25,1},{2,26},{10... | collective-permute-start | bytes 786440 | tf_op jit(solution)/shard_map/pre3/ppermute | solution.py:17
  104.1 0.8 collective-permute-start.28
  104.9 6.9 %collective-permute-done.31 = bf16[3,3,128,128]{3,2,1,0:T(8,128)(2,1)S(1)} collective-permute-done((bf16[3,3,128,128]{3,2,1,0:T(8,128)(2,1)S(1)}, bf16[3,3,128,128]{3,2,1,0:T(8,128)(2,1)S(1)}, u32[]{:S(2)}, u32[]{:S(2)}) %collective-permute-start.31) | collective-permute-done | bytes 294944 | tf_op jit(solution)/shard_map/grad_low/ppermute | solution.py:17
  111.8 1.5 %collective-permute-start.27 = (bf16[1024,128]{1,0:T(8,128)(2,1)S(1)}, bf16[1024,128]{1,0:T(8,128)(2,1)S(1)}, u32[]{:S(2)}, u32[]{:S(2)}) collective-permute-start(bf16[1024,128]{1,0:T(8,128)(2,1)S(1)} %fusion.5.refs_2_), channel_id=1, source_target_pairs={{0,8},{8,0},{16,24},{24,16},{1,9},{9,1},{17,25},{25,17},{2,10},{10... | collective-permute-start | bytes 786440 | tf_op jit(solution)/shard_map/pre1/ppermute | solution.py:17
  113.5 1.2 maximum_add_fusion
  114.7 1.0 copy-done.4
  115.7 3.7 %grad_one_own.1.refs_7_ = f32[3,3,256,128]{3,2,1,0:T(8,128)} custom-call(s32[2]{0:T(128)} %pad_add_fusion.place, bf16[1024,128]{1,0:T(8,128)(2,1)} %copy-done.1, bf16[4,1024,128]{2,1,0:T(8,128)(2,1)} %copy-done.4, bf16[1024,128]{1,0:T(8,128)(2,1)} %copy-done.3), custom_call_target="tpu_custom_call" | custom-call | flops 603979776 | bytes 2097152 | tf_op jit(solution)/shard_map/grad_one_own/pallas_call | solution.py:418
  119.5 0.7 copy-done.34
  120.2 0.7 copy-done.36
  120.9 6.3 %grad_one.1 = f32[3,3,256,128]{3,2,1,0:T(8,128)} custom-call(s32[2]{0:T(128)} %pad_add_fusion.place, bf16[1024,128]{1,0:T(8,128)(2,1)} %copy-done.19, bf16[1024,128]{1,0:T(8,128)(2,1)} %copy-done.21, bf16[1024,128]{1,0:T(8,128)(2,1)} %copy-done.22, bf16[4,1024,128]{2,1,0:T(8,128)(2,1)} %copy-done.4, bf16[1024,128]{1,0:T(8,128)(2,1)} %copy-done.36, ...), custom_call_target="tpu_custom_call" | custom-call | flops 1811939328 | bytes 6291456 | tf_op jit(solution)/shard_map/grad_one/pallas_call | solution.py:418
  (117 shorter events, 5.5 us)
Async XLA Ops:
  0.6 20.3 %collective-permute-start.2 = (bf16[3,3,256,128]{3,2,1,0:T(8,128)(2,1)}, bf16[3,3,256,128]{3,2,1,0:T(8,128)(2,1)S(1)}, u32[]{:S(2)}, u32[]{:S(2)}) collective-permute-start(bf16[3,3,256,128]{3,2,1,0:T(8,128)(2,1)} %refs_8_.1), channel_id=1, source_target_pairs={{0,8},{8,0},{16,24},{24,16},{1,9},{9,1},{17,25},{25,17},{2,10},{10... | collective-permute-start | bytes 1769480 | tf_op jit(solution)/shard_map/one_x/ppermute | solution.py:17
  3.6 17.3 %collective-permute-start.3 = (bf16[3,3,256,128]{3,2,1,0:T(8,128)(2,1)}, bf16[3,3,256,128]{3,2,1,0:T(8,128)(2,1)S(1)}, u32[]{:S(2)}, u32[]{:S(2)}) collective-permute-start(bf16[3,3,256,128]{3,2,1,0:T(8,128)(2,1)} %refs_8_.1), channel_id=1, source_target_pairs={{0,16},{8,24},{16,0},{24,8},{1,17},{9,25},{17,1},{25,9},{2,18},{10... | collective-permute-start | bytes 1769480 | tf_op jit(solution)/shard_map/one_y/ppermute | solution.py:17
  5.2 4.8 %collective-permute-start.4 = (bf16[1024,128]{1,0:T(8,128)(2,1)}, bf16[1024,128]{1,0:T(8,128)(2,1)S(1)}, u32[]{:S(2)}, u32[]{:S(2)}) collective-permute-start(bf16[1024,128]{1,0:T(8,128)(2,1)} %bitcast.52), channel_id=1, source_target_pairs={{0,1},{1,0},{2,3},{3,2},{4,5},{5,4},{6,7},{7,6},{8,9},{9,8},{10,11... | collective-permute-start | bytes 786440 | tf_op jit(solution)/shard_map/field_core0/ppermute | solution.py:17
  5.2 15.6 %collective-permute-start.1 = (bf16[1024,128]{1,0:T(8,128)(2,1)}, bf16[1024,128]{1,0:T(8,128)(2,1)S(1)}, u32[]{:S(2)}, u32[]{:S(2)}) collective-permute-start(bf16[1024,128]{1,0:T(8,128)(2,1)} %bitcast.53), channel_id=1, source_target_pairs={{0,4},{1,5},{2,6},{3,7},{4,0},{5,1},{6,2},{7,3},{8,12},{9,13},{10,... | collective-permute-start | bytes 786440 | tf_op jit(solution)/shard_map/field_far/ppermute | solution.py:17
  7.7 13.2 %collective-permute-start = (bf16[1024,128]{1,0:T(8,128)(2,1)}, bf16[1024,128]{1,0:T(8,128)(2,1)S(1)}, u32[]{:S(2)}, u32[]{:S(2)}) collective-permute-start(bf16[1024,128]{1,0:T(8,128)(2,1)} %bitcast.54), channel_id=1, source_target_pairs={{0,2},{1,3},{2,0},{3,1},{4,6},{5,7},{6,4},{7,5},{8,10},{9,11},{10,... | collective-permute-start | bytes 786440 | tf_op jit(solution)/shard_map/field_near/ppermute | solution.py:17
  9.9 25.7 %copy-start.31 = (bf16[1024,128]{1,0:T(8,128)(2,1)}, bf16[1024,128]{1,0:T(8,128)(2,1)S(1)}, u32[]{:S(2)}) copy-start(bf16[1024,128]{1,0:T(8,128)(2,1)S(1)} %collective-permute-done.4.refs_4_) | copy-start | bytes 786436
  20.7 14.9 %copy-start.11 = (bf16[1024,128]{1,0:T(8,128)(2,1)}, bf16[1024,128]{1,0:T(8,128)(2,1)S(1)}, u32[]{:S(2)}) copy-start(bf16[1024,128]{1,0:T(8,128)(2,1)S(1)} %collective-permute-done.1.refs_2_) | copy-start | bytes 786436
  20.9 14.7 %copy-start.13 = (bf16[1024,128]{1,0:T(8,128)(2,1)}, bf16[1024,128]{1,0:T(8,128)(2,1)S(1)}, u32[]{:S(2)}) copy-start(bf16[1024,128]{1,0:T(8,128)(2,1)S(1)} %collective-permute-done.refs_1_) | copy-start | bytes 786436
  20.9 14.7 %copy-start.26 = (bf16[3,3,256,128]{3,2,1,0:T(8,128)(2,1)}, bf16[3,3,256,128]{3,2,1,0:T(8,128)(2,1)S(1)}, u32[]{:S(2)}) copy-start(bf16[3,3,256,128]{3,2,1,0:T(8,128)(2,1)S(1)} %collective-permute-done.2.refs_9_) | copy-start | bytes 1769476
  20.9 11.6 %copy-start.27 = (bf16[3,3,256,128]{3,2,1,0:T(8,128)(2,1)}, bf16[3,3,256,128]{3,2,1,0:T(8,128)(2,1)S(1)}, u32[]{:S(2)}) copy-start(bf16[3,3,256,128]{3,2,1,0:T(8,128)(2,1)S(1)} %collective-permute-done.3.refs_10_) | copy-start | bytes 1769476
  21.0 9.8 %collective-permute-start.9 = (bf16[3,3,128,128]{3,2,1,0:T(8,128)(2,1)S(1)}, bf16[3,3,128,128]{3,2,1,0:T(8,128)(2,1)S(1)}, u32[]{:S(2)}, u32[]{:S(2)}) collective-permute-start(bf16[3,3,128,128]{3,2,1,0:T(8,128)(2,1)S(1)} %slice.49), channel_id=1, source_target_pairs={{0,8},{8,0},{16,24},{24,16},{1,9},{9,1},{17,25},{25,17},{2,10},{10... | collective-permute-start | bytes 884744 | tf_op jit(solution)/shard_map/one_high/ppermute | solution.py:17
  21.6 9.2 %collective-permute-start.8 = (bf16[3,3,128,128]{3,2,1,0:T(8,128)(2,1)S(1)}, bf16[3,3,128,128]{3,2,1,0:T(8,128)(2,1)S(1)}, u32[]{:S(2)}, u32[]{:S(2)}) collective-permute-start(bf16[3,3,128,128]{3,2,1,0:T(8,128)(2,1)S(1)} %slice.48), channel_id=1, source_target_pairs={{0,16},{8,24},{16,0},{24,8},{1,17},{9,25},{17,1},{25,9},{2,18},{10... | collective-permute-start | bytes 884744 | tf_op jit(solution)/shard_map/one_low/ppermute | solution.py:17
  22.0 2.0 %collective-permute-start.6 = (bf16[1024,128]{1,0:T(8,128)(2,1)S(1)}, bf16[1024,128]{1,0:T(8,128)(2,1)S(1)}, u32[]{:S(2)}, u32[]{:S(2)}) collective-permute-start(bf16[1024,128]{1,0:T(8,128)(2,1)S(1)} %collective-permute-done.refs_1_), channel_id=1, source_target_pairs={{0,1},{1,0},{2,3},{3,2},{4,5},{5,4},{6,7},{7,6},{8,9},{9,8},{10,11... | collective-permute-start | bytes 786440 | tf_op jit(solution)/shard_map/field_core1/ppermute | solution.py:17
  22.0 2.0 %collective-permute-start.7 = (bf16[1024,128]{1,0:T(8,128)(2,1)S(1)}, bf16[1024,128]{1,0:T(8,128)(2,1)S(1)}, u32[]{:S(2)}, u32[]{:S(2)}) collective-permute-start(bf16[1024,128]{1,0:T(8,128)(2,1)S(1)} %collective-permute-done.1.refs_2_), channel_id=1, source_target_pairs={{0,1},{1,0},{2,3},{3,2},{4,5},{5,4},{6,7},{7,6},{8,9},{9,8},{10,11... | collective-permute-start | bytes 786440 | tf_op jit(solution)/shard_map/field_core2/ppermute | solution.py:17
  22.5 8.2 %collective-permute-start.5 = (bf16[1024,128]{1,0:T(8,128)(2,1)S(1)}, bf16[1024,128]{1,0:T(8,128)(2,1)S(1)}, u32[]{:S(2)}, u32[]{:S(2)}) collective-permute-start(bf16[1024,128]{1,0:T(8,128)(2,1)S(1)} %collective-permute-done.1.refs_2_), channel_id=1, source_target_pairs={{0,2},{1,3},{2,0},{3,1},{4,6},{5,7},{6,4},{7,5},{8,10},{9,11},{10,... | collective-permute-start | bytes 786440 | tf_op jit(solution)/shard_map/field_last/ppermute | solution.py:17
  24.0 10.1 %copy-start.32 = (bf16[1024,128]{1,0:T(8,128)(2,1)}, bf16[1024,128]{1,0:T(8,128)(2,1)S(1)}, u32[]{:S(2)}) copy-start(bf16[1024,128]{1,0:T(8,128)(2,1)S(1)} %collective-permute-done.6.refs_5_) | copy-start | bytes 786436
  30.8 1.7 %collective-permute-start.10 = (bf16[1024,128]{1,0:T(8,128)(2,1)S(1)}, bf16[1024,128]{1,0:T(8,128)(2,1)}, u32[]{:S(2)}, u32[]{:S(2)}) collective-permute-start(bf16[1024,128]{1,0:T(8,128)(2,1)S(1)} %collective-permute-done.5.refs_3_), channel_id=1, source_target_pairs={{0,1},{1,0},{2,3},{3,2},{4,5},{5,4},{6,7},{7,6},{8,9},{9,8},{10,11... | collective-permute-start | bytes 786440 | tf_op jit(solution)/shard_map/field_core3/ppermute | solution.py:17
  32.5 15.6 %collective-permute-start.12 = (bf16[3,3,256,128]{3,2,1,0:T(8,128)(2,1)}, bf16[3,3,256,128]{3,2,1,0:T(8,128)(2,1)S(1)}, u32[]{:S(2)}, u32[]{:S(2)}) collective-permute-start(bf16[3,3,256,128]{3,2,1,0:T(8,128)(2,1)} %refs_5_.1), channel_id=1, source_target_pairs={{0,16},{8,24},{16,0},{24,8},{1,17},{9,25},{17,1},{25,9},{2,18},{10... | collective-permute-start | bytes 1769480 | tf_op jit(solution)/shard_map/two_y/ppermute | solution.py:17
  34.1 15.3 %collective-permute-start.11 = (bf16[3,3,256,128]{3,2,1,0:T(8,128)(2,1)}, bf16[3,3,256,128]{3,2,1,0:T(8,128)(2,1)S(1)}, u32[]{:S(2)}, u32[]{:S(2)}) collective-permute-start(bf16[3,3,256,128]{3,2,1,0:T(8,128)(2,1)} %refs_5_.1), channel_id=1, source_target_pairs={{0,8},{8,0},{16,24},{24,16},{1,9},{9,1},{17,25},{25,17},{2,10},{10... | collective-permute-start | bytes 1769480 | tf_op jit(solution)/shard_map/two_x/ppermute | solution.py:17
  43.0 14.8 %collective-permute-start.16 = (bf16[1024,128]{1,0:T(8,128)(2,1)}, bf16[1024,128]{1,0:T(8,128)(2,1)S(1)}, u32[]{:S(2)}, u32[]{:S(2)}) collective-permute-start(bf16[1024,128]{1,0:T(8,128)(2,1)} %get-tuple-element.74.refs_0_), channel_id=1, source_target_pairs={{0,2},{1,3},{2,0},{3,1},{4,6},{5,7},{6,4},{7,5},{8,10},{9,11},{10,... | collective-permute-start | bytes 786440 | tf_op jit(solution)/shard_map/hidden_near/ppermute | solution.py:17
  44.5 14.3 %collective-permute-start.15 = (bf16[1024,128]{1,0:T(8,128)(2,1)}, bf16[1024,128]{1,0:T(8,128)(2,1)S(1)}, u32[]{:S(2)}, u32[]{:S(2)}) collective-permute-start(bf16[1024,128]{1,0:T(8,128)(2,1)} %get-tuple-element.74.refs_0_), channel_id=1, source_target_pairs={{0,4},{1,5},{2,6},{3,7},{4,0},{5,1},{6,2},{7,3},{8,12},{9,13},{10,... | collective-permute-start | bytes 786440 | tf_op jit(solution)/shard_map/hidden_far/ppermute | solution.py:17
  49.5 9.3 %collective-permute-start.14 = (bf16[3,3,128,128]{3,2,1,0:T(8,128)(2,1)S(1)}, bf16[3,3,128,128]{3,2,1,0:T(8,128)(2,1)S(1)}, u32[]{:S(2)}, u32[]{:S(2)}) collective-permute-start(bf16[3,3,128,128]{3,2,1,0:T(8,128)(2,1)S(1)} %slice.51), channel_id=1, source_target_pairs={{0,8},{8,0},{16,24},{24,16},{1,9},{9,1},{17,25},{25,17},{2,10},{10... | collective-permute-start | bytes 884744 | tf_op jit(solution)/shard_map/two_high/ppermute | solution.py:17
  51.0 7.8 %collective-permute-start.13 = (bf16[3,3,128,128]{3,2,1,0:T(8,128)(2,1)S(1)}, bf16[3,3,128,128]{3,2,1,0:T(8,128)(2,1)S(1)}, u32[]{:S(2)}, u32[]{:S(2)}) collective-permute-start(bf16[3,3,128,128]{3,2,1,0:T(8,128)(2,1)S(1)} %slice.50), channel_id=1, source_target_pairs={{0,16},{8,24},{16,0},{24,8},{1,17},{9,25},{17,1},{25,9},{2,18},{10... | collective-permute-start | bytes 884744 | tf_op jit(solution)/shard_map/two_low/ppermute | solution.py:17
  57.8 38.4 %copy-start.1 = (bf16[1024,128]{1,0:T(8,128)(2,1)}, bf16[1024,128]{1,0:T(8,128)(2,1)S(1)}, u32[]{:S(2)}) copy-start(bf16[1024,128]{1,0:T(8,128)(2,1)S(1)} %get-tuple-element.106.refs_0_) | copy-start | bytes 786436
  57.8 15.2 %copy-start.18 = (bf16[1024,128]{1,0:T(8,128)(2,1)}, bf16[1024,128]{1,0:T(8,128)(2,1)S(1)}, u32[]{:S(2)}) copy-start(bf16[1024,128]{1,0:T(8,128)(2,1)S(1)} %collective-permute-done.16.refs_1_) | copy-start | bytes 786436
  58.8 14.3 %copy-start.20 = (bf16[1024,128]{1,0:T(8,128)(2,1)}, bf16[1024,128]{1,0:T(8,128)(2,1)S(1)}, u32[]{:S(2)}) copy-start(bf16[1024,128]{1,0:T(8,128)(2,1)S(1)} %collective-permute-done.15.refs_2_) | copy-start | bytes 786436
  58.8 6.4 %collective-permute-start.17 = (bf16[1024,128]{1,0:T(8,128)(2,1)S(1)}, bf16[1024,128]{1,0:T(8,128)(2,1)S(1)}, u32[]{:S(2)}, u32[]{:S(2)}) collective-permute-start(bf16[1024,128]{1,0:T(8,128)(2,1)S(1)} %collective-permute-done.15.refs_2_), channel_id=1, source_target_pairs={{0,2},{1,3},{2,0},{3,1},{4,6},{5,7},{6,4},{7,5},{8,10},{9,11},{10,... | collective-permute-start | bytes 786440 | tf_op jit(solution)/shard_map/hidden_last/ppermute | solution.py:17
  65.2 2.9 %collective-permute-start.18 = (bf16[4,1024,128]{2,1,0:T(8,128)(2,1)}, bf16[4,1024,128]{2,1,0:T(8,128)(2,1)S(1)}, u32[]{:S(2)}, u32[]{:S(2)}) collective-permute-start(bf16[4,1024,128]{2,1,0:T(8,128)(2,1)} %get-tuple-element.91), channel_id=1, source_target_pairs={{0,1},{1,0},{2,3},{3,2},{4,5},{5,4},{6,7},{7,6},{8,9},{9,8},{10,11... | collective-permute-start | bytes 3145736 | tf_op jit(solution)/shard_map/back_core/ppermute | solution.py:17
  65.4 7.6 %collective-permute-start.20 = (bf16[4,1024,128]{2,1,0:T(8,128)(2,1)S(1)}, bf16[4,1024,128]{2,1,0:T(8,128)(2,1)S(1)}, u32[]{:S(2)}, u32[]{:S(2)}) collective-permute-start(bf16[4,1024,128]{2,1,0:T(8,128)(2,1)S(1)} %pad_maximum_fusion), channel_id=1, source_target_pairs={{0,1},{1,0},{2,3},{3,2},{4,5},{5,4},{6,7},{7,6},{8,9},{9,8},{10,11... | collective-permute-start | bytes 3145736 | tf_op jit(solution)/shard_map/hidden_core/ppermute | solution.py:17
  68.3 12.2 %collective-permute-start.19 = (bf16[1024,128]{1,0:T(8,128)(2,1)S(1)}, bf16[1024,128]{1,0:T(8,128)(2,1)S(1)}, u32[]{:S(2)}, u32[]{:S(2)}) collective-permute-start(bf16[1024,128]{1,0:T(8,128)(2,1)S(1)} %get-tuple-element.119), channel_id=1, source_target_pairs={{0,2},{1,3},{2,0},{3,1},{4,6},{5,7},{6,4},{7,5},{8,10},{9,11},{10,... | collective-permute-start | bytes 786440 | tf_op jit(solution)/shard_map/relayed/ppermute | solution.py:17
  69.5 11.1 %collective-permute-start.21 = (bf16[1024,128]{1,0:T(8,128)(2,1)S(1)}, bf16[1024,128]{1,0:T(8,128)(2,1)S(1)}, u32[]{:S(2)}, u32[]{:S(2)}) collective-permute-start(bf16[1024,128]{1,0:T(8,128)(2,1)S(1)} %get-tuple-element.97), channel_id=1, source_target_pairs={{0,8},{8,0},{16,24},{24,16},{1,9},{9,1},{17,25},{25,17},{2,10},{10... | collective-permute-start | bytes 786440 | tf_op jit(solution)/shard_map/input1/ppermute | solution.py:17
  70.1 10.6 %collective-permute-start.22 = (bf16[1024,128]{1,0:T(8,128)(2,1)S(1)}, bf16[1024,128]{1,0:T(8,128)(2,1)S(1)}, u32[]{:S(2)}, u32[]{:S(2)}) collective-permute-start(bf16[1024,128]{1,0:T(8,128)(2,1)S(1)} %get-tuple-element.98), channel_id=1, source_target_pairs={{0,16},{8,24},{16,0},{24,8},{1,17},{9,25},{17,1},{25,9},{2,18},{10... | collective-permute-start | bytes 786440 | tf_op jit(solution)/shard_map/input2/ppermute | solution.py:17
  71.2 12.6 %collective-permute-start.23 = (bf16[1024,128]{1,0:T(8,128)(2,1)S(1)}, bf16[1024,128]{1,0:T(8,128)(2,1)S(1)}, u32[]{:S(2)}, u32[]{:S(2)}) collective-permute-start(bf16[1024,128]{1,0:T(8,128)(2,1)S(1)} %get-tuple-element.99), channel_id=1, source_target_pairs={{0,24},{8,16},{16,8},{24,0},{1,25},{9,17},{17,9},{25,1},{2,26},{10... | collective-permute-start | bytes 786440 | tf_op jit(solution)/shard_map/input3/ppermute | solution.py:17
  80.7 15.6 %copy-start.19 = (bf16[1024,128]{1,0:T(8,128)(2,1)}, bf16[1024,128]{1,0:T(8,128)(2,1)S(1)}, u32[]{:S(2)}) copy-start(bf16[1024,128]{1,0:T(8,128)(2,1)S(1)} %collective-permute-done.21.refs_0_) | copy-start | bytes 786436
  80.7 15.6 %copy-start.21 = (bf16[1024,128]{1,0:T(8,128)(2,1)}, bf16[1024,128]{1,0:T(8,128)(2,1)S(1)}, u32[]{:S(2)}) copy-start(bf16[1024,128]{1,0:T(8,128)(2,1)S(1)} %collective-permute-done.22.refs_1_) | copy-start | bytes 786436
  83.8 12.5 %copy-start.22 = (bf16[1024,128]{1,0:T(8,128)(2,1)}, bf16[1024,128]{1,0:T(8,128)(2,1)S(1)}, u32[]{:S(2)}) copy-start(bf16[1024,128]{1,0:T(8,128)(2,1)S(1)} %collective-permute-done.23.refs_2_) | copy-start | bytes 786436
  83.8 15.0 %collective-permute-start.30 = (bf16[2,3,3,128,128]{4,3,2,1,0:T(8,128)(2,1)}, bf16[2,3,3,128,128]{4,3,2,1,0:T(8,128)(2,1)S(1)}, u32[]{:S(2)}, u32[]{:S(2)}) collective-permute-start(bf16[2,3,3,128,128]{4,3,2,1,0:T(8,128)(2,1)} %get-tuple-element.115), channel_id=1, source_target_pairs={{0,8},{8,0},{16,24},{24,16},{1,9},{9,1},{17,25},{25,17},{2,10},{10... | collective-permute-start | bytes 1769480 | tf_op jit(solution)/shard_map/grad_x/ppermute | solution.py:17
  85.0 12.8 %collective-permute-start.24 = (bf16[1024,128]{1,0:T(8,128)(2,1)S(1)}, bf16[1024,128]{1,0:T(8,128)(2,1)S(1)}, u32[]{:S(2)}, u32[]{:S(2)}) collective-permute-start(bf16[1024,128]{1,0:T(8,128)(2,1)S(1)} %fusion.6), channel_id=1, source_target_pairs={{0,4},{1,5},{2,6},{3,7},{4,0},{5,1},{6,2},{7,3},{8,12},{9,13},{10,... | collective-permute-start | bytes 786440 | tf_op jit(solution)/shard_map/distant/ppermute | solution.py:17
  87.4 11.4 %collective-permute-start.25 = (bf16[1024,128]{1,0:T(8,128)(2,1)S(1)}, bf16[1024,128]{1,0:T(8,128)(2,1)S(1)}, u32[]{:S(2)}, u32[]{:S(2)}) collective-permute-start(bf16[1024,128]{1,0:T(8,128)(2,1)S(1)} %get-tuple-element.101), channel_id=1, source_target_pairs={{0,2},{1,3},{2,0},{3,1},{4,6},{5,7},{6,4},{7,5},{8,10},{9,11},{10,... | collective-permute-start | bytes 786440 | tf_op jit(solution)/shard_map/nearby/ppermute | solution.py:17
  87.7 13.1 %collective-permute-start.32 = (bf16[2,3,3,128,128]{4,3,2,1,0:T(8,128)(2,1)}, bf16[2,3,3,128,128]{4,3,2,1,0:T(8,128)(2,1)S(1)}, u32[]{:S(2)}, u32[]{:S(2)}) collective-permute-start(bf16[2,3,3,128,128]{4,3,2,1,0:T(8,128)(2,1)} %get-tuple-element.117), channel_id=1, source_target_pairs={{0,16},{8,24},{16,0},{24,8},{1,17},{9,25},{17,1},{25,9},{2,18},{10... | collective-permute-start | bytes 1769480 | tf_op jit(solution)/shard_map/grad_y/ppermute | solution.py:17
  96.4 18.3 %collective-permute-start.26 = (bf16[4,1024,128]{2,1,0:T(8,128)(2,1)S(1)}, bf16[4,1024,128]{2,1,0:T(8,128)(2,1)S(1)}, u32[]{:S(2)}, u32[]{:S(2)}) collective-permute-start(bf16[4,1024,128]{2,1,0:T(8,128)(2,1)S(1)} %pad_maximum_fusion.1), channel_id=1, source_target_pairs={{0,1},{1,0},{2,3},{3,2},{4,5},{5,4},{6,7},{7,6},{8,9},{9,8},{10,11... | collective-permute-start | bytes 3145736 | tf_op jit(solution)/shard_map/field_swap/ppermute | solution.py:17
  98.9 12.9 %collective-permute-start.31 = (bf16[3,3,128,128]{3,2,1,0:T(8,128)(2,1)S(1)}, bf16[3,3,128,128]{3,2,1,0:T(8,128)(2,1)S(1)}, u32[]{:S(2)}, u32[]{:S(2)}) collective-permute-start(bf16[3,3,128,128]{3,2,1,0:T(8,128)(2,1)S(1)} %fusion.1), channel_id=1, source_target_pairs={{0,16},{8,24},{16,0},{24,8},{1,17},{9,25},{17,1},{25,9},{2,18},{10... | collective-permute-start | bytes 884744 | tf_op jit(solution)/shard_map/grad_low/ppermute | solution.py:17
  101.0 12.5 %collective-permute-start.33 = (bf16[3,3,128,128]{3,2,1,0:T(8,128)(2,1)S(1)}, bf16[3,3,128,128]{3,2,1,0:T(8,128)(2,1)S(1)}, u32[]{:S(2)}, u32[]{:S(2)}) collective-permute-start(bf16[3,3,128,128]{3,2,1,0:T(8,128)(2,1)S(1)} %fusion), channel_id=1, source_target_pairs={{0,8},{8,0},{16,24},{24,16},{1,9},{9,1},{17,25},{25,17},{2,10},{10... | collective-permute-start | bytes 884744 | tf_op jit(solution)/shard_map/grad_high/ppermute | solution.py:17
  102.7 10.8 %copy-start.3 = (bf16[1024,128]{1,0:T(8,128)(2,1)}, bf16[1024,128]{1,0:T(8,128)(2,1)S(1)}, u32[]{:S(2)}) copy-start(bf16[1024,128]{1,0:T(8,128)(2,1)S(1)} %fusion.5.refs_2_) | copy-start | bytes 786436
  102.7 10.8 %copy-start.2 = (f32[3,3,256,128]{3,2,1,0:T(8,128)S(1)}, f32[3,3,256,128]{3,2,1,0:T(8,128)}, u32[]{:S(2)}) copy-start(f32[3,3,256,128]{3,2,1,0:T(8,128)} %get-tuple-element.114) | copy-start | bytes 3538948
  102.7 16.7 %collective-permute-start.29 = (bf16[1024,128]{1,0:T(8,128)(2,1)S(1)}, bf16[1024,128]{1,0:T(8,128)(2,1)S(1)}, u32[]{:S(2)}, u32[]{:S(2)}) collective-permute-start(bf16[1024,128]{1,0:T(8,128)(2,1)S(1)} %fusion.5.refs_2_), channel_id=1, source_target_pairs={{0,24},{8,16},{16,8},{24,0},{1,25},{9,17},{17,9},{25,1},{2,26},{10... | collective-permute-start | bytes 786440 | tf_op jit(solution)/shard_map/pre3/ppermute | solution.py:17
  104.1 15.4 %collective-permute-start.28 = (bf16[1024,128]{1,0:T(8,128)(2,1)S(1)}, bf16[1024,128]{1,0:T(8,128)(2,1)S(1)}, u32[]{:S(2)}, u32[]{:S(2)}) collective-permute-start(bf16[1024,128]{1,0:T(8,128)(2,1)S(1)} %fusion.5.refs_2_), channel_id=1, source_target_pairs={{0,16},{8,24},{16,0},{24,8},{1,17},{9,25},{17,1},{25,9},{2,18},{10... | collective-permute-start | bytes 786440 | tf_op jit(solution)/shard_map/pre2/ppermute | solution.py:17
  111.8 7.6 %collective-permute-start.27 = (bf16[1024,128]{1,0:T(8,128)(2,1)S(1)}, bf16[1024,128]{1,0:T(8,128)(2,1)S(1)}, u32[]{:S(2)}, u32[]{:S(2)}) collective-permute-start(bf16[1024,128]{1,0:T(8,128)(2,1)S(1)} %fusion.5.refs_2_), channel_id=1, source_target_pairs={{0,8},{8,0},{16,24},{24,16},{1,9},{9,1},{17,25},{25,17},{2,10},{10... | collective-permute-start | bytes 786440 | tf_op jit(solution)/shard_map/pre1/ppermute | solution.py:17
  (23 other events, 88.2 us)

commit v5 on v4

--- a/solution.py
+++ b/solution.py
@@ -478,11 +478,10 @@
     one_low, one_high = far_weights(one_x, one_y, "one")
     field_last = over_filter(field_far, 2, "field_last")
     field_core1, field_core2 = over_filter(field_near, 1, "field_core1"), over_filter(field_far, 1, "field_core2")
-    field_last, field_core1, field_core2, one_low, one_high = together(
-        field_last, field_core1, field_core2, one_low, one_high)
+    field_last, field_core1, field_core2, one_low, one_high, weight_gated = together(
+        field_last, field_core1, field_core2, one_low, one_high, weight_two)
     field_core3 = over_filter(field_last, 1, "field_core3")
     field_z = (fields, field_near, field_far, field_last)
-    field_core3, weight_gated = together(field_core3, weight_two)
     two_x, two_y = over_dp(weight_gated, 1, "two_x"), over_dp(weight_gated, 2, "two_y")
     pre_one, hidden = scoped(
         "conv_one", conv, 0, place, (*field_z, field_core0, field_core1, field_core2, field_core3),
@@ -518,14 +517,15 @@
     got_x, got_y = over_dp(out_x, 1, "grad_x"), over_dp(out_y, 2, "grad_y")
     full_two = (weight_two, two_x, two_y, two_low, two_high)
     output = scoped("conv_two", conv, 1, place, (*hidden_z, hidden_core), full_two)[0]
-    distant, nearby, output = together(distant, nearby, output)
-
     field_swapped = over_filter(jnp.stack(inputs), 1, "field_swap")
+    distant, nearby, output, field_swapped = together(distant, nearby, output, field_swapped)
+
     back = chip(0) + nearby.astype(F32) + distant.astype(F32)
     sigma = jax.nn.sigmoid(pre_one)
     back_pre = (back * sigma * (1.0 + pre_one * (1.0 - sigma))).astype(BF16)
     back_all = others([back_pre] * 4, "pre")
     grad_one = scoped("grad_one_own", weight_grads, place, inputs[:1], field_swapped, back_all[:1], None, (0,))
+    got_x, got_y, gate = together(got_x, got_y, back_pre)
     wide = lambda value: value.astype(F32)
     to_y = (wide(pass_low) + wide(got_x[0])).astype(BF16)
     to_x = (wide(pass_high) + wide(got_y[0])).astype(BF16)

time: 128 us -> 127 us (level)
  starting transfers between devices: 38.4 us -> 36.1 us
  waiting for transfers between devices: 40 us -> 41.6 us
    ppermute x34, starting transfers between devices: 38.4 us -> 36.1 us  [swap(): return lax.ppermute(values, axis, [(i, i ^ flip) for i in range(size)])]
    ppermute x34, waiting for transfers between devices: 40 us -> 41.6 us  [swap(): return lax.ppermute(values, axis, [(i, i ^ flip) for i in range(size)])]
    unnamed x74 -> x72, local copies, waits for them, and re-layouts: 3.54 us -> 4.19 us
  transfers between devices with their start and end apart: 34 -> 34, of which waited for: 14 -> 13; matrix products, arithmetic and copies ran while one was open for 2% -> 1% of each run, Pallas kernels for 27% -> 32%
where the time goes in v5:
time: 127 us
  waiting for transfers between devices  41.6 us (33%)
  Pallas kernels  41 us (32%)
  starting transfers between devices  36.1 us (28%)
  local copies, waits for them, and re-layouts  4.28 us (3%)
  other arithmetic  2.92 us (2%)
    ppermute x34, waiting for transfers between devices, swap(): return lax.ppermute(values, axis, [(i, i ^ flip) for i in range(size)])  41.6 us
    ppermute x34, starting transfers between devices, swap(): return lax.ppermute(values, axis, [(i, i ^ flip) for i in range(size)])  36.1 us
    pallas_call x2, Pallas kernels, conv(): kernel_call(functools.partial(conv_kernel, layer, len(fields)), ([f32(CEL...  14.7 us
    pallas_call x2, Pallas kernels, weight_grads(): kernel_call(functools.partial(grad_kernel, slots, adds), [f32(3, 3, TALL,...  10 us
    pallas_call x1, Pallas kernels, crop_grads(): kernel_call(functools.partial(crop_grad_kernel, len(fields)), [bf16(2, 3,...  6.52 us
    pallas_call x1, Pallas kernels, back_near(): kernel_call(back_near_kernel, [bf16(4, CELLS, WIDE)] * 2, [SMEM, VMEM] +...  6.04 us
    unnamed x72, local copies, waits for them, and re-layouts  4.19 us
    pallas_call x1, Pallas kernels, back_far(): kernel_call(back_far_kernel, [bf16(4, CELLS, WIDE)] * 2, [SMEM, VMEM] + [...  3.71 us
  transfers between devices with their start and end apart: 34, of which 13 were waited for; matrix products, arithmetic and copies ran while one was open for 1% of the time, Pallas kernels for 32%

profile of v5, /device:TPU:0, one launch (start us, length us, event | category | flops | bytes accessed | tf_op | source)
XLA Modules:
  0.0 127.0 jit_solution(5911270876349570911)
XLA Ops:
  0.6 3.0 %collective-permute-start.2 = (bf16[3,3,256,128]{3,2,1,0:T(8,128)(2,1)}, bf16[3,3,256,128]{3,2,1,0:T(8,128)(2,1)S(1)}, u32[]{:S(2)}, u32[]{:S(2)}) collective-permute-start(bf16[3,3,256,128]{3,2,1,0:T(8,128)(2,1)} %refs_8_.1), channel_id=1, source_target_pairs={{0,8},{8,0},{16,24},{24,16},{1,9},{9,1},{17,25},{25,17},{2,10},{10... | collective-permute-start | bytes 1769480 | tf_op jit(solution)/shard_map/one_x/ppermute | solution.py:17
  3.6 1.5 %collective-permute-start.3 = (bf16[3,3,256,128]{3,2,1,0:T(8,128)(2,1)}, bf16[3,3,256,128]{3,2,1,0:T(8,128)(2,1)S(1)}, u32[]{:S(2)}, u32[]{:S(2)}) collective-permute-start(bf16[3,3,256,128]{3,2,1,0:T(8,128)(2,1)} %refs_8_.1), channel_id=1, source_target_pairs={{0,16},{8,24},{16,0},{24,8},{1,17},{9,25},{17,1},{25,9},{2,18},{10... | collective-permute-start | bytes 1769480 | tf_op jit(solution)/shard_map/one_y/ppermute | solution.py:17
  5.2 2.6 %collective-permute-start.1 = (bf16[1024,128]{1,0:T(8,128)(2,1)}, bf16[1024,128]{1,0:T(8,128)(2,1)S(1)}, u32[]{:S(2)}, u32[]{:S(2)}) collective-permute-start(bf16[1024,128]{1,0:T(8,128)(2,1)} %bitcast.45), channel_id=1, source_target_pairs={{0,4},{1,5},{2,6},{3,7},{4,0},{5,1},{6,2},{7,3},{8,12},{9,13},{10,... | collective-permute-start | bytes 786440 | tf_op jit(solution)/shard_map/field_far/ppermute | solution.py:17
  7.7 1.6 %collective-permute-start = (bf16[1024,128]{1,0:T(8,128)(2,1)}, bf16[1024,128]{1,0:T(8,128)(2,1)S(1)}, u32[]{:S(2)}, u32[]{:S(2)}) collective-permute-start(bf16[1024,128]{1,0:T(8,128)(2,1)} %bitcast.46), channel_id=1, source_target_pairs={{0,2},{1,3},{2,0},{3,1},{4,6},{5,7},{6,4},{7,5},{8,10},{9,11},{10,... | collective-permute-start | bytes 786440 | tf_op jit(solution)/shard_map/field_near/ppermute | solution.py:17
  9.3 0.6 pad_add_fusion.place
  9.9 10.8 %collective-permute-done.1.refs_2_ = bf16[1024,128]{1,0:T(8,128)(2,1)S(1)} collective-permute-done((bf16[1024,128]{1,0:T(8,128)(2,1)}, bf16[1024,128]{1,0:T(8,128)(2,1)S(1)}, u32[]{:S(2)}, u32[]{:S(2)}) %collective-permute-start.1) | collective-permute-done | bytes 262176 | tf_op jit(solution)/shard_map/field_far/ppermute | solution.py:17
  21.0 0.6 collective-permute-start.9
  22.5 1.5 %collective-permute-start.5 = (bf16[1024,128]{1,0:T(8,128)(2,1)S(1)}, bf16[1024,128]{1,0:T(8,128)(2,1)S(1)}, u32[]{:S(2)}, u32[]{:S(2)}) collective-permute-start(bf16[1024,128]{1,0:T(8,128)(2,1)S(1)} %collective-permute-done.1.refs_2_), channel_id=1, source_target_pairs={{0,2},{1,3},{2,0},{3,1},{4,6},{5,7},{6,4},{7,5},{8,10},{9,11},{10,... | collective-permute-start | bytes 786440 | tf_op jit(solution)/shard_map/field_last/ppermute | solution.py:17
  24.1 6.7 %collective-permute-done.5.refs_3_ = bf16[1024,128]{1,0:T(8,128)(2,1)S(1)} collective-permute-done((bf16[1024,128]{1,0:T(8,128)(2,1)S(1)}, bf16[1024,128]{1,0:T(8,128)(2,1)S(1)}, u32[]{:S(2)}, u32[]{:S(2)}) %collective-permute-start.5) | collective-permute-done | bytes 262176 | tf_op jit(solution)/shard_map/field_last/ppermute | solution.py:17
  30.8 1.6 %collective-permute-start.11 = (bf16[3,3,256,128]{3,2,1,0:T(8,128)(2,1)}, bf16[3,3,256,128]{3,2,1,0:T(8,128)(2,1)S(1)}, u32[]{:S(2)}, u32[]{:S(2)}) collective-permute-start(bf16[3,3,256,128]{3,2,1,0:T(8,128)(2,1)} %refs_5_.1), channel_id=1, source_target_pairs={{0,16},{8,24},{16,0},{24,8},{1,17},{9,25},{17,1},{25,9},{2,18},{10... | collective-permute-start | bytes 1769480 | tf_op jit(solution)/shard_map/two_y/ppermute | solution.py:17
  32.5 1.5 %collective-permute-start.10 = (bf16[3,3,256,128]{3,2,1,0:T(8,128)(2,1)}, bf16[3,3,256,128]{3,2,1,0:T(8,128)(2,1)S(1)}, u32[]{:S(2)}, u32[]{:S(2)}) collective-permute-start(bf16[3,3,256,128]{3,2,1,0:T(8,128)(2,1)} %refs_5_.1), channel_id=1, source_target_pairs={{0,8},{8,0},{16,24},{24,16},{1,9},{9,1},{17,25},{25,17},{2,10},{10... | collective-permute-start | bytes 1769480 | tf_op jit(solution)/shard_map/two_x/ppermute | solution.py:17
  33.9 1.7 %collective-permute-done.12.refs_7_ = bf16[1024,128]{1,0:T(8,128)(2,1)} collective-permute-done((bf16[1024,128]{1,0:T(8,128)(2,1)S(1)}, bf16[1024,128]{1,0:T(8,128)(2,1)}, u32[]{:S(2)}, u32[]{:S(2)}) %collective-permute-start.12) | collective-permute-done | bytes 262176 | tf_op jit(solution)/shard_map/field_core3/ppermute | solution.py:17
  35.7 7.3 %conv_one.1 = (f32[1024,128]{1,0:T(8,128)}, bf16[1024,128]{1,0:T(8,128)(2,1)}) custom-call(s32[2]{0:T(128)} %pad_add_fusion.place, bf16[1024,128]{1,0:T(8,128)(2,1)} %bitcast.47, bf16[1024,128]{1,0:T(8,128)(2,1)} %copy-done.13, bf16[1024,128]{1,0:T(8,128)(2,1)} %copy-done.11, bf16[1024,128]{1,0:T(8,128)(2,1)} %copy-done.15, bf16[1024,128]{1,0:T(8,128)(2,1)} %copy-done.30, ...), custom_call_target="tpu_custom_call" | custom-call | flops 2415919104 | bytes 8388608 | tf_op jit(solution)/shard_map/conv_one/pallas_call | solution.py:258
  43.0 1.5 %collective-permute-start.16 = (bf16[1024,128]{1,0:T(8,128)(2,1)}, bf16[1024,128]{1,0:T(8,128)(2,1)S(1)}, u32[]{:S(2)}, u32[]{:S(2)}) collective-permute-start(bf16[1024,128]{1,0:T(8,128)(2,1)} %get-tuple-element.75.refs_0_), channel_id=1, source_target_pairs={{0,2},{1,3},{2,0},{3,1},{4,6},{5,7},{6,4},{7,5},{8,10},{9,11},{10,... | collective-permute-start | bytes 786440 | tf_op jit(solution)/shard_map/hidden_near/ppermute | solution.py:17
  44.5 2.3 %collective-permute-start.15 = (bf16[1024,128]{1,0:T(8,128)(2,1)}, bf16[1024,128]{1,0:T(8,128)(2,1)S(1)}, u32[]{:S(2)}, u32[]{:S(2)}) collective-permute-start(bf16[1024,128]{1,0:T(8,128)(2,1)} %get-tuple-element.75.refs_0_), channel_id=1, source_target_pairs={{0,4},{1,5},{2,6},{3,7},{4,0},{5,1},{6,2},{7,3},{8,12},{9,13},{10,... | collective-permute-start | bytes 786440 | tf_op jit(solution)/shard_map/hidden_far/ppermute | solution.py:17
  46.9 1.5 %collective-permute-start.14 = (bf16[3,3,128,128]{3,2,1,0:T(8,128)(2,1)S(1)}, bf16[3,3,128,128]{3,2,1,0:T(8,128)(2,1)S(1)}, u32[]{:S(2)}, u32[]{:S(2)}) collective-permute-start(bf16[3,3,128,128]{3,2,1,0:T(8,128)(2,1)S(1)} %slice.51), channel_id=1, source_target_pairs={{0,8},{8,0},{16,24},{24,16},{1,9},{9,1},{17,25},{25,17},{2,10},{10... | collective-permute-start | bytes 884744 | tf_op jit(solution)/shard_map/two_high/ppermute | solution.py:17
  48.9 6.0 %back_near.1 = (bf16[4,1024,128]{2,1,0:T(8,128)(2,1)}, bf16[4,1024,128]{2,1,0:T(8,128)(2,1)}) custom-call(s32[2]{0:T(128)} %pad_add_fusion.place, bf16[1024,128]{1,0:T(8,128)(2,1)} %bitcast.49, bf16[3,3,256,128]{3,2,1,0:T(8,128)(2,1)} %refs_5_.1, bf16[3,3,256,128]{3,2,1,0:T(8,128)(2,1)} %copy-done.25, bf16[3,3,256,128]{3,2,1,0:T(8,128)(2,1)} %copy-done.24), custom_call_target="tpu_custom_call" | custom-call | flops 1811939328 | bytes 6291456 | tf_op jit(solution)/shard_map/back_near/pallas_call | solution.py:303
  55.2 1.6 %collective-permute-done.16.refs_1_ = bf16[1024,128]{1,0:T(8,128)(2,1)S(1)} collective-permute-done((bf16[1024,128]{1,0:T(8,128)(2,1)}, bf16[1024,128]{1,0:T(8,128)(2,1)S(1)}, u32[]{:S(2)}, u32[]{:S(2)}) %collective-permute-start.16) | collective-permute-done | bytes 262176 | tf_op jit(solution)/shard_map/hidden_near/ppermute | solution.py:17
  56.7 2.6 %collective-permute-done.15.refs_2_ = bf16[1024,128]{1,0:T(8,128)(2,1)S(1)} collective-permute-done((bf16[1024,128]{1,0:T(8,128)(2,1)}, bf16[1024,128]{1,0:T(8,128)(2,1)S(1)}, u32[]{:S(2)}, u32[]{:S(2)}) %collective-permute-start.15) | collective-permute-done | bytes 262176 | tf_op jit(solution)/shard_map/hidden_far/ppermute | solution.py:17
  59.5 0.6 copy-done.6
  60.2 3.7 %back_far.1 = (bf16[4,1024,128]{2,1,0:T(8,128)(2,1)}, bf16[4,1024,128]{2,1,0:T(8,128)(2,1)}) custom-call(s32[2]{0:T(128)} %pad_add_fusion.place, bf16[1024,128]{1,0:T(8,128)(2,1)} %bitcast.50, bf16[3,3,128,128]{3,2,1,0:T(8,128)(2,1)} %copy-done.7, bf16[3,3,128,128]{3,2,1,0:T(8,128)(2,1)} %copy-done.6, ...), custom_call_target="tpu_custom_call", output_to_operand_aliasing={{0}: (4, {}), {1}: (5, {})} | custom-call | flops 603979776 | bytes 2097152 | tf_op jit(solution)/shard_map/back_far/pallas_call | solution.py:334
  63.9 1.9 %collective-permute-done.17.refs_3_ = bf16[1024,128]{1,0:T(8,128)(2,1)S(1)} collective-permute-done((bf16[1024,128]{1,0:T(8,128)(2,1)S(1)}, bf16[1024,128]{1,0:T(8,128)(2,1)S(1)}, u32[]{:S(2)}, u32[]{:S(2)}) %collective-permute-start.17) | collective-permute-done | bytes 262176 | tf_op jit(solution)/shard_map/hidden_last/ppermute | solution.py:17
  66.0 0.6 collective-permute-start.20
  66.5 2.2 %collective-permute-done.18 = bf16[4,1024,128]{2,1,0:T(8,128)(2,1)S(1)} collective-permute-done((bf16[4,1024,128]{2,1,0:T(8,128)(2,1)}, bf16[4,1024,128]{2,1,0:T(8,128)(2,1)S(1)}, u32[]{:S(2)}, u32[]{:S(2)}) %collective-permute-start.18) | collective-permute-done | bytes 1048608 | tf_op jit(solution)/shard_map/back_core/ppermute | solution.py:17
  68.8 1.2 collective-permute-start.19
  71.1 2.4 %collective-permute-start.23 = (bf16[1024,128]{1,0:T(8,128)(2,1)S(1)}, bf16[1024,128]{1,0:T(8,128)(2,1)S(1)}, u32[]{:S(2)}, u32[]{:S(2)}) collective-permute-start(bf16[1024,128]{1,0:T(8,128)(2,1)S(1)} %get-tuple-element.100), channel_id=1, source_target_pairs={{0,24},{8,16},{16,8},{24,0},{1,25},{9,17},{17,9},{25,1},{2,26},{10... | collective-permute-start | bytes 786440 | tf_op jit(solution)/shard_map/input3/ppermute | solution.py:17
  73.5 1.0 copy-done.28
  74.5 6.5 %crop_grads.1 = (bf16[2,3,3,128,128]{4,3,2,1,0:T(8,128)(2,1)}, bf16[2,3,3,128,128]{4,3,2,1,0:T(8,128)(2,1)}, bf16[3,3,128,128]{3,2,1,0:T(8,128)(2,1)}, bf16[3,3,...) custom-call(s32[2]{0:T(128)} %pad_add_fusion.place, bf16[1024,128]{1,0:T(8,128)(2,1)} %bitcast.51, ...), custom_call_target="tpu_custom_call" | custom-call | flops 2415919104 | bytes 8388608 | tf_op jit(solution)/shard_map/crop_grads/pallas_call | solution.py:379
  81.2 2.8 %collective-permute-done.22.refs_1_ = bf16[1024,128]{1,0:T(8,128)(2,1)S(1)} collective-permute-done((bf16[1024,128]{1,0:T(8,128)(2,1)S(1)}, bf16[1024,128]{1,0:T(8,128)(2,1)S(1)}, u32[]{:S(2)}, u32[]{:S(2)}) %collective-permute-start.22) | collective-permute-done | bytes 262176 | tf_op jit(solution)/shard_map/input2/ppermute | solution.py:17
  84.1 0.6 copy-done.22
  84.7 1.5 %collective-permute-start.30 = (bf16[2,3,3,128,128]{4,3,2,1,0:T(8,128)(2,1)}, bf16[2,3,3,128,128]{4,3,2,1,0:T(8,128)(2,1)S(1)}, u32[]{:S(2)}, u32[]{:S(2)}) collective-permute-start(bf16[2,3,3,128,128]{4,3,2,1,0:T(8,128)(2,1)} %get-tuple-element.117), channel_id=1, source_target_pairs={{0,8},{8,0},{16,24},{24,16},{1,9},{9,1},{17,25},{25,17},{2,10},{10... | collective-permute-start | bytes 1769480 | tf_op jit(solution)/shard_map/grad_x/ppermute | solution.py:17
  86.7 1.6 %collective-permute-start.24 = (bf16[1024,128]{1,0:T(8,128)(2,1)S(1)}, bf16[1024,128]{1,0:T(8,128)(2,1)S(1)}, u32[]{:S(2)}, u32[]{:S(2)}) collective-permute-start(bf16[1024,128]{1,0:T(8,128)(2,1)S(1)} %fusion.6), channel_id=1, source_target_pairs={{0,4},{1,5},{2,6},{3,7},{4,0},{5,1},{6,2},{7,3},{8,12},{9,13},{10,... | collective-permute-start | bytes 786440 | tf_op jit(solution)/shard_map/distant/ppermute | solution.py:17
  88.3 0.7 collective-permute-start.25
  89.0 7.3 %conv_two.1 = bf16[1024,128]{1,0:T(8,128)(2,1)} custom-call(s32[2]{0:T(128)} %pad_add_fusion.place, bf16[1024,128]{1,0:T(8,128)(2,1)} %get-tuple-element.75.refs_0_, bf16[1024,128]{1,0:T(8,128)(2,1)} %copy-done.18, bf16[1024,128]{1,0:T(8,128)(2,1)} %copy-done.19, bf16[1024,128]{1,0:T(8,128)(2,1)} %copy-done.23, bf16[4,1024,128]{2,1,0:T(8,128)(2,1)} %copy-done.28, ...), custom_call_target="tpu_custom_call" | custom-call | flops 2415919104 | bytes 8388608 | tf_op jit(solution)/shard_map/conv_two/pallas_call | solution.py:258
  96.4 5.0 %collective-permute-done.24 = bf16[1024,128]{1,0:T(8,128)(2,1)S(1)} collective-permute-done((bf16[1024,128]{1,0:T(8,128)(2,1)S(1)}, bf16[1024,128]{1,0:T(8,128)(2,1)S(1)}, u32[]{:S(2)}, u32[]{:S(2)}) %collective-permute-start.24) | collective-permute-done | bytes 262176 | tf_op jit(solution)/shard_map/distant/ppermute | solution.py:17
  101.7 1.6 %collective-permute-start.29 = (bf16[1024,128]{1,0:T(8,128)(2,1)S(1)}, bf16[1024,128]{1,0:T(8,128)(2,1)S(1)}, u32[]{:S(2)}, u32[]{:S(2)}) collective-permute-start(bf16[1024,128]{1,0:T(8,128)(2,1)S(1)} %fusion.5.refs_2_), channel_id=1, source_target_pairs={{0,24},{8,16},{16,8},{24,0},{1,25},{9,17},{17,9},{25,1},{2,26},{10... | collective-permute-start | bytes 786440 | tf_op jit(solution)/shard_map/pre3/ppermute | solution.py:17
  103.3 1.2 collective-permute-start.28
  104.5 0.8 collective-permute-start.27
  105.4 1.3 collective-permute-start.33
  106.8 0.9 collective-permute-start.32
  107.7 3.7 %grad_one_own.1.refs_7_ = f32[3,3,256,128]{3,2,1,0:T(8,128)} custom-call(s32[2]{0:T(128)} %pad_add_fusion.place, bf16[1024,128]{1,0:T(8,128)(2,1)} %copy-done.1, bf16[4,1024,128]{2,1,0:T(8,128)(2,1)} %copy-done.4, bf16[1024,128]{1,0:T(8,128)(2,1)} %copy-done.3), custom_call_target="tpu_custom_call" | custom-call | flops 603979776 | bytes 2097152 | tf_op jit(solution)/shard_map/grad_one_own/pallas_call | solution.py:418
  111.4 0.6 collective-permute-done.29.refs_6_
  112.0 4.3 %collective-permute-done.28.refs_5_ = bf16[1024,128]{1,0:T(8,128)(2,1)S(1)} collective-permute-done((bf16[1024,128]{1,0:T(8,128)(2,1)S(1)}, bf16[1024,128]{1,0:T(8,128)(2,1)S(1)}, u32[]{:S(2)}, u32[]{:S(2)}) %collective-permute-start.28) | collective-permute-done | bytes 262176 | tf_op jit(solution)/shard_map/pre2/ppermute | solution.py:17
  116.3 1.3 %collective-permute-done.27.refs_4_ = bf16[1024,128]{1,0:T(8,128)(2,1)S(1)} collective-permute-done((bf16[1024,128]{1,0:T(8,128)(2,1)S(1)}, bf16[1024,128]{1,0:T(8,128)(2,1)S(1)}, u32[]{:S(2)}, u32[]{:S(2)}) %collective-permute-start.27) | collective-permute-done | bytes 262176 | tf_op jit(solution)/shard_map/pre1/ppermute | solution.py:17
  117.6 0.7 copy-done.35
  118.3 6.3 %grad_one.1 = f32[3,3,256,128]{3,2,1,0:T(8,128)} custom-call(s32[2]{0:T(128)} %pad_add_fusion.place, bf16[1024,128]{1,0:T(8,128)(2,1)} %copy-done.20, bf16[1024,128]{1,0:T(8,128)(2,1)} %copy-done.21, bf16[1024,128]{1,0:T(8,128)(2,1)} %copy-done.22, bf16[4,1024,128]{2,1,0:T(8,128)(2,1)} %copy-done.4, bf16[1024,128]{1,0:T(8,128)(2,1)} %copy-done.35, ...), custom_call_target="tpu_custom_call" | custom-call | flops 1811939328 | bytes 6291456 | tf_op jit(solution)/shard_map/grad_one/pallas_call | solution.py:418
  124.8 1.1 copy-done.2
  125.9 1.1 maximum_add_fusion
  (115 shorter events, 4.9 us)
Async XLA Ops:
  0.6 20.3 %collective-permute-start.2 = (bf16[3,3,256,128]{3,2,1,0:T(8,128)(2,1)}, bf16[3,3,256,128]{3,2,1,0:T(8,128)(2,1)S(1)}, u32[]{:S(2)}, u32[]{:S(2)}) collective-permute-start(bf16[3,3,256,128]{3,2,1,0:T(8,128)(2,1)} %refs_8_.1), channel_id=1, source_target_pairs={{0,8},{8,0},{16,24},{24,16},{1,9},{9,1},{17,25},{25,17},{2,10},{10... | collective-permute-start | bytes 1769480 | tf_op jit(solution)/shard_map/one_x/ppermute | solution.py:17
  3.6 17.3 %collective-permute-start.3 = (bf16[3,3,256,128]{3,2,1,0:T(8,128)(2,1)}, bf16[3,3,256,128]{3,2,1,0:T(8,128)(2,1)S(1)}, u32[]{:S(2)}, u32[]{:S(2)}) collective-permute-start(bf16[3,3,256,128]{3,2,1,0:T(8,128)(2,1)} %refs_8_.1), channel_id=1, source_target_pairs={{0,16},{8,24},{16,0},{24,8},{1,17},{9,25},{17,1},{25,9},{2,18},{10... | collective-permute-start | bytes 1769480 | tf_op jit(solution)/shard_map/one_y/ppermute | solution.py:17
  5.2 4.7 %collective-permute-start.4 = (bf16[1024,128]{1,0:T(8,128)(2,1)}, bf16[1024,128]{1,0:T(8,128)(2,1)S(1)}, u32[]{:S(2)}, u32[]{:S(2)}) collective-permute-start(bf16[1024,128]{1,0:T(8,128)(2,1)} %bitcast.44), channel_id=1, source_target_pairs={{0,1},{1,0},{2,3},{3,2},{4,5},{5,4},{6,7},{7,6},{8,9},{9,8},{10,11... | collective-permute-start | bytes 786440 | tf_op jit(solution)/shard_map/field_core0/ppermute | solution.py:17
  5.2 15.6 %collective-permute-start.1 = (bf16[1024,128]{1,0:T(8,128)(2,1)}, bf16[1024,128]{1,0:T(8,128)(2,1)S(1)}, u32[]{:S(2)}, u32[]{:S(2)}) collective-permute-start(bf16[1024,128]{1,0:T(8,128)(2,1)} %bitcast.45), channel_id=1, source_target_pairs={{0,4},{1,5},{2,6},{3,7},{4,0},{5,1},{6,2},{7,3},{8,12},{9,13},{10,... | collective-permute-start | bytes 786440 | tf_op jit(solution)/shard_map/field_far/ppermute | solution.py:17
  7.7 13.2 %collective-permute-start = (bf16[1024,128]{1,0:T(8,128)(2,1)}, bf16[1024,128]{1,0:T(8,128)(2,1)S(1)}, u32[]{:S(2)}, u32[]{:S(2)}) collective-permute-start(bf16[1024,128]{1,0:T(8,128)(2,1)} %bitcast.46), channel_id=1, source_target_pairs={{0,2},{1,3},{2,0},{3,1},{4,6},{5,7},{6,4},{7,5},{8,10},{9,11},{10,... | collective-permute-start | bytes 786440 | tf_op jit(solution)/shard_map/field_near/ppermute | solution.py:17
  9.9 20.9 %copy-start.30 = (bf16[1024,128]{1,0:T(8,128)(2,1)}, bf16[1024,128]{1,0:T(8,128)(2,1)S(1)}, u32[]{:S(2)}) copy-start(bf16[1024,128]{1,0:T(8,128)(2,1)S(1)} %collective-permute-done.4.refs_4_) | copy-start | bytes 786436
  20.7 14.9 %copy-start.11 = (bf16[1024,128]{1,0:T(8,128)(2,1)}, bf16[1024,128]{1,0:T(8,128)(2,1)S(1)}, u32[]{:S(2)}) copy-start(bf16[1024,128]{1,0:T(8,128)(2,1)S(1)} %collective-permute-done.1.refs_2_) | copy-start | bytes 786436
  20.9 14.7 %copy-start.13 = (bf16[1024,128]{1,0:T(8,128)(2,1)}, bf16[1024,128]{1,0:T(8,128)(2,1)S(1)}, u32[]{:S(2)}) copy-start(bf16[1024,128]{1,0:T(8,128)(2,1)S(1)} %collective-permute-done.refs_1_) | copy-start | bytes 786436
  20.9 14.7 %copy-start.26 = (bf16[3,3,256,128]{3,2,1,0:T(8,128)(2,1)}, bf16[3,3,256,128]{3,2,1,0:T(8,128)(2,1)S(1)}, u32[]{:S(2)}) copy-start(bf16[3,3,256,128]{3,2,1,0:T(8,128)(2,1)S(1)} %collective-permute-done.2.refs_9_) | copy-start | bytes 1769476
  20.9 14.7 %copy-start.27 = (bf16[3,3,256,128]{3,2,1,0:T(8,128)(2,1)}, bf16[3,3,256,128]{3,2,1,0:T(8,128)(2,1)S(1)}, u32[]{:S(2)}) copy-start(bf16[3,3,256,128]{3,2,1,0:T(8,128)(2,1)S(1)} %collective-permute-done.3.refs_10_) | copy-start | bytes 1769476
  21.0 9.8 %collective-permute-start.9 = (bf16[3,3,128,128]{3,2,1,0:T(8,128)(2,1)S(1)}, bf16[3,3,128,128]{3,2,1,0:T(8,128)(2,1)S(1)}, u32[]{:S(2)}, u32[]{:S(2)}) collective-permute-start(bf16[3,3,128,128]{3,2,1,0:T(8,128)(2,1)S(1)} %slice.49), channel_id=1, source_target_pairs={{0,8},{8,0},{16,24},{24,16},{1,9},{9,1},{17,25},{25,17},{2,10},{10... | collective-permute-start | bytes 884744 | tf_op jit(solution)/shard_map/one_high/ppermute | solution.py:17
  21.6 9.2 %collective-permute-start.8 = (bf16[3,3,128,128]{3,2,1,0:T(8,128)(2,1)S(1)}, bf16[3,3,128,128]{3,2,1,0:T(8,128)(2,1)}, u32[]{:S(2)}, u32[]{:S(2)}) collective-permute-start(bf16[3,3,128,128]{3,2,1,0:T(8,128)(2,1)S(1)} %slice.48), channel_id=1, source_target_pairs={{0,16},{8,24},{16,0},{24,8},{1,17},{9,25},{17,1},{25,9},{2,18},{10... | collective-permute-start | bytes 884744 | tf_op jit(solution)/shard_map/one_low/ppermute | solution.py:17
  22.0 2.0 %collective-permute-start.6 = (bf16[1024,128]{1,0:T(8,128)(2,1)S(1)}, bf16[1024,128]{1,0:T(8,128)(2,1)S(1)}, u32[]{:S(2)}, u32[]{:S(2)}) collective-permute-start(bf16[1024,128]{1,0:T(8,128)(2,1)S(1)} %collective-permute-done.refs_1_), channel_id=1, source_target_pairs={{0,1},{1,0},{2,3},{3,2},{4,5},{5,4},{6,7},{7,6},{8,9},{9,8},{10,11... | collective-permute-start | bytes 786440 | tf_op jit(solution)/shard_map/field_core1/ppermute | solution.py:17
  22.0 2.0 %collective-permute-start.7 = (bf16[1024,128]{1,0:T(8,128)(2,1)S(1)}, bf16[1024,128]{1,0:T(8,128)(2,1)S(1)}, u32[]{:S(2)}, u32[]{:S(2)}) collective-permute-start(bf16[1024,128]{1,0:T(8,128)(2,1)S(1)} %collective-permute-done.1.refs_2_), channel_id=1, source_target_pairs={{0,1},{1,0},{2,3},{3,2},{4,5},{5,4},{6,7},{7,6},{8,9},{9,8},{10,11... | collective-permute-start | bytes 786440 | tf_op jit(solution)/shard_map/field_core2/ppermute | solution.py:17
  22.5 8.2 %collective-permute-start.5 = (bf16[1024,128]{1,0:T(8,128)(2,1)S(1)}, bf16[1024,128]{1,0:T(8,128)(2,1)S(1)}, u32[]{:S(2)}, u32[]{:S(2)}) collective-permute-start(bf16[1024,128]{1,0:T(8,128)(2,1)S(1)} %collective-permute-done.1.refs_2_), channel_id=1, source_target_pairs={{0,2},{1,3},{2,0},{3,1},{4,6},{5,7},{6,4},{7,5},{8,10},{9,11},{10,... | collective-permute-start | bytes 786440 | tf_op jit(solution)/shard_map/field_last/ppermute | solution.py:17
  24.0 6.8 %copy-start.31 = (bf16[1024,128]{1,0:T(8,128)(2,1)}, bf16[1024,128]{1,0:T(8,128)(2,1)S(1)}, u32[]{:S(2)}) copy-start(bf16[1024,128]{1,0:T(8,128)(2,1)S(1)} %collective-permute-done.6.refs_5_) | copy-start | bytes 786436
  24.0 6.7 %copy-start.32 = (bf16[1024,128]{1,0:T(8,128)(2,1)}, bf16[1024,128]{1,0:T(8,128)(2,1)S(1)}, u32[]{:S(2)}) copy-start(bf16[1024,128]{1,0:T(8,128)(2,1)S(1)} %collective-permute-done.7.refs_6_) | copy-start | bytes 786436
  30.8 16.0 %collective-permute-start.11 = (bf16[3,3,256,128]{3,2,1,0:T(8,128)(2,1)}, bf16[3,3,256,128]{3,2,1,0:T(8,128)(2,1)S(1)}, u32[]{:S(2)}, u32[]{:S(2)}) collective-permute-start(bf16[3,3,256,128]{3,2,1,0:T(8,128)(2,1)} %refs_5_.1), channel_id=1, source_target_pairs={{0,16},{8,24},{16,0},{24,8},{1,17},{9,25},{17,1},{25,9},{2,18},{10... | collective-permute-start | bytes 1769480 | tf_op jit(solution)/shard_map/two_y/ppermute | solution.py:17
  32.5 14.4 %collective-permute-start.10 = (bf16[3,3,256,128]{3,2,1,0:T(8,128)(2,1)}, bf16[3,3,256,128]{3,2,1,0:T(8,128)(2,1)S(1)}, u32[]{:S(2)}, u32[]{:S(2)}) collective-permute-start(bf16[3,3,256,128]{3,2,1,0:T(8,128)(2,1)} %refs_5_.1), channel_id=1, source_target_pairs={{0,8},{8,0},{16,24},{24,16},{1,9},{9,1},{17,25},{25,17},{2,10},{10... | collective-permute-start | bytes 1769480 | tf_op jit(solution)/shard_map/two_x/ppermute | solution.py:17
  33.9 1.7 %collective-permute-start.12 = (bf16[1024,128]{1,0:T(8,128)(2,1)S(1)}, bf16[1024,128]{1,0:T(8,128)(2,1)}, u32[]{:S(2)}, u32[]{:S(2)}) collective-permute-start(bf16[1024,128]{1,0:T(8,128)(2,1)S(1)} %collective-permute-done.5.refs_3_), channel_id=1, source_target_pairs={{0,1},{1,0},{2,3},{3,2},{4,5},{5,4},{6,7},{7,6},{8,9},{9,8},{10,11... | collective-permute-start | bytes 786440 | tf_op jit(solution)/shard_map/field_core3/ppermute | solution.py:17
  43.0 13.7 %collective-permute-start.16 = (bf16[1024,128]{1,0:T(8,128)(2,1)}, bf16[1024,128]{1,0:T(8,128)(2,1)S(1)}, u32[]{:S(2)}, u32[]{:S(2)}) collective-permute-start(bf16[1024,128]{1,0:T(8,128)(2,1)} %get-tuple-element.75.refs_0_), channel_id=1, source_target_pairs={{0,2},{1,3},{2,0},{3,1},{4,6},{5,7},{6,4},{7,5},{8,10},{9,11},{10,... | collective-permute-start | bytes 786440 | tf_op jit(solution)/shard_map/hidden_near/ppermute | solution.py:17
  44.5 14.8 %collective-permute-start.15 = (bf16[1024,128]{1,0:T(8,128)(2,1)}, bf16[1024,128]{1,0:T(8,128)(2,1)S(1)}, u32[]{:S(2)}, u32[]{:S(2)}) collective-permute-start(bf16[1024,128]{1,0:T(8,128)(2,1)} %get-tuple-element.75.refs_0_), channel_id=1, source_target_pairs={{0,4},{1,5},{2,6},{3,7},{4,0},{5,1},{6,2},{7,3},{8,12},{9,13},{10,... | collective-permute-start | bytes 786440 | tf_op jit(solution)/shard_map/hidden_far/ppermute | solution.py:17
  46.9 12.4 %collective-permute-start.14 = (bf16[3,3,128,128]{3,2,1,0:T(8,128)(2,1)S(1)}, bf16[3,3,128,128]{3,2,1,0:T(8,128)(2,1)S(1)}, u32[]{:S(2)}, u32[]{:S(2)}) collective-permute-start(bf16[3,3,128,128]{3,2,1,0:T(8,128)(2,1)S(1)} %slice.51), channel_id=1, source_target_pairs={{0,8},{8,0},{16,24},{24,16},{1,9},{9,1},{17,25},{25,17},{2,10},{10... | collective-permute-start | bytes 884744 | tf_op jit(solution)/shard_map/two_high/ppermute | solution.py:17
  48.4 11.0 %collective-permute-start.13 = (bf16[3,3,128,128]{3,2,1,0:T(8,128)(2,1)S(1)}, bf16[3,3,128,128]{3,2,1,0:T(8,128)(2,1)S(1)}, u32[]{:S(2)}, u32[]{:S(2)}) collective-permute-start(bf16[3,3,128,128]{3,2,1,0:T(8,128)(2,1)S(1)} %slice.50), channel_id=1, source_target_pairs={{0,16},{8,24},{16,0},{24,8},{1,17},{9,25},{17,1},{25,9},{2,18},{10... | collective-permute-start | bytes 884744 | tf_op jit(solution)/shard_map/two_low/ppermute | solution.py:17
  55.1 28.8 %copy-start.1 = (bf16[1024,128]{1,0:T(8,128)(2,1)}, bf16[1024,128]{1,0:T(8,128)(2,1)S(1)}, u32[]{:S(2)}) copy-start(bf16[1024,128]{1,0:T(8,128)(2,1)S(1)} %get-tuple-element.103.refs_0_) | copy-start | bytes 786436
  56.7 16.8 %copy-start.18 = (bf16[1024,128]{1,0:T(8,128)(2,1)}, bf16[1024,128]{1,0:T(8,128)(2,1)S(1)}, u32[]{:S(2)}) copy-start(bf16[1024,128]{1,0:T(8,128)(2,1)S(1)} %collective-permute-done.16.refs_1_) | copy-start | bytes 786436
  59.3 14.2 %copy-start.19 = (bf16[1024,128]{1,0:T(8,128)(2,1)}, bf16[1024,128]{1,0:T(8,128)(2,1)S(1)}, u32[]{:S(2)}) copy-start(bf16[1024,128]{1,0:T(8,128)(2,1)S(1)} %collective-permute-done.15.refs_2_) | copy-start | bytes 786436
  59.4 6.4 %collective-permute-start.17 = (bf16[1024,128]{1,0:T(8,128)(2,1)S(1)}, bf16[1024,128]{1,0:T(8,128)(2,1)S(1)}, u32[]{:S(2)}, u32[]{:S(2)}) collective-permute-start(bf16[1024,128]{1,0:T(8,128)(2,1)S(1)} %collective-permute-done.15.refs_2_), channel_id=1, source_target_pairs={{0,2},{1,3},{2,0},{3,1},{4,6},{5,7},{6,4},{7,5},{8,10},{9,11},{10,... | collective-permute-start | bytes 786440 | tf_op jit(solution)/shard_map/hidden_last/ppermute | solution.py:17
  65.8 2.9 %collective-permute-start.18 = (bf16[4,1024,128]{2,1,0:T(8,128)(2,1)}, bf16[4,1024,128]{2,1,0:T(8,128)(2,1)S(1)}, u32[]{:S(2)}, u32[]{:S(2)}) collective-permute-start(bf16[4,1024,128]{2,1,0:T(8,128)(2,1)} %get-tuple-element.92), channel_id=1, source_target_pairs={{0,1},{1,0},{2,3},{3,2},{4,5},{5,4},{6,7},{7,6},{8,9},{9,8},{10,11... | collective-permute-start | bytes 3145736 | tf_op jit(solution)/shard_map/back_core/ppermute | solution.py:17
  66.0 7.6 %collective-permute-start.20 = (bf16[4,1024,128]{2,1,0:T(8,128)(2,1)S(1)}, bf16[4,1024,128]{2,1,0:T(8,128)(2,1)S(1)}, u32[]{:S(2)}, u32[]{:S(2)}) collective-permute-start(bf16[4,1024,128]{2,1,0:T(8,128)(2,1)S(1)} %pad_maximum_fusion), channel_id=1, source_target_pairs={{0,1},{1,0},{2,3},{3,2},{4,5},{5,4},{6,7},{7,6},{8,9},{9,8},{10,11... | collective-permute-start | bytes 3145736 | tf_op jit(solution)/shard_map/hidden_core/ppermute | solution.py:17
  68.8 12.2 %collective-permute-start.19 = (bf16[1024,128]{1,0:T(8,128)(2,1)S(1)}, bf16[1024,128]{1,0:T(8,128)(2,1)S(1)}, u32[]{:S(2)}, u32[]{:S(2)}) collective-permute-start(bf16[1024,128]{1,0:T(8,128)(2,1)S(1)} %get-tuple-element.123), channel_id=1, source_target_pairs={{0,2},{1,3},{2,0},{3,1},{4,6},{5,7},{6,4},{7,5},{8,10},{9,11},{10,... | collective-permute-start | bytes 786440 | tf_op jit(solution)/shard_map/relayed/ppermute | solution.py:17
  70.0 11.1 %collective-permute-start.21 = (bf16[1024,128]{1,0:T(8,128)(2,1)S(1)}, bf16[1024,128]{1,0:T(8,128)(2,1)S(1)}, u32[]{:S(2)}, u32[]{:S(2)}) collective-permute-start(bf16[1024,128]{1,0:T(8,128)(2,1)S(1)} %get-tuple-element.98), channel_id=1, source_target_pairs={{0,8},{8,0},{16,24},{24,16},{1,9},{9,1},{17,25},{25,17},{2,10},{10... | collective-permute-start | bytes 786440 | tf_op jit(solution)/shard_map/input1/ppermute | solution.py:17
  70.6 13.4 %collective-permute-start.22 = (bf16[1024,128]{1,0:T(8,128)(2,1)S(1)}, bf16[1024,128]{1,0:T(8,128)(2,1)S(1)}, u32[]{:S(2)}, u32[]{:S(2)}) collective-permute-start(bf16[1024,128]{1,0:T(8,128)(2,1)S(1)} %get-tuple-element.99), channel_id=1, source_target_pairs={{0,16},{8,24},{16,0},{24,8},{1,17},{9,25},{17,1},{25,9},{2,18},{10... | collective-permute-start | bytes 786440 | tf_op jit(solution)/shard_map/input2/ppermute | solution.py:17
  71.1 12.9 %collective-permute-start.23 = (bf16[1024,128]{1,0:T(8,128)(2,1)S(1)}, bf16[1024,128]{1,0:T(8,128)(2,1)S(1)}, u32[]{:S(2)}, u32[]{:S(2)}) collective-permute-start(bf16[1024,128]{1,0:T(8,128)(2,1)S(1)} %get-tuple-element.100), channel_id=1, source_target_pairs={{0,24},{8,16},{16,8},{24,0},{1,25},{9,17},{17,9},{25,1},{2,26},{10... | collective-permute-start | bytes 786440 | tf_op jit(solution)/shard_map/input3/ppermute | solution.py:17
  81.2 15.2 %copy-start.20 = (bf16[1024,128]{1,0:T(8,128)(2,1)}, bf16[1024,128]{1,0:T(8,128)(2,1)S(1)}, u32[]{:S(2)}) copy-start(bf16[1024,128]{1,0:T(8,128)(2,1)S(1)} %collective-permute-done.21.refs_0_) | copy-start | bytes 786436
  84.0 12.4 %copy-start.21 = (bf16[1024,128]{1,0:T(8,128)(2,1)}, bf16[1024,128]{1,0:T(8,128)(2,1)S(1)}, u32[]{:S(2)}) copy-start(bf16[1024,128]{1,0:T(8,128)(2,1)S(1)} %collective-permute-done.22.refs_1_) | copy-start | bytes 786436
  84.7 16.7 %copy-start.5 = (f32[1024,128]{1,0:T(8,128)S(1)}, f32[1024,128]{1,0:T(8,128)}, u32[]{:S(2)}) copy-start(f32[1024,128]{1,0:T(8,128)} %get-tuple-element.111) | copy-start | bytes 1572868
  84.7 16.7 %collective-permute-start.26 = (bf16[4,1024,128]{2,1,0:T(8,128)(2,1)S(1)}, bf16[4,1024,128]{2,1,0:T(8,128)(2,1)S(1)}, u32[]{:S(2)}, u32[]{:S(2)}) collective-permute-start(bf16[4,1024,128]{2,1,0:T(8,128)(2,1)S(1)} %pad_maximum_fusion.1), channel_id=1, source_target_pairs={{0,1},{1,0},{2,3},{3,2},{4,5},{5,4},{6,7},{7,6},{8,9},{9,8},{10,11... | collective-permute-start | bytes 3145736 | tf_op jit(solution)/shard_map/field_swap/ppermute | solution.py:17
  84.7 20.6 %collective-permute-start.30 = (bf16[2,3,3,128,128]{4,3,2,1,0:T(8,128)(2,1)}, bf16[2,3,3,128,128]{4,3,2,1,0:T(8,128)(2,1)S(1)}, u32[]{:S(2)}, u32[]{:S(2)}) collective-permute-start(bf16[2,3,3,128,128]{4,3,2,1,0:T(8,128)(2,1)} %get-tuple-element.117), channel_id=1, source_target_pairs={{0,8},{8,0},{16,24},{24,16},{1,9},{9,1},{17,25},{25,17},{2,10},{10... | collective-permute-start | bytes 1769480 | tf_op jit(solution)/shard_map/grad_x/ppermute | solution.py:17
  86.2 19.1 %collective-permute-start.31 = (bf16[2,3,3,128,128]{4,3,2,1,0:T(8,128)(2,1)}, bf16[2,3,3,128,128]{4,3,2,1,0:T(8,128)(2,1)S(1)}, u32[]{:S(2)}, u32[]{:S(2)}) collective-permute-start(bf16[2,3,3,128,128]{4,3,2,1,0:T(8,128)(2,1)} %get-tuple-element.118), channel_id=1, source_target_pairs={{0,16},{8,24},{16,0},{24,8},{1,17},{9,25},{17,1},{25,9},{2,18},{10... | collective-permute-start | bytes 1769480 | tf_op jit(solution)/shard_map/grad_y/ppermute | solution.py:17
  86.7 14.7 %collective-permute-start.24 = (bf16[1024,128]{1,0:T(8,128)(2,1)S(1)}, bf16[1024,128]{1,0:T(8,128)(2,1)S(1)}, u32[]{:S(2)}, u32[]{:S(2)}) collective-permute-start(bf16[1024,128]{1,0:T(8,128)(2,1)S(1)} %fusion.6), channel_id=1, source_target_pairs={{0,4},{1,5},{2,6},{3,7},{4,0},{5,1},{6,2},{7,3},{8,12},{9,13},{10,... | collective-permute-start | bytes 786440 | tf_op jit(solution)/shard_map/distant/ppermute | solution.py:17
  88.3 13.1 %collective-permute-start.25 = (bf16[1024,128]{1,0:T(8,128)(2,1)S(1)}, bf16[1024,128]{1,0:T(8,128)(2,1)S(1)}, u32[]{:S(2)}, u32[]{:S(2)}) collective-permute-start(bf16[1024,128]{1,0:T(8,128)(2,1)S(1)} %get-tuple-element.102), channel_id=1, source_target_pairs={{0,2},{1,3},{2,0},{3,1},{4,6},{5,7},{6,4},{7,5},{8,10},{9,11},{10,... | collective-permute-start | bytes 786440 | tf_op jit(solution)/shard_map/nearby/ppermute | solution.py:17
  96.4 8.9 %copy-start.9 = (bf16[3,3,128,128]{3,2,1,0:T(8,128)(2,1)S(1)}, bf16[3,3,128,128]{3,2,1,0:T(8,128)(2,1)}, u32[]{:S(2)}) copy-start(bf16[3,3,128,128]{3,2,1,0:T(8,128)(2,1)} %get-tuple-element.122) | copy-start | bytes 884740
  101.7 10.2 %collective-permute-start.29 = (bf16[1024,128]{1,0:T(8,128)(2,1)S(1)}, bf16[1024,128]{1,0:T(8,128)(2,1)S(1)}, u32[]{:S(2)}, u32[]{:S(2)}) collective-permute-start(bf16[1024,128]{1,0:T(8,128)(2,1)S(1)} %fusion.5.refs_2_), channel_id=1, source_target_pairs={{0,24},{8,16},{16,8},{24,0},{1,25},{9,17},{17,9},{25,1},{2,26},{10... | collective-permute-start | bytes 786440 | tf_op jit(solution)/shard_map/pre3/ppermute | solution.py:17
  103.3 13.0 %collective-permute-start.28 = (bf16[1024,128]{1,0:T(8,128)(2,1)S(1)}, bf16[1024,128]{1,0:T(8,128)(2,1)S(1)}, u32[]{:S(2)}, u32[]{:S(2)}) collective-permute-start(bf16[1024,128]{1,0:T(8,128)(2,1)S(1)} %fusion.5.refs_2_), channel_id=1, source_target_pairs={{0,16},{8,24},{16,0},{24,8},{1,17},{9,25},{17,1},{25,9},{2,18},{10... | collective-permute-start | bytes 786440 | tf_op jit(solution)/shard_map/pre2/ppermute | solution.py:17
  104.5 13.1 %collective-permute-start.27 = (bf16[1024,128]{1,0:T(8,128)(2,1)S(1)}, bf16[1024,128]{1,0:T(8,128)(2,1)S(1)}, u32[]{:S(2)}, u32[]{:S(2)}) collective-permute-start(bf16[1024,128]{1,0:T(8,128)(2,1)S(1)} %fusion.5.refs_2_), channel_id=1, source_target_pairs={{0,8},{8,0},{16,24},{24,16},{1,9},{9,1},{17,25},{25,17},{2,10},{10... | collective-permute-start | bytes 786440 | tf_op jit(solution)/shard_map/pre1/ppermute | solution.py:17
  105.4 19.2 %collective-permute-start.33 = (bf16[3,3,128,128]{3,2,1,0:T(8,128)(2,1)S(1)}, bf16[3,3,128,128]{3,2,1,0:T(8,128)(2,1)S(1)}, u32[]{:S(2)}, u32[]{:S(2)}) collective-permute-start(bf16[3,3,128,128]{3,2,1,0:T(8,128)(2,1)S(1)} %fusion), channel_id=1, source_target_pairs={{0,8},{8,0},{16,24},{24,16},{1,9},{9,1},{17,25},{25,17},{2,10},{10... | collective-permute-start | bytes 884744 | tf_op jit(solution)/shard_map/grad_high/ppermute | solution.py:17
  106.8 17.9 %collective-permute-start.32 = (bf16[3,3,128,128]{3,2,1,0:T(8,128)(2,1)S(1)}, bf16[3,3,128,128]{3,2,1,0:T(8,128)(2,1)S(1)}, u32[]{:S(2)}, u32[]{:S(2)}) collective-permute-start(bf16[3,3,128,128]{3,2,1,0:T(8,128)(2,1)S(1)} %fusion.1), channel_id=1, source_target_pairs={{0,16},{8,24},{16,0},{24,8},{1,17},{9,25},{17,1},{25,9},{2,18},{10... | collective-permute-start | bytes 884744 | tf_op jit(solution)/shard_map/grad_low/ppermute | solution.py:17
  (22 other events, 79.8 us)

commit v6 on v5

--- a/solution.py
+++ b/solution.py
@@ -156,7 +156,7 @@
 TAPS = range(3)
 
 
-def kernel_call(kernel, out_shape, in_specs, scratch, share, out_specs=None, aliases=None):
+def kernel_call(kernel, out_shape, in_specs, scratch, share, out_specs=None, aliases=None, limit=56):
     return pl.pallas_call(
         kernel,
         out_shape=out_shape,
@@ -164,7 +164,7 @@
         out_specs=out_specs or [VMEM] * len(out_shape),
         scratch_shapes=scratch,
         input_output_aliases=aliases or {},
-        compiler_params=pltpu.CompilerParams(vmem_limit_bytes=56 * 2**20),
+        compiler_params=pltpu.CompilerParams(vmem_limit_bytes=limit * 2**20),
         cost_estimate=pl.CostEstimate(
             flops=int(share * 2 * 9 * CELLS * CELLS * WIDE), bytes_accessed=int(share * 2**23), transcendentals=0
         ),
@@ -426,6 +426,7 @@
             pltpu.SemaphoreType.DMA((3 * count,)),
         ],
         count / 4,
+        limit=20,
     )(place, *mine, other, *grads, *([] if before is None else [before]))[0]
 
 

time: 127 us -> 125 us (0.984)
  Pallas kernels: 41 us -> 37.3 us
  waiting for transfers between devices: 41.6 us -> 43.9 us
    pallas_call x2, Pallas kernels: 10 us -> 6.37 us  [weight_grads(): kernel_call(functools.partial(grad_kernel, slots, adds), [f32(3, 3, TALL,...]
    ppermute x34, waiting for transfers between devices: 41.6 us -> 43.9 us  [swap(): return lax.ppermute(values, axis, [(i, i ^ flip) for i in range(size)])]
    unnamed x72 -> x56, local copies, waits for them, and re-layouts: 4.19 us -> 3.45 us
  transfers between devices with their start and end apart: 34 -> 34, of which waited for: 13 -> 14; matrix products, arithmetic and copies ran while one was open for 1% -> 1% of each run, Pallas kernels for 32% -> 30%
where the time goes in v6:
time: 125 us
  waiting for transfers between devices  43.9 us (35%)
  Pallas kernels  37.3 us (30%)
  starting transfers between devices  36.2 us (29%)
  local copies, waits for them, and re-layouts  3.53 us (3%)
  other arithmetic  2.97 us (2%)
    ppermute x34, waiting for transfers between devices, swap(): return lax.ppermute(values, axis, [(i, i ^ flip) for i in range(size)])  43.9 us
    ppermute x34, starting transfers between devices, swap(): return lax.ppermute(values, axis, [(i, i ^ flip) for i in range(size)])  36.2 us
    pallas_call x2, Pallas kernels, conv(): kernel_call(functools.partial(conv_kernel, layer, len(fields)), ([f32(CEL...  14.7 us
    pallas_call x1, Pallas kernels, crop_grads(): kernel_call(functools.partial(crop_grad_kernel, len(fields)), [bf16(2, 3,...  6.49 us
    pallas_call x2, Pallas kernels, weight_grads(): kernel_call(functools.partial(grad_kernel, slots, adds), [f32(3, 3, TALL,...  6.37 us
    pallas_call x1, Pallas kernels, back_near(): kernel_call(back_near_kernel, [bf16(4, CELLS, WIDE)] * 2, [SMEM, VMEM] +...  6.04 us
    pallas_call x1, Pallas kernels, back_far(): kernel_call(back_far_kernel, [bf16(4, CELLS, WIDE)] * 2, [SMEM, VMEM] + [...  3.71 us
    unnamed x56, local copies, waits for them, and re-layouts  3.45 us
  transfers between devices with their start and end apart: 34, of which 14 were waited for; matrix products, arithmetic and copies ran while one was open for 1% of the time, Pallas kernels for 30%

profile of v6, /device:TPU:0, one launch (start us, length us, event | category | flops | bytes accessed | tf_op | source)
XLA Modules:
  0.0 125.0 jit_solution(7432800295180604622)
XLA Ops:
  0.6 3.0 %collective-permute-start.2 = (bf16[3,3,256,128]{3,2,1,0:T(8,128)(2,1)}, bf16[3,3,256,128]{3,2,1,0:T(8,128)(2,1)S(1)}, u32[]{:S(2)}, u32[]{:S(2)}) collective-permute-start(bf16[3,3,256,128]{3,2,1,0:T(8,128)(2,1)} %refs_8_.1), channel_id=1, source_target_pairs={{0,8},{8,0},{16,24},{24,16},{1,9},{9,1},{17,25},{25,17},{2,10},{10... | collective-permute-start | bytes 1769480 | tf_op jit(solution)/shard_map/one_x/ppermute | solution.py:17
  3.6 1.5 %collective-permute-start.3 = (bf16[3,3,256,128]{3,2,1,0:T(8,128)(2,1)}, bf16[3,3,256,128]{3,2,1,0:T(8,128)(2,1)S(1)}, u32[]{:S(2)}, u32[]{:S(2)}) collective-permute-start(bf16[3,3,256,128]{3,2,1,0:T(8,128)(2,1)} %refs_8_.1), channel_id=1, source_target_pairs={{0,16},{8,24},{16,0},{24,8},{1,17},{9,25},{17,1},{25,9},{2,18},{10... | collective-permute-start | bytes 1769480 | tf_op jit(solution)/shard_map/one_y/ppermute | solution.py:17
  5.2 2.6 %collective-permute-start.1 = (bf16[1024,128]{1,0:T(8,128)(2,1)}, bf16[1024,128]{1,0:T(8,128)(2,1)S(1)}, u32[]{:S(2)}, u32[]{:S(2)}) collective-permute-start(bf16[1024,128]{1,0:T(8,128)(2,1)} %bitcast.48), channel_id=1, source_target_pairs={{0,4},{1,5},{2,6},{3,7},{4,0},{5,1},{6,2},{7,3},{8,12},{9,13},{10,... | collective-permute-start | bytes 786440 | tf_op jit(solution)/shard_map/field_far/ppermute | solution.py:17
  7.7 1.6 %collective-permute-start = (bf16[1024,128]{1,0:T(8,128)(2,1)}, bf16[1024,128]{1,0:T(8,128)(2,1)S(1)}, u32[]{:S(2)}, u32[]{:S(2)}) collective-permute-start(bf16[1024,128]{1,0:T(8,128)(2,1)} %bitcast.49), channel_id=1, source_target_pairs={{0,2},{1,3},{2,0},{3,1},{4,6},{5,7},{6,4},{7,5},{8,10},{9,11},{10,... | collective-permute-start | bytes 786440 | tf_op jit(solution)/shard_map/field_near/ppermute | solution.py:17
  9.3 0.6 pad_add_fusion.place
  9.9 10.8 %collective-permute-done.1.refs_2_ = bf16[1024,128]{1,0:T(8,128)(2,1)S(1)} collective-permute-done((bf16[1024,128]{1,0:T(8,128)(2,1)}, bf16[1024,128]{1,0:T(8,128)(2,1)S(1)}, u32[]{:S(2)}, u32[]{:S(2)}) %collective-permute-start.1) | collective-permute-done | bytes 262176 | tf_op jit(solution)/shard_map/field_far/ppermute | solution.py:17
  21.0 0.6 collective-permute-start.9
  22.5 1.5 %collective-permute-start.5 = (bf16[1024,128]{1,0:T(8,128)(2,1)S(1)}, bf16[1024,128]{1,0:T(8,128)(2,1)S(1)}, u32[]{:S(2)}, u32[]{:S(2)}) collective-permute-start(bf16[1024,128]{1,0:T(8,128)(2,1)S(1)} %collective-permute-done.1.refs_2_), channel_id=1, source_target_pairs={{0,2},{1,3},{2,0},{3,1},{4,6},{5,7},{6,4},{7,5},{8,10},{9,11},{10,... | collective-permute-start | bytes 786440 | tf_op jit(solution)/shard_map/field_last/ppermute | solution.py:17
  24.1 6.7 %collective-permute-done.5.refs_3_ = bf16[1024,128]{1,0:T(8,128)(2,1)S(1)} collective-permute-done((bf16[1024,128]{1,0:T(8,128)(2,1)S(1)}, bf16[1024,128]{1,0:T(8,128)(2,1)S(1)}, u32[]{:S(2)}, u32[]{:S(2)}) %collective-permute-start.5) | collective-permute-done | bytes 262176 | tf_op jit(solution)/shard_map/field_last/ppermute | solution.py:17
  30.8 0.8 copy-done.24
  31.6 1.6 %collective-permute-start.11 = (bf16[3,3,256,128]{3,2,1,0:T(8,128)(2,1)}, bf16[3,3,256,128]{3,2,1,0:T(8,128)(2,1)S(1)}, u32[]{:S(2)}, u32[]{:S(2)}) collective-permute-start(bf16[3,3,256,128]{3,2,1,0:T(8,128)(2,1)} %refs_5_.1), channel_id=1, source_target_pairs={{0,16},{8,24},{16,0},{24,8},{1,17},{9,25},{17,1},{25,9},{2,18},{10... | collective-permute-start | bytes 1769480 | tf_op jit(solution)/shard_map/two_y/ppermute | solution.py:17
  33.1 1.5 %collective-permute-start.10 = (bf16[3,3,256,128]{3,2,1,0:T(8,128)(2,1)}, bf16[3,3,256,128]{3,2,1,0:T(8,128)(2,1)S(1)}, u32[]{:S(2)}, u32[]{:S(2)}) collective-permute-start(bf16[3,3,256,128]{3,2,1,0:T(8,128)(2,1)} %refs_5_.1), channel_id=1, source_target_pairs={{0,8},{8,0},{16,24},{24,16},{1,9},{9,1},{17,25},{25,17},{2,10},{10... | collective-permute-start | bytes 1769480 | tf_op jit(solution)/shard_map/two_x/ppermute | solution.py:17
  34.6 1.7 %collective-permute-done.12.refs_7_ = bf16[1024,128]{1,0:T(8,128)(2,1)} collective-permute-done((bf16[1024,128]{1,0:T(8,128)(2,1)S(1)}, bf16[1024,128]{1,0:T(8,128)(2,1)}, u32[]{:S(2)}, u32[]{:S(2)}) %collective-permute-start.12) | collective-permute-done | bytes 262176 | tf_op jit(solution)/shard_map/field_core3/ppermute | solution.py:17
  36.3 7.3 %conv_one.1 = (f32[1024,128]{1,0:T(8,128)}, bf16[1024,128]{1,0:T(8,128)(2,1)}) custom-call(s32[2]{0:T(128)} %pad_add_fusion.place, bf16[1024,128]{1,0:T(8,128)(2,1)} %bitcast.50, bf16[1024,128]{1,0:T(8,128)(2,1)} %copy-done.11, bf16[1024,128]{1,0:T(8,128)(2,1)} %copy-done.9, bf16[1024,128]{1,0:T(8,128)(2,1)} %copy-done.13, bf16[1024,128]{1,0:T(8,128)(2,1)} %copy-done.25, ...), custom_call_target="tpu_custom_call" | custom-call | flops 2415919104 | bytes 8388608 | tf_op jit(solution)/shard_map/conv_one/pallas_call | solution.py:258
  43.7 1.5 %collective-permute-start.16 = (bf16[1024,128]{1,0:T(8,128)(2,1)}, bf16[1024,128]{1,0:T(8,128)(2,1)S(1)}, u32[]{:S(2)}, u32[]{:S(2)}) collective-permute-start(bf16[1024,128]{1,0:T(8,128)(2,1)} %get-tuple-element.75.refs_0_), channel_id=1, source_target_pairs={{0,2},{1,3},{2,0},{3,1},{4,6},{5,7},{6,4},{7,5},{8,10},{9,11},{10,... | collective-permute-start | bytes 786440 | tf_op jit(solution)/shard_map/hidden_near/ppermute | solution.py:17
  45.2 2.3 %collective-permute-start.15 = (bf16[1024,128]{1,0:T(8,128)(2,1)}, bf16[1024,128]{1,0:T(8,128)(2,1)S(1)}, u32[]{:S(2)}, u32[]{:S(2)}) collective-permute-start(bf16[1024,128]{1,0:T(8,128)(2,1)} %get-tuple-element.75.refs_0_), channel_id=1, source_target_pairs={{0,4},{1,5},{2,6},{3,7},{4,0},{5,1},{6,2},{7,3},{8,12},{9,13},{10,... | collective-permute-start | bytes 786440 | tf_op jit(solution)/shard_map/hidden_far/ppermute | solution.py:17
  47.6 1.5 %collective-permute-start.14 = (bf16[3,3,128,128]{3,2,1,0:T(8,128)(2,1)S(1)}, bf16[3,3,128,128]{3,2,1,0:T(8,128)(2,1)S(1)}, u32[]{:S(2)}, u32[]{:S(2)}) collective-permute-start(bf16[3,3,128,128]{3,2,1,0:T(8,128)(2,1)S(1)} %slice.51), channel_id=1, source_target_pairs={{0,8},{8,0},{16,24},{24,16},{1,9},{9,1},{17,25},{25,17},{2,10},{10... | collective-permute-start | bytes 884744 | tf_op jit(solution)/shard_map/two_high/ppermute | solution.py:17
  49.6 6.0 %back_near.1 = (bf16[4,1024,128]{2,1,0:T(8,128)(2,1)}, bf16[4,1024,128]{2,1,0:T(8,128)(2,1)}) custom-call(s32[2]{0:T(128)} %pad_add_fusion.place, bf16[1024,128]{1,0:T(8,128)(2,1)} %bitcast.52, bf16[3,3,256,128]{3,2,1,0:T(8,128)(2,1)} %refs_5_.1, bf16[3,3,256,128]{3,2,1,0:T(8,128)(2,1)} %copy-done.20, bf16[3,3,256,128]{3,2,1,0:T(8,128)(2,1)} %copy-done.19), custom_call_target="tpu_custom_call" | custom-call | flops 1811939328 | bytes 6291456 | tf_op jit(solution)/shard_map/back_near/pallas_call | solution.py:303
  55.8 1.6 %collective-permute-done.16.refs_1_ = bf16[1024,128]{1,0:T(8,128)(2,1)S(1)} collective-permute-done((bf16[1024,128]{1,0:T(8,128)(2,1)}, bf16[1024,128]{1,0:T(8,128)(2,1)S(1)}, u32[]{:S(2)}, u32[]{:S(2)}) %collective-permute-start.16) | collective-permute-done | bytes 262176 | tf_op jit(solution)/shard_map/hidden_near/ppermute | solution.py:17
  57.4 2.6 %collective-permute-done.15.refs_2_ = bf16[1024,128]{1,0:T(8,128)(2,1)S(1)} collective-permute-done((bf16[1024,128]{1,0:T(8,128)(2,1)}, bf16[1024,128]{1,0:T(8,128)(2,1)S(1)}, u32[]{:S(2)}, u32[]{:S(2)}) %collective-permute-start.15) | collective-permute-done | bytes 262176 | tf_op jit(solution)/shard_map/hidden_far/ppermute | solution.py:17
  60.1 0.6 copy-done.4
  60.8 3.7 %back_far.1 = (bf16[4,1024,128]{2,1,0:T(8,128)(2,1)}, bf16[4,1024,128]{2,1,0:T(8,128)(2,1)}) custom-call(s32[2]{0:T(128)} %pad_add_fusion.place, bf16[1024,128]{1,0:T(8,128)(2,1)} %bitcast.53, bf16[3,3,128,128]{3,2,1,0:T(8,128)(2,1)} %copy-done.5, bf16[3,3,128,128]{3,2,1,0:T(8,128)(2,1)} %copy-done.4, ...), custom_call_target="tpu_custom_call", output_to_operand_aliasing={{0}: (4, {}), {1}: (5, {})} | custom-call | flops 603979776 | bytes 2097152 | tf_op jit(solution)/shard_map/back_far/pallas_call | solution.py:334
  64.6 1.9 %collective-permute-done.17.refs_3_ = bf16[1024,128]{1,0:T(8,128)(2,1)S(1)} collective-permute-done((bf16[1024,128]{1,0:T(8,128)(2,1)S(1)}, bf16[1024,128]{1,0:T(8,128)(2,1)S(1)}, u32[]{:S(2)}, u32[]{:S(2)}) %collective-permute-start.17) | collective-permute-done | bytes 262176 | tf_op jit(solution)/shard_map/hidden_last/ppermute | solution.py:17
  66.6 0.6 collective-permute-start.20
  67.2 2.2 %collective-permute-done.18 = bf16[4,1024,128]{2,1,0:T(8,128)(2,1)S(1)} collective-permute-done((bf16[4,1024,128]{2,1,0:T(8,128)(2,1)}, bf16[4,1024,128]{2,1,0:T(8,128)(2,1)S(1)}, u32[]{:S(2)}, u32[]{:S(2)}) %collective-permute-start.18) | collective-permute-done | bytes 1048608 | tf_op jit(solution)/shard_map/back_core/ppermute | solution.py:17
  69.5 1.2 collective-permute-start.19
  70.7 0.5 collective-permute-start.21
  71.7 2.4 %collective-permute-start.23 = (bf16[1024,128]{1,0:T(8,128)(2,1)S(1)}, bf16[1024,128]{1,0:T(8,128)(2,1)S(1)}, u32[]{:S(2)}, u32[]{:S(2)}) collective-permute-start(bf16[1024,128]{1,0:T(8,128)(2,1)S(1)} %get-tuple-element.100), channel_id=1, source_target_pairs={{0,24},{8,16},{16,8},{24,0},{1,25},{9,17},{17,9},{25,1},{2,26},{10... | collective-permute-start | bytes 786440 | tf_op jit(solution)/shard_map/input3/ppermute | solution.py:17
  74.2 1.0 copy-done.23
  75.2 6.5 %crop_grads.1 = (bf16[2,3,3,128,128]{4,3,2,1,0:T(8,128)(2,1)}, bf16[2,3,3,128,128]{4,3,2,1,0:T(8,128)(2,1)}, bf16[3,3,128,128]{3,2,1,0:T(8,128)(2,1)}, bf16[3,3,...) custom-call(s32[2]{0:T(128)} %pad_add_fusion.place, bf16[1024,128]{1,0:T(8,128)(2,1)} %bitcast.54, ...), custom_call_target="tpu_custom_call" | custom-call | flops 2415919104 | bytes 8388608 | tf_op jit(solution)/shard_map/crop_grads/pallas_call | solution.py:379
  81.8 2.8 %collective-permute-done.22.refs_1_ = bf16[1024,128]{1,0:T(8,128)(2,1)S(1)} collective-permute-done((bf16[1024,128]{1,0:T(8,128)(2,1)S(1)}, bf16[1024,128]{1,0:T(8,128)(2,1)S(1)}, u32[]{:S(2)}, u32[]{:S(2)}) %collective-permute-start.22) | collective-permute-done | bytes 262176 | tf_op jit(solution)/shard_map/input2/ppermute | solution.py:17
  84.9 1.6 %collective-permute-start.30 = (bf16[2,3,3,128,128]{4,3,2,1,0:T(8,128)(2,1)}, bf16[2,3,3,128,128]{4,3,2,1,0:T(8,128)(2,1)S(1)}, u32[]{:S(2)}, u32[]{:S(2)}) collective-permute-start(bf16[2,3,3,128,128]{4,3,2,1,0:T(8,128)(2,1)} %get-tuple-element.117), channel_id=1, source_target_pairs={{0,8},{8,0},{16,24},{24,16},{1,9},{9,1},{17,25},{25,17},{2,10},{10... | collective-permute-start | bytes 1769480 | tf_op jit(solution)/shard_map/grad_x/ppermute | solution.py:17
  86.9 1.6 %collective-permute-start.24 = (bf16[1024,128]{1,0:T(8,128)(2,1)S(1)}, bf16[1024,128]{1,0:T(8,128)(2,1)S(1)}, u32[]{:S(2)}, u32[]{:S(2)}) collective-permute-start(bf16[1024,128]{1,0:T(8,128)(2,1)S(1)} %fusion.6), channel_id=1, source_target_pairs={{0,4},{1,5},{2,6},{3,7},{4,0},{5,1},{6,2},{7,3},{8,12},{9,13},{10,... | collective-permute-start | bytes 786440 | tf_op jit(solution)/shard_map/distant/ppermute | solution.py:17
  88.5 0.7 collective-permute-start.25
  89.2 7.4 %conv_two.1 = bf16[1024,128]{1,0:T(8,128)(2,1)} custom-call(s32[2]{0:T(128)} %pad_add_fusion.place, bf16[1024,128]{1,0:T(8,128)(2,1)} %get-tuple-element.75.refs_0_, bf16[1024,128]{1,0:T(8,128)(2,1)} %copy-done.16, bf16[1024,128]{1,0:T(8,128)(2,1)} %copy-done.17, bf16[1024,128]{1,0:T(8,128)(2,1)} %copy-done.18, bf16[4,1024,128]{2,1,0:T(8,128)(2,1)} %copy-done.23, ...), custom_call_target="tpu_custom_call" | custom-call | flops 2415919104 | bytes 8388608 | tf_op jit(solution)/shard_map/conv_two/pallas_call | solution.py:258
  96.6 4.9 %collective-permute-done.24 = bf16[1024,128]{1,0:T(8,128)(2,1)S(1)} collective-permute-done((bf16[1024,128]{1,0:T(8,128)(2,1)S(1)}, bf16[1024,128]{1,0:T(8,128)(2,1)S(1)}, u32[]{:S(2)}, u32[]{:S(2)}) %collective-permute-start.24) | collective-permute-done | bytes 262176 | tf_op jit(solution)/shard_map/distant/ppermute | solution.py:17
  101.9 1.6 %collective-permute-start.29 = (bf16[1024,128]{1,0:T(8,128)(2,1)S(1)}, bf16[1024,128]{1,0:T(8,128)(2,1)S(1)}, u32[]{:S(2)}, u32[]{:S(2)}) collective-permute-start(bf16[1024,128]{1,0:T(8,128)(2,1)S(1)} %fusion.5.refs_2_), channel_id=1, source_target_pairs={{0,24},{8,16},{16,8},{24,0},{1,25},{9,17},{17,9},{25,1},{2,26},{10... | collective-permute-start | bytes 786440 | tf_op jit(solution)/shard_map/pre3/ppermute | solution.py:17
  103.4 1.2 collective-permute-start.28
  104.6 0.8 collective-permute-start.27
  105.5 1.3 %collective-permute-start.33 = (bf16[3,3,128,128]{3,2,1,0:T(8,128)(2,1)S(1)}, bf16[3,3,128,128]{3,2,1,0:T(8,128)(2,1)S(1)}, u32[]{:S(2)}, u32[]{:S(2)}) collective-permute-start(bf16[3,3,128,128]{3,2,1,0:T(8,128)(2,1)S(1)} %fusion), channel_id=1, source_target_pairs={{0,8},{8,0},{16,24},{24,16},{1,9},{9,1},{17,25},{25,17},{2,10},{10... | collective-permute-start | bytes 884744 | tf_op jit(solution)/shard_map/grad_high/ppermute | solution.py:17
  106.9 0.9 collective-permute-start.32
  107.8 1.6 %grad_one_own.1.refs_7_ = f32[3,3,256,128]{3,2,1,0:T(8,128)S(1)} custom-call(s32[2]{0:T(128)S(1)} %copy-done, bf16[1024,128]{1,0:T(8,128)(2,1)S(1)} %get-tuple-element.103.refs_0_, bf16[4,1024,128]{2,1,0:T(8,128)(2,1)S(1)} %collective-permute-done.26.refs_1_.refs_3_, bf16[1024,128]{1,0:T(8,128)(2,1)S(1)} %fusion.5.refs_2_), custom_call_target="tpu_custom_call" | custom-call | flops 603979776 | bytes 2097152 | tf_op jit(solution)/shard_map/grad_one_own/pallas_call | solution.py:418
  109.4 2.7 %collective-permute-done.29.refs_6_ = bf16[1024,128]{1,0:T(8,128)(2,1)S(1)} collective-permute-done((bf16[1024,128]{1,0:T(8,128)(2,1)S(1)}, bf16[1024,128]{1,0:T(8,128)(2,1)S(1)}, u32[]{:S(2)}, u32[]{:S(2)}) %collective-permute-start.29) | collective-permute-done | bytes 262176 | tf_op jit(solution)/shard_map/pre3/ppermute | solution.py:17
  112.1 4.3 %collective-permute-done.28.refs_5_ = bf16[1024,128]{1,0:T(8,128)(2,1)S(1)} collective-permute-done((bf16[1024,128]{1,0:T(8,128)(2,1)S(1)}, bf16[1024,128]{1,0:T(8,128)(2,1)S(1)}, u32[]{:S(2)}, u32[]{:S(2)}) %collective-permute-start.28) | collective-permute-done | bytes 262176 | tf_op jit(solution)/shard_map/pre2/ppermute | solution.py:17
  116.4 1.3 %collective-permute-done.27.refs_4_ = bf16[1024,128]{1,0:T(8,128)(2,1)S(1)} collective-permute-done((bf16[1024,128]{1,0:T(8,128)(2,1)S(1)}, bf16[1024,128]{1,0:T(8,128)(2,1)S(1)}, u32[]{:S(2)}, u32[]{:S(2)}) %collective-permute-start.27) | collective-permute-done | bytes 262176 | tf_op jit(solution)/shard_map/pre1/ppermute | solution.py:17
  117.7 4.8 %grad_one.1 = f32[3,3,256,128]{3,2,1,0:T(8,128)} custom-call(s32[2]{0:T(128)S(1)} %copy-done, bf16[1024,128]{1,0:T(8,128)(2,1)S(1)} %collective-permute-done.21.refs_0_, bf16[1024,128]{1,0:T(8,128)(2,1)S(1)} %collective-permute-done.22.refs_1_, bf16[1024,128]{1,0:T(8,128)(2,1)S(1)} %collective-permute-done.23.refs_2_, ...), custom_call_target="tpu_custom_call" | custom-call | flops 1811939328 | bytes 6291456 | tf_op jit(solution)/shard_map/grad_one/pallas_call | solution.py:418
  122.9 0.9 copy-done.2
  123.8 1.1 maximum_add_fusion
  (99 shorter events, 4.6 us)
Async XLA Ops:
  0.6 20.3 %collective-permute-start.2 = (bf16[3,3,256,128]{3,2,1,0:T(8,128)(2,1)}, bf16[3,3,256,128]{3,2,1,0:T(8,128)(2,1)S(1)}, u32[]{:S(2)}, u32[]{:S(2)}) collective-permute-start(bf16[3,3,256,128]{3,2,1,0:T(8,128)(2,1)} %refs_8_.1), channel_id=1, source_target_pairs={{0,8},{8,0},{16,24},{24,16},{1,9},{9,1},{17,25},{25,17},{2,10},{10... | collective-permute-start | bytes 1769480 | tf_op jit(solution)/shard_map/one_x/ppermute | solution.py:17
  3.6 17.3 %collective-permute-start.3 = (bf16[3,3,256,128]{3,2,1,0:T(8,128)(2,1)}, bf16[3,3,256,128]{3,2,1,0:T(8,128)(2,1)S(1)}, u32[]{:S(2)}, u32[]{:S(2)}) collective-permute-start(bf16[3,3,256,128]{3,2,1,0:T(8,128)(2,1)} %refs_8_.1), channel_id=1, source_target_pairs={{0,16},{8,24},{16,0},{24,8},{1,17},{9,25},{17,1},{25,9},{2,18},{10... | collective-permute-start | bytes 1769480 | tf_op jit(solution)/shard_map/one_y/ppermute | solution.py:17
  5.2 4.8 %collective-permute-start.4 = (bf16[1024,128]{1,0:T(8,128)(2,1)}, bf16[1024,128]{1,0:T(8,128)(2,1)S(1)}, u32[]{:S(2)}, u32[]{:S(2)}) collective-permute-start(bf16[1024,128]{1,0:T(8,128)(2,1)} %bitcast.47), channel_id=1, source_target_pairs={{0,1},{1,0},{2,3},{3,2},{4,5},{5,4},{6,7},{7,6},{8,9},{9,8},{10,11... | collective-permute-start | bytes 786440 | tf_op jit(solution)/shard_map/field_core0/ppermute | solution.py:17
  5.2 15.6 %collective-permute-start.1 = (bf16[1024,128]{1,0:T(8,128)(2,1)}, bf16[1024,128]{1,0:T(8,128)(2,1)S(1)}, u32[]{:S(2)}, u32[]{:S(2)}) collective-permute-start(bf16[1024,128]{1,0:T(8,128)(2,1)} %bitcast.48), channel_id=1, source_target_pairs={{0,4},{1,5},{2,6},{3,7},{4,0},{5,1},{6,2},{7,3},{8,12},{9,13},{10,... | collective-permute-start | bytes 786440 | tf_op jit(solution)/shard_map/field_far/ppermute | solution.py:17
  7.7 13.2 %collective-permute-start = (bf16[1024,128]{1,0:T(8,128)(2,1)}, bf16[1024,128]{1,0:T(8,128)(2,1)S(1)}, u32[]{:S(2)}, u32[]{:S(2)}) collective-permute-start(bf16[1024,128]{1,0:T(8,128)(2,1)} %bitcast.49), channel_id=1, source_target_pairs={{0,2},{1,3},{2,0},{3,1},{4,6},{5,7},{6,4},{7,5},{8,10},{9,11},{10,... | collective-permute-start | bytes 786440 | tf_op jit(solution)/shard_map/field_near/ppermute | solution.py:17
  9.9 12.1 %copy-start.25 = (bf16[1024,128]{1,0:T(8,128)(2,1)}, bf16[1024,128]{1,0:T(8,128)(2,1)S(1)}, u32[]{:S(2)}) copy-start(bf16[1024,128]{1,0:T(8,128)(2,1)S(1)} %collective-permute-done.4.refs_4_) | copy-start | bytes 786436
  20.7 15.6 %copy-start.9 = (bf16[1024,128]{1,0:T(8,128)(2,1)}, bf16[1024,128]{1,0:T(8,128)(2,1)S(1)}, u32[]{:S(2)}) copy-start(bf16[1024,128]{1,0:T(8,128)(2,1)S(1)} %collective-permute-done.1.refs_2_) | copy-start | bytes 786436
  20.9 15.4 %copy-start.11 = (bf16[1024,128]{1,0:T(8,128)(2,1)}, bf16[1024,128]{1,0:T(8,128)(2,1)S(1)}, u32[]{:S(2)}) copy-start(bf16[1024,128]{1,0:T(8,128)(2,1)S(1)} %collective-permute-done.refs_1_) | copy-start | bytes 786436
  20.9 15.4 %copy-start.21 = (bf16[3,3,256,128]{3,2,1,0:T(8,128)(2,1)}, bf16[3,3,256,128]{3,2,1,0:T(8,128)(2,1)S(1)}, u32[]{:S(2)}) copy-start(bf16[3,3,256,128]{3,2,1,0:T(8,128)(2,1)S(1)} %collective-permute-done.2.refs_9_) | copy-start | bytes 1769476
  20.9 15.4 %copy-start.22 = (bf16[3,3,256,128]{3,2,1,0:T(8,128)(2,1)}, bf16[3,3,256,128]{3,2,1,0:T(8,128)(2,1)S(1)}, u32[]{:S(2)}) copy-start(bf16[3,3,256,128]{3,2,1,0:T(8,128)(2,1)S(1)} %collective-permute-done.3.refs_10_) | copy-start | bytes 1769476
  21.0 9.8 %collective-permute-start.9 = (bf16[3,3,128,128]{3,2,1,0:T(8,128)(2,1)S(1)}, bf16[3,3,128,128]{3,2,1,0:T(8,128)(2,1)S(1)}, u32[]{:S(2)}, u32[]{:S(2)}) collective-permute-start(bf16[3,3,128,128]{3,2,1,0:T(8,128)(2,1)S(1)} %slice.49), channel_id=1, source_target_pairs={{0,8},{8,0},{16,24},{24,16},{1,9},{9,1},{17,25},{25,17},{2,10},{10... | collective-permute-start | bytes 884744 | tf_op jit(solution)/shard_map/one_high/ppermute | solution.py:17
  21.6 10.0 %collective-permute-start.8 = (bf16[3,3,128,128]{3,2,1,0:T(8,128)(2,1)S(1)}, bf16[3,3,128,128]{3,2,1,0:T(8,128)(2,1)}, u32[]{:S(2)}, u32[]{:S(2)}) collective-permute-start(bf16[3,3,128,128]{3,2,1,0:T(8,128)(2,1)S(1)} %slice.48), channel_id=1, source_target_pairs={{0,16},{8,24},{16,0},{24,8},{1,17},{9,25},{17,1},{25,9},{2,18},{10... | collective-permute-start | bytes 884744 | tf_op jit(solution)/shard_map/one_low/ppermute | solution.py:17
  22.0 2.0 %collective-permute-start.6 = (bf16[1024,128]{1,0:T(8,128)(2,1)S(1)}, bf16[1024,128]{1,0:T(8,128)(2,1)S(1)}, u32[]{:S(2)}, u32[]{:S(2)}) collective-permute-start(bf16[1024,128]{1,0:T(8,128)(2,1)S(1)} %collective-permute-done.refs_1_), channel_id=1, source_target_pairs={{0,1},{1,0},{2,3},{3,2},{4,5},{5,4},{6,7},{7,6},{8,9},{9,8},{10,11... | collective-permute-start | bytes 786440 | tf_op jit(solution)/shard_map/field_core1/ppermute | solution.py:17
  22.0 2.0 %collective-permute-start.7 = (bf16[1024,128]{1,0:T(8,128)(2,1)S(1)}, bf16[1024,128]{1,0:T(8,128)(2,1)S(1)}, u32[]{:S(2)}, u32[]{:S(2)}) collective-permute-start(bf16[1024,128]{1,0:T(8,128)(2,1)S(1)} %collective-permute-done.1.refs_2_), channel_id=1, source_target_pairs={{0,1},{1,0},{2,3},{3,2},{4,5},{5,4},{6,7},{7,6},{8,9},{9,8},{10,11... | collective-permute-start | bytes 786440 | tf_op jit(solution)/shard_map/field_core2/ppermute | solution.py:17
  22.5 8.2 %collective-permute-start.5 = (bf16[1024,128]{1,0:T(8,128)(2,1)S(1)}, bf16[1024,128]{1,0:T(8,128)(2,1)S(1)}, u32[]{:S(2)}, u32[]{:S(2)}) collective-permute-start(bf16[1024,128]{1,0:T(8,128)(2,1)S(1)} %collective-permute-done.1.refs_2_), channel_id=1, source_target_pairs={{0,2},{1,3},{2,0},{3,1},{4,6},{5,7},{6,4},{7,5},{8,10},{9,11},{10,... | collective-permute-start | bytes 786440 | tf_op jit(solution)/shard_map/field_last/ppermute | solution.py:17
  24.0 6.7 %copy-start.26 = (bf16[1024,128]{1,0:T(8,128)(2,1)}, bf16[1024,128]{1,0:T(8,128)(2,1)S(1)}, u32[]{:S(2)}) copy-start(bf16[1024,128]{1,0:T(8,128)(2,1)S(1)} %collective-permute-done.6.refs_5_) | copy-start | bytes 786436
  24.1 6.7 %copy-start.27 = (bf16[1024,128]{1,0:T(8,128)(2,1)}, bf16[1024,128]{1,0:T(8,128)(2,1)S(1)}, u32[]{:S(2)}) copy-start(bf16[1024,128]{1,0:T(8,128)(2,1)S(1)} %collective-permute-done.7.refs_6_) | copy-start | bytes 786436
  31.6 16.0 %collective-permute-start.11 = (bf16[3,3,256,128]{3,2,1,0:T(8,128)(2,1)}, bf16[3,3,256,128]{3,2,1,0:T(8,128)(2,1)S(1)}, u32[]{:S(2)}, u32[]{:S(2)}) collective-permute-start(bf16[3,3,256,128]{3,2,1,0:T(8,128)(2,1)} %refs_5_.1), channel_id=1, source_target_pairs={{0,16},{8,24},{16,0},{24,8},{1,17},{9,25},{17,1},{25,9},{2,18},{10... | collective-permute-start | bytes 1769480 | tf_op jit(solution)/shard_map/two_y/ppermute | solution.py:17
  33.1 14.4 %collective-permute-start.10 = (bf16[3,3,256,128]{3,2,1,0:T(8,128)(2,1)}, bf16[3,3,256,128]{3,2,1,0:T(8,128)(2,1)S(1)}, u32[]{:S(2)}, u32[]{:S(2)}) collective-permute-start(bf16[3,3,256,128]{3,2,1,0:T(8,128)(2,1)} %refs_5_.1), channel_id=1, source_target_pairs={{0,8},{8,0},{16,24},{24,16},{1,9},{9,1},{17,25},{25,17},{2,10},{10... | collective-permute-start | bytes 1769480 | tf_op jit(solution)/shard_map/two_x/ppermute | solution.py:17
  34.6 1.7 %collective-permute-start.12 = (bf16[1024,128]{1,0:T(8,128)(2,1)S(1)}, bf16[1024,128]{1,0:T(8,128)(2,1)}, u32[]{:S(2)}, u32[]{:S(2)}) collective-permute-start(bf16[1024,128]{1,0:T(8,128)(2,1)S(1)} %collective-permute-done.5.refs_3_), channel_id=1, source_target_pairs={{0,1},{1,0},{2,3},{3,2},{4,5},{5,4},{6,7},{7,6},{8,9},{9,8},{10,11... | collective-permute-start | bytes 786440 | tf_op jit(solution)/shard_map/field_core3/ppermute | solution.py:17
  43.7 13.7 %collective-permute-start.16 = (bf16[1024,128]{1,0:T(8,128)(2,1)}, bf16[1024,128]{1,0:T(8,128)(2,1)S(1)}, u32[]{:S(2)}, u32[]{:S(2)}) collective-permute-start(bf16[1024,128]{1,0:T(8,128)(2,1)} %get-tuple-element.75.refs_0_), channel_id=1, source_target_pairs={{0,2},{1,3},{2,0},{3,1},{4,6},{5,7},{6,4},{7,5},{8,10},{9,11},{10,... | collective-permute-start | bytes 786440 | tf_op jit(solution)/shard_map/hidden_near/ppermute | solution.py:17
  45.2 14.8 %collective-permute-start.15 = (bf16[1024,128]{1,0:T(8,128)(2,1)}, bf16[1024,128]{1,0:T(8,128)(2,1)S(1)}, u32[]{:S(2)}, u32[]{:S(2)}) collective-permute-start(bf16[1024,128]{1,0:T(8,128)(2,1)} %get-tuple-element.75.refs_0_), channel_id=1, source_target_pairs={{0,4},{1,5},{2,6},{3,7},{4,0},{5,1},{6,2},{7,3},{8,12},{9,13},{10,... | collective-permute-start | bytes 786440 | tf_op jit(solution)/shard_map/hidden_far/ppermute | solution.py:17
  47.6 12.4 %collective-permute-start.14 = (bf16[3,3,128,128]{3,2,1,0:T(8,128)(2,1)S(1)}, bf16[3,3,128,128]{3,2,1,0:T(8,128)(2,1)S(1)}, u32[]{:S(2)}, u32[]{:S(2)}) collective-permute-start(bf16[3,3,128,128]{3,2,1,0:T(8,128)(2,1)S(1)} %slice.51), channel_id=1, source_target_pairs={{0,8},{8,0},{16,24},{24,16},{1,9},{9,1},{17,25},{25,17},{2,10},{10... | collective-permute-start | bytes 884744 | tf_op jit(solution)/shard_map/two_high/ppermute | solution.py:17
  49.1 11.0 %collective-permute-start.13 = (bf16[3,3,128,128]{3,2,1,0:T(8,128)(2,1)S(1)}, bf16[3,3,128,128]{3,2,1,0:T(8,128)(2,1)S(1)}, u32[]{:S(2)}, u32[]{:S(2)}) collective-permute-start(bf16[3,3,128,128]{3,2,1,0:T(8,128)(2,1)S(1)} %slice.50), channel_id=1, source_target_pairs={{0,16},{8,24},{16,0},{24,8},{1,17},{9,25},{17,1},{25,9},{2,18},{10... | collective-permute-start | bytes 884744 | tf_op jit(solution)/shard_map/two_low/ppermute | solution.py:17
  49.6 6.1 %copy-start.12 = (bf16[1024,128]{1,0:T(8,128)(2,1)S(1)}, bf16[1024,128]{1,0:T(8,128)(2,1)}, u32[]{:S(2)}) copy-start(bf16[1024,128]{1,0:T(8,128)(2,1)} %copy-done.11) | copy-start | bytes 786436
  49.6 6.1 %copy-start.14 = (bf16[1024,128]{1,0:T(8,128)(2,1)S(1)}, bf16[1024,128]{1,0:T(8,128)(2,1)}, u32[]{:S(2)}) copy-start(bf16[1024,128]{1,0:T(8,128)(2,1)} %copy-done.13) | copy-start | bytes 786436
  57.4 16.8 %copy-start.16 = (bf16[1024,128]{1,0:T(8,128)(2,1)}, bf16[1024,128]{1,0:T(8,128)(2,1)S(1)}, u32[]{:S(2)}) copy-start(bf16[1024,128]{1,0:T(8,128)(2,1)S(1)} %collective-permute-done.16.refs_1_) | copy-start | bytes 786436
  60.0 14.2 %copy-start.17 = (bf16[1024,128]{1,0:T(8,128)(2,1)}, bf16[1024,128]{1,0:T(8,128)(2,1)S(1)}, u32[]{:S(2)}) copy-start(bf16[1024,128]{1,0:T(8,128)(2,1)S(1)} %collective-permute-done.15.refs_2_) | copy-start | bytes 786436
  60.0 6.5 %copy-start.15 = (bf16[1024,128]{1,0:T(8,128)(2,1)S(1)}, bf16[1024,128]{1,0:T(8,128)(2,1)}, u32[]{:S(2)}) copy-start(bf16[1024,128]{1,0:T(8,128)(2,1)} %get-tuple-element.75.refs_0_) | copy-start | bytes 786436
  60.0 6.4 %collective-permute-start.17 = (bf16[1024,128]{1,0:T(8,128)(2,1)S(1)}, bf16[1024,128]{1,0:T(8,128)(2,1)S(1)}, u32[]{:S(2)}, u32[]{:S(2)}) collective-permute-start(bf16[1024,128]{1,0:T(8,128)(2,1)S(1)} %collective-permute-done.15.refs_2_), channel_id=1, source_target_pairs={{0,2},{1,3},{2,0},{3,1},{4,6},{5,7},{6,4},{7,5},{8,10},{9,11},{10,... | collective-permute-start | bytes 786440 | tf_op jit(solution)/shard_map/hidden_last/ppermute | solution.py:17
  66.5 2.9 %collective-permute-start.18 = (bf16[4,1024,128]{2,1,0:T(8,128)(2,1)}, bf16[4,1024,128]{2,1,0:T(8,128)(2,1)S(1)}, u32[]{:S(2)}, u32[]{:S(2)}) collective-permute-start(bf16[4,1024,128]{2,1,0:T(8,128)(2,1)} %get-tuple-element.92), channel_id=1, source_target_pairs={{0,1},{1,0},{2,3},{3,2},{4,5},{5,4},{6,7},{7,6},{8,9},{9,8},{10,11... | collective-permute-start | bytes 3145736 | tf_op jit(solution)/shard_map/back_core/ppermute | solution.py:17
  66.6 7.6 %collective-permute-start.20 = (bf16[4,1024,128]{2,1,0:T(8,128)(2,1)S(1)}, bf16[4,1024,128]{2,1,0:T(8,128)(2,1)S(1)}, u32[]{:S(2)}, u32[]{:S(2)}) collective-permute-start(bf16[4,1024,128]{2,1,0:T(8,128)(2,1)S(1)} %pad_maximum_fusion), channel_id=1, source_target_pairs={{0,1},{1,0},{2,3},{3,2},{4,5},{5,4},{6,7},{7,6},{8,9},{9,8},{10,11... | collective-permute-start | bytes 3145736 | tf_op jit(solution)/shard_map/hidden_core/ppermute | solution.py:17
  69.5 12.2 %collective-permute-start.19 = (bf16[1024,128]{1,0:T(8,128)(2,1)S(1)}, bf16[1024,128]{1,0:T(8,128)(2,1)S(1)}, u32[]{:S(2)}, u32[]{:S(2)}) collective-permute-start(bf16[1024,128]{1,0:T(8,128)(2,1)S(1)} %get-tuple-element.123), channel_id=1, source_target_pairs={{0,2},{1,3},{2,0},{3,1},{4,6},{5,7},{6,4},{7,5},{8,10},{9,11},{10,... | collective-permute-start | bytes 786440 | tf_op jit(solution)/shard_map/relayed/ppermute | solution.py:17
  70.7 11.1 %collective-permute-start.21 = (bf16[1024,128]{1,0:T(8,128)(2,1)S(1)}, bf16[1024,128]{1,0:T(8,128)(2,1)S(1)}, u32[]{:S(2)}, u32[]{:S(2)}) collective-permute-start(bf16[1024,128]{1,0:T(8,128)(2,1)S(1)} %get-tuple-element.98), channel_id=1, source_target_pairs={{0,8},{8,0},{16,24},{24,16},{1,9},{9,1},{17,25},{25,17},{2,10},{10... | collective-permute-start | bytes 786440 | tf_op jit(solution)/shard_map/input1/ppermute | solution.py:17
  71.2 13.4 %collective-permute-start.22 = (bf16[1024,128]{1,0:T(8,128)(2,1)S(1)}, bf16[1024,128]{1,0:T(8,128)(2,1)S(1)}, u32[]{:S(2)}, u32[]{:S(2)}) collective-permute-start(bf16[1024,128]{1,0:T(8,128)(2,1)S(1)} %get-tuple-element.99), channel_id=1, source_target_pairs={{0,16},{8,24},{16,0},{24,8},{1,17},{9,25},{17,1},{25,9},{2,18},{10... | collective-permute-start | bytes 786440 | tf_op jit(solution)/shard_map/input2/ppermute | solution.py:17
  71.7 12.9 %collective-permute-start.23 = (bf16[1024,128]{1,0:T(8,128)(2,1)S(1)}, bf16[1024,128]{1,0:T(8,128)(2,1)S(1)}, u32[]{:S(2)}, u32[]{:S(2)}) collective-permute-start(bf16[1024,128]{1,0:T(8,128)(2,1)S(1)} %get-tuple-element.100), channel_id=1, source_target_pairs={{0,24},{8,16},{16,8},{24,0},{1,25},{9,17},{17,9},{25,1},{2,26},{10... | collective-permute-start | bytes 786440 | tf_op jit(solution)/shard_map/input3/ppermute | solution.py:17
  84.8 16.8 %copy-start.3 = (f32[1024,128]{1,0:T(8,128)S(1)}, f32[1024,128]{1,0:T(8,128)}, u32[]{:S(2)}) copy-start(f32[1024,128]{1,0:T(8,128)} %get-tuple-element.111) | copy-start | bytes 1572868
  84.8 16.8 %collective-permute-start.26 = (bf16[4,1024,128]{2,1,0:T(8,128)(2,1)S(1)}, bf16[4,1024,128]{2,1,0:T(8,128)(2,1)S(1)}, u32[]{:S(2)}, u32[]{:S(2)}) collective-permute-start(bf16[4,1024,128]{2,1,0:T(8,128)(2,1)S(1)} %pad_maximum_fusion.1), channel_id=1, source_target_pairs={{0,1},{1,0},{2,3},{3,2},{4,5},{5,4},{6,7},{7,6},{8,9},{9,8},{10,11... | collective-permute-start | bytes 3145736 | tf_op jit(solution)/shard_map/field_swap/ppermute | solution.py:17
  84.9 20.6 %collective-permute-start.30 = (bf16[2,3,3,128,128]{4,3,2,1,0:T(8,128)(2,1)}, bf16[2,3,3,128,128]{4,3,2,1,0:T(8,128)(2,1)S(1)}, u32[]{:S(2)}, u32[]{:S(2)}) collective-permute-start(bf16[2,3,3,128,128]{4,3,2,1,0:T(8,128)(2,1)} %get-tuple-element.117), channel_id=1, source_target_pairs={{0,8},{8,0},{16,24},{24,16},{1,9},{9,1},{17,25},{25,17},{2,10},{10... | collective-permute-start | bytes 1769480 | tf_op jit(solution)/shard_map/grad_x/ppermute | solution.py:17
  86.4 19.0 %collective-permute-start.31 = (bf16[2,3,3,128,128]{4,3,2,1,0:T(8,128)(2,1)}, bf16[2,3,3,128,128]{4,3,2,1,0:T(8,128)(2,1)S(1)}, u32[]{:S(2)}, u32[]{:S(2)}) collective-permute-start(bf16[2,3,3,128,128]{4,3,2,1,0:T(8,128)(2,1)} %get-tuple-element.118), channel_id=1, source_target_pairs={{0,16},{8,24},{16,0},{24,8},{1,17},{9,25},{17,1},{25,9},{2,18},{10... | collective-permute-start | bytes 1769480 | tf_op jit(solution)/shard_map/grad_y/ppermute | solution.py:17
  86.9 14.6 %collective-permute-start.24 = (bf16[1024,128]{1,0:T(8,128)(2,1)S(1)}, bf16[1024,128]{1,0:T(8,128)(2,1)S(1)}, u32[]{:S(2)}, u32[]{:S(2)}) collective-permute-start(bf16[1024,128]{1,0:T(8,128)(2,1)S(1)} %fusion.6), channel_id=1, source_target_pairs={{0,4},{1,5},{2,6},{3,7},{4,0},{5,1},{6,2},{7,3},{8,12},{9,13},{10,... | collective-permute-start | bytes 786440 | tf_op jit(solution)/shard_map/distant/ppermute | solution.py:17
  88.5 13.0 %collective-permute-start.25 = (bf16[1024,128]{1,0:T(8,128)(2,1)S(1)}, bf16[1024,128]{1,0:T(8,128)(2,1)S(1)}, u32[]{:S(2)}, u32[]{:S(2)}) collective-permute-start(bf16[1024,128]{1,0:T(8,128)(2,1)S(1)} %get-tuple-element.102), channel_id=1, source_target_pairs={{0,2},{1,3},{2,0},{3,1},{4,6},{5,7},{6,4},{7,5},{8,10},{9,11},{10,... | collective-permute-start | bytes 786440 | tf_op jit(solution)/shard_map/nearby/ppermute | solution.py:17
  96.6 8.9 %copy-start.7 = (bf16[3,3,128,128]{3,2,1,0:T(8,128)(2,1)S(1)}, bf16[3,3,128,128]{3,2,1,0:T(8,128)(2,1)}, u32[]{:S(2)}) copy-start(bf16[3,3,128,128]{3,2,1,0:T(8,128)(2,1)} %get-tuple-element.122) | copy-start | bytes 884740
  101.9 10.2 %collective-permute-start.29 = (bf16[1024,128]{1,0:T(8,128)(2,1)S(1)}, bf16[1024,128]{1,0:T(8,128)(2,1)S(1)}, u32[]{:S(2)}, u32[]{:S(2)}) collective-permute-start(bf16[1024,128]{1,0:T(8,128)(2,1)S(1)} %fusion.5.refs_2_), channel_id=1, source_target_pairs={{0,24},{8,16},{16,8},{24,0},{1,25},{9,17},{17,9},{25,1},{2,26},{10... | collective-permute-start | bytes 786440 | tf_op jit(solution)/shard_map/pre3/ppermute | solution.py:17
  103.4 13.0 %collective-permute-start.28 = (bf16[1024,128]{1,0:T(8,128)(2,1)S(1)}, bf16[1024,128]{1,0:T(8,128)(2,1)S(1)}, u32[]{:S(2)}, u32[]{:S(2)}) collective-permute-start(bf16[1024,128]{1,0:T(8,128)(2,1)S(1)} %fusion.5.refs_2_), channel_id=1, source_target_pairs={{0,16},{8,24},{16,0},{24,8},{1,17},{9,25},{17,1},{25,9},{2,18},{10... | collective-permute-start | bytes 786440 | tf_op jit(solution)/shard_map/pre2/ppermute | solution.py:17
  104.6 13.1 %collective-permute-start.27 = (bf16[1024,128]{1,0:T(8,128)(2,1)S(1)}, bf16[1024,128]{1,0:T(8,128)(2,1)S(1)}, u32[]{:S(2)}, u32[]{:S(2)}) collective-permute-start(bf16[1024,128]{1,0:T(8,128)(2,1)S(1)} %fusion.5.refs_2_), channel_id=1, source_target_pairs={{0,8},{8,0},{16,24},{24,16},{1,9},{9,1},{17,25},{25,17},{2,10},{10... | collective-permute-start | bytes 786440 | tf_op jit(solution)/shard_map/pre1/ppermute | solution.py:17
  105.5 17.2 %collective-permute-start.33 = (bf16[3,3,128,128]{3,2,1,0:T(8,128)(2,1)S(1)}, bf16[3,3,128,128]{3,2,1,0:T(8,128)(2,1)S(1)}, u32[]{:S(2)}, u32[]{:S(2)}) collective-permute-start(bf16[3,3,128,128]{3,2,1,0:T(8,128)(2,1)S(1)} %fusion), channel_id=1, source_target_pairs={{0,8},{8,0},{16,24},{24,16},{1,9},{9,1},{17,25},{25,17},{2,10},{10... | collective-permute-start | bytes 884744 | tf_op jit(solution)/shard_map/grad_high/ppermute | solution.py:17
  106.9 15.9 %collective-permute-start.32 = (bf16[3,3,128,128]{3,2,1,0:T(8,128)(2,1)S(1)}, bf16[3,3,128,128]{3,2,1,0:T(8,128)(2,1)S(1)}, u32[]{:S(2)}, u32[]{:S(2)}) collective-permute-start(bf16[3,3,128,128]{3,2,1,0:T(8,128)(2,1)S(1)} %fusion.1), channel_id=1, source_target_pairs={{0,16},{8,24},{16,0},{24,8},{1,17},{9,25},{17,1},{25,9},{2,18},{10... | collective-permute-start | bytes 884744 | tf_op jit(solution)/shard_map/grad_low/ppermute | solution.py:17
  (14 other events, 45.4 us)
